TPU v7x, 32 devices: a whole 2x2x4 slice. The times are simulated.
32 devices in a mesh: ctx: 8 (over z, x), fsdp: 4 (over y, core).
Axes of the slice: x: 2, y: 2, z: 4, core: 2. Of those that a mesh axis runs over, the one named last changes fastest.
Arguments:
- tokens: bfloat16 [4, 1024, 1536], P('fsdp', 'ctx'), may hold values from -6 to 6
- segments: int32 [4, 1024], P('fsdp'), may hold values from 0 to 3, never falling along the last dimension, each value on 1 to 512 neighbouring positions
- gain_attn: bfloat16 [1536], replicated, may hold values from 0.5 to 1.5
- w_query: bfloat16 [1536, 1536], P('fsdp'), may hold values from -0.15625 to 0.15625
- w_key: bfloat16 [1536, 1536], P('fsdp'), may hold values from -0.15625 to 0.15625
- w_value: bfloat16 [1536, 1536], P('fsdp'), may hold values from -0.15625 to 0.15625
- w_forget: bfloat16 [1536, 24], P('fsdp'), may hold values from -0.15625 to 0.15625
- forget_bias: float32 [24], replicated, may hold values from 2 to 8
- w_outgate: bfloat16 [1536, 1536], P('fsdp'), may hold values from -0.15625 to 0.15625
- w_out: bfloat16 [1536, 1536], P('fsdp'), may hold values from -0.625 to 0.625
- gain_ffn: bfloat16 [1536], replicated, may hold values from 0.5 to 1.5
- w_gate: bfloat16 [1536, 4096], P('fsdp'), may hold values from -0.15625 to 0.15625
- w_up: bfloat16 [1536, 4096], P('fsdp'), may hold values from -0.15625 to 0.15625
- w_down: bfloat16 [4096, 1536], P('fsdp'), may hold values from -0.09375 to 0.09375
- cotangent: bfloat16 [4, 1024, 1536], P('fsdp', 'ctx'), may hold values from -6 to 6
Outputs:
- output: bfloat16 [4, 1024, 1536], P('fsdp', 'ctx')
- grad_tokens: float32 [4, 1024, 1536], P('fsdp', 'ctx')
- grad_gain_attn: float32 [1536], replicated
- grad_query: float32 [1536, 1536], P('fsdp')
- grad_key: float32 [1536, 1536], P('fsdp')
- grad_value: float32 [1536, 1536], P('fsdp')
- grad_forget: float32 [1536, 24], P('fsdp')
- grad_bias: float32 [24], replicated
- grad_outgate: float32 [1536, 1536], P('fsdp')
- grad_out: float32 [1536, 1536], P('fsdp')
- grad_gain_ffn: float32 [1536], replicated
- grad_gate: float32 [1536, 4096], P('fsdp')
- grad_up: float32 [1536, 4096], P('fsdp')
- grad_down: float32 [4096, 1536], P('fsdp')
Inputs may be any that keep to these rules, and one draw needn't show every extreme that they name: `segments`: along each sequence the document numbers never fall; every document has 1 to 512 tokens and one has exactly 512.
All inputs are finite; a program needn't handle non-finite values.
Results may differ from a plain program's by a relative error of at most 0.014.
Values may be sent and summed in bfloat16 or wider, within the bound.
A program may use at most 448 MiB of HBM per device.

v0:
```python
import math

import jax
import jax.numpy as jnp
from jax import lax
from jax.sharding import PartitionSpec as P

EPSILON = 1e-06
NEGATIVE = -1e30


def entering(value, axis, join, neutral, backward):
    count, mine = (lax.axis_size(axis), lax.axis_index(axis))
    pieces = lax.all_gather(value, axis)
    if backward:
        pieces = pieces[::-1]
        mine = count - 1 - mine
    subtotal = jnp.full_like(value, 0) + jnp.asarray(neutral, value.dtype)

    def hop(position, subtotal):
        longer = join(subtotal, pieces[position])
        return jnp.where(position < mine, longer, subtotal)

    return lax.fori_loop(0, count - 1, hop, subtotal)


def matmul(left, right):
    return jnp.dot(left, right, preferred_element_type=jnp.float32)


def matmul_rows(left, right):
    return lax.dot_general(
        left, right, (((1,), (1,)), ((), ())), preferred_element_type=jnp.float32
    )


def weight_grad(left, right):
    return lax.dot_general(
        left, right, (((0,), (0,)), ((), ())), preferred_element_type=jnp.float32
    )


def rms_stats(values):
    rstat = lax.rsqrt(jnp.mean(values * values, axis=-1, keepdims=True) + EPSILON)
    return (values * rstat, rstat)


def norm_back(grad_in, normed, rstat, gain):
    grad_normed = grad_in * gain
    grad_gain = jnp.sum(grad_in * normed, axis=0)
    grad_values = rstat * (
        grad_normed - normed * jnp.mean(grad_normed * normed, axis=-1, keepdims=True)
    )
    return (grad_values, grad_gain)


def shards(
    tokens,
    segments,
    gain_attn,
    w_query,
    w_key,
    w_value,
    w_forget,
    forget_bias,
    w_outgate,
    w_out,
    gain_ffn,
    w_gate,
    w_up,
    w_down,
    cotangent,
):
    gathered = (
        lax.all_gather(w_query, "fsdp", axis=0, tiled=True),
        lax.all_gather(w_key, "fsdp", axis=0, tiled=True),
        lax.all_gather(w_value, "fsdp", axis=0, tiled=True),
        lax.all_gather(w_forget, "fsdp", axis=0, tiled=True),
        lax.all_gather(w_outgate, "fsdp", axis=0, tiled=True),
        lax.all_gather(w_out, "fsdp", axis=0, tiled=True),
        lax.all_gather(w_gate, "fsdp", axis=0, tiled=True),
        lax.all_gather(w_up, "fsdp", axis=0, tiled=True),
        lax.all_gather(w_down, "fsdp", axis=0, tiled=True),
    )
    (
        full_query,
        full_key,
        full_value,
        full_forget,
        full_outgate,
        full_out,
        full_gate,
        full_up,
        full_down,
    ) = gathered
    inputs = tokens[0].astype(jnp.float32)
    tok_rows = inputs.shape[0]
    model_width = inputs.shape[1]
    n_heads = forget_bias.shape[0]
    head_dim = model_width // n_heads
    per_group = math.gcd(n_heads, 2)
    n_groups = n_heads // per_group
    group_width = per_group * head_dim
    scaling = head_dim ** (-0.5)
    n_ctx = lax.axis_size("ctx")
    position = lax.axis_index("ctx")
    seq_rows = tok_rows * n_ctx
    seg_all = segments[0]
    first_row = position * tok_rows
    pos_here = first_row + jnp.arange(tok_rows, dtype=jnp.int32)
    seg_here = lax.dynamic_slice_in_dim(seg_all, first_row, tok_rows, 0)
    pos_all = jnp.arange(seq_rows, dtype=jnp.int32)
    allowed = (pos_all[None, :] <= pos_here[:, None]) & (seg_all[None, :] == seg_here[:, None])
    gain_one = gain_attn.astype(jnp.float32)
    normed_one, rstat_one = rms_stats(inputs)
    normed = (normed_one * gain_one).astype(jnp.bfloat16)
    queries = matmul(normed, full_query).astype(jnp.bfloat16)
    key_own = matmul(normed, full_key).astype(jnp.bfloat16)
    value_own = matmul(normed, full_value).astype(jnp.bfloat16)
    forget_logits = matmul(normed, full_forget) + forget_bias
    log_keep = jax.nn.log_sigmoid(forget_logits)
    before = entering(
        jnp.sum(log_keep, axis=0), "ctx", jnp.add, jnp.zeros((n_heads,), jnp.float32), False
    )
    sent_rows = before[None, :] + jnp.cumsum(log_keep, axis=0)
    arrived = lax.all_gather(sent_rows, "ctx", axis=0, tiled=True)
    keys_all, values_all = (
        lax.all_gather(key_own, "ctx", axis=0, tiled=True),
        lax.all_gather(value_own, "ctx", axis=0, tiled=True),
    )

    def group_slices(group_index):
        column = group_index * group_width
        query_part = lax.dynamic_slice_in_dim(queries, column, group_width, 1).reshape(
            tok_rows, per_group, head_dim
        )
        key_part = lax.dynamic_slice_in_dim(keys_all, column, group_width, 1).reshape(
            seq_rows, per_group, head_dim
        )
        value_part = lax.dynamic_slice_in_dim(values_all, column, group_width, 1).reshape(
            seq_rows, per_group, head_dim
        )
        decay_rows = lax.dynamic_slice_in_dim(sent_rows, group_index * per_group, per_group, 1)
        decay_keys = lax.dynamic_slice_in_dim(arrived, group_index * per_group, per_group, 1)
        scores = (
            jnp.einsum("bhd,nhd->hbn", query_part, key_part, preferred_element_type=jnp.float32)
            * scaling
        )
        scores = scores + decay_rows.T[:, :, None] - decay_keys.T[:, None, :]
        scores = jnp.where(allowed[None], scores, NEGATIVE)
        return (query_part, key_part, value_part, scores)

    def forward_group(group_index):
        query_part, key_part, value_part, scores = group_slices(group_index)
        row_max = jnp.max(scores, axis=-1, keepdims=True)
        raised = jnp.exp(scores - row_max)
        row_total = jnp.sum(raised, axis=-1, keepdims=True)
        probabilities = raised / row_total
        mixed_part = jnp.einsum(
            "hbn,nhd->bhd",
            probabilities.astype(jnp.bfloat16),
            value_part,
            preferred_element_type=jnp.float32,
        )
        return (mixed_part.reshape(tok_rows, group_width), (row_max + jnp.log(row_total))[:, :, 0])

    mixed_groups, log_totals = lax.map(forward_group, jnp.arange(n_groups, dtype=jnp.int32))
    attended = jnp.moveaxis(mixed_groups, 0, 1).reshape(tok_rows, model_width)
    gate_logits = matmul(normed, full_outgate)
    gate_value = jax.nn.sigmoid(gate_logits)
    gated_out = (attended * gate_value).astype(jnp.bfloat16)
    middle = inputs + matmul(gated_out, full_out)
    gain_two = gain_ffn.astype(jnp.float32)
    normed_two_f, rstat_two = rms_stats(middle)
    normed_two = (normed_two_f * gain_two).astype(jnp.bfloat16)
    gate_part = matmul(normed_two, full_gate)
    up_part = matmul(normed_two, full_up)
    sig_gate = jax.nn.sigmoid(gate_part)
    silu_gate = gate_part * sig_gate
    hidden = (silu_gate * up_part).astype(jnp.bfloat16)
    output = middle + matmul(hidden, full_down)
    grad_out_low = cotangent[0]
    grad_output = grad_out_low.astype(jnp.float32)
    grad_hidden = matmul_rows(grad_out_low, full_down)
    grad_gate_low = (
        grad_hidden * up_part * (sig_gate * (1.0 + gate_part * (1.0 - sig_gate)))
    ).astype(jnp.bfloat16)
    grad_up_low = (grad_hidden * silu_gate).astype(jnp.bfloat16)
    grad_normed_two = matmul_rows(grad_gate_low, full_gate) + matmul_rows(grad_up_low, full_up)
    back_two, grad_gain_two = norm_back(grad_normed_two, normed_two_f, rstat_two, gain_two)
    grad_middle = grad_output + back_two
    ffn_parts = (
        lax.psum_scatter(
            weight_grad(normed_two, grad_gate_low), "fsdp", scatter_dimension=0, tiled=True
        ),
        lax.psum_scatter(
            weight_grad(normed_two, grad_up_low), "fsdp", scatter_dimension=0, tiled=True
        ),
        lax.psum_scatter(
            weight_grad(hidden, grad_out_low), "fsdp", scatter_dimension=0, tiled=True
        ),
    )
    grad_branch_low = grad_middle.astype(jnp.bfloat16)
    grad_gated = matmul_rows(grad_branch_low, full_out)
    grad_attn_low = (grad_gated * gate_value).astype(jnp.bfloat16)
    grad_gatelog_low = (grad_gated * attended * (gate_value * (1.0 - gate_value))).astype(
        jnp.bfloat16
    )

    def backward_group(group_index, carried):
        grad_queries, grad_keys, grad_values, grad_rowdecay, grad_keydecay = carried
        query_part, key_part, value_part, scores = group_slices(group_index)
        probabilities = jnp.exp(scores - log_totals[group_index][:, :, None])
        column = group_index * group_width
        grad_part = lax.dynamic_slice_in_dim(grad_attn_low, column, group_width, 1).reshape(
            tok_rows, per_group, head_dim
        )
        grad_vpart = jnp.einsum(
            "hbn,bhd->nhd",
            probabilities.astype(jnp.bfloat16),
            grad_part,
            preferred_element_type=jnp.float32,
        )
        grad_probs = jnp.einsum(
            "bhd,nhd->hbn", grad_part, value_part, preferred_element_type=jnp.float32
        )
        row_inner = jnp.sum(probabilities * grad_probs, axis=-1, keepdims=True)
        grad_scores = (probabilities * (grad_probs - row_inner)).astype(jnp.bfloat16)
        grad_qpart = (
            jnp.einsum("hbn,nhd->bhd", grad_scores, key_part, preferred_element_type=jnp.float32)
            * scaling
        )
        grad_kpart = (
            jnp.einsum("hbn,bhd->nhd", grad_scores, query_part, preferred_element_type=jnp.float32)
            * scaling
        )
        score_sums = grad_scores.astype(jnp.float32)
        grad_queries = lax.dynamic_update_slice_in_dim(
            grad_queries, grad_qpart.reshape(tok_rows, group_width), column, 1
        )
        grad_keys = lax.dynamic_update_slice_in_dim(
            grad_keys, grad_kpart.reshape(seq_rows, group_width), column, 1
        )
        grad_values = lax.dynamic_update_slice_in_dim(
            grad_values, grad_vpart.reshape(seq_rows, group_width), column, 1
        )
        grad_rowdecay = lax.dynamic_update_slice_in_dim(
            grad_rowdecay, jnp.sum(score_sums, axis=-1).T, group_index * per_group, 1
        )
        grad_keydecay = lax.dynamic_update_slice_in_dim(
            grad_keydecay, -jnp.sum(score_sums, axis=1).T, group_index * per_group, 1
        )
        return (grad_queries, grad_keys, grad_values, grad_rowdecay, grad_keydecay)

    initial = (
        jnp.zeros((tok_rows, model_width), jnp.float32),
        jnp.zeros((seq_rows, model_width), jnp.float32),
        jnp.zeros((seq_rows, model_width), jnp.float32),
        jnp.zeros((tok_rows, n_heads), jnp.float32),
        jnp.zeros((seq_rows, n_heads), jnp.float32),
    )
    grad_queries, grad_keys, grad_values, grad_rowdecay, grad_keydecay = lax.fori_loop(
        0, n_groups, backward_group, initial
    )
    key_back = (
        lax.psum_scatter(grad_keys, "ctx", scatter_dimension=0, tiled=True),
        lax.psum_scatter(grad_values, "ctx", scatter_dimension=0, tiled=True),
        lax.psum_scatter(grad_keydecay, "ctx", scatter_dimension=0, tiled=True),
    )
    grad_query_low = grad_queries.astype(jnp.bfloat16)
    grad_key_low = key_back[0].astype(jnp.bfloat16)
    grad_value_low = key_back[1].astype(jnp.bfloat16)
    decay_grad = grad_rowdecay + key_back[2]
    local_suffix = jnp.flip(jnp.cumsum(jnp.flip(decay_grad, 0), axis=0), 0)
    block_total = jnp.sum(decay_grad, axis=0)
    later_sum = entering(block_total, "ctx", jnp.add, jnp.zeros((n_heads,), jnp.float32), True)
    grad_logits_low = ((local_suffix + later_sum[None, :]) * jax.nn.sigmoid(-forget_logits)).astype(
        jnp.bfloat16
    )
    grad_bias = jnp.sum(grad_logits_low.astype(jnp.float32), axis=0)
    grad_normed = (
        matmul_rows(grad_query_low, full_query)
        + matmul_rows(grad_key_low, full_key)
        + matmul_rows(grad_value_low, full_value)
        + matmul_rows(grad_logits_low, full_forget)
        + matmul_rows(grad_gatelog_low, full_outgate)
    )
    back_one, grad_gain_one = norm_back(grad_normed, normed_one, rstat_one, gain_one)
    grad_inputs = grad_middle + back_one
    attn_parts = (
        lax.psum_scatter(
            weight_grad(normed, grad_query_low), "fsdp", scatter_dimension=0, tiled=True
        ),
        lax.psum_scatter(
            weight_grad(normed, grad_key_low), "fsdp", scatter_dimension=0, tiled=True
        ),
        lax.psum_scatter(
            weight_grad(normed, grad_value_low), "fsdp", scatter_dimension=0, tiled=True
        ),
        lax.psum_scatter(
            weight_grad(normed, grad_logits_low), "fsdp", scatter_dimension=0, tiled=True
        ),
        lax.psum_scatter(
            weight_grad(normed, grad_gatelog_low), "fsdp", scatter_dimension=0, tiled=True
        ),
        lax.psum_scatter(
            weight_grad(gated_out, grad_branch_low), "fsdp", scatter_dimension=0, tiled=True
        ),
    )
    summed = lax.psum(
        (
            ffn_parts[0],
            ffn_parts[1],
            ffn_parts[2],
            attn_parts[0],
            attn_parts[1],
            attn_parts[2],
            attn_parts[3],
            attn_parts[4],
            attn_parts[5],
        ),
        "ctx",
    )
    small_grads = lax.psum((grad_gain_one, grad_gain_two, grad_bias), ("ctx", "fsdp"))
    return (
        output.astype(jnp.bfloat16)[None],
        grad_inputs[None],
        small_grads[0],
        summed[3],
        summed[4],
        summed[5],
        summed[6],
        small_grads[2],
        summed[7],
        summed[8],
        small_grads[1],
        summed[0],
        summed[1],
        summed[2],
    )


def solution(mesh):
    return jax.shard_map(
        shards,
        mesh=mesh,
        in_specs=(
            P("fsdp", "ctx", None),
            P("fsdp", None),
            P(),
            P("fsdp", None),
            P("fsdp", None),
            P("fsdp", None),
            P("fsdp", None),
            P(),
            P("fsdp", None),
            P("fsdp", None),
            P(),
            P("fsdp", None),
            P("fsdp", None),
            P("fsdp", None),
            P("fsdp", "ctx", None),
        ),
        out_specs=(
            P("fsdp", "ctx", None),
            P("fsdp", "ctx", None),
            P(),
            P("fsdp", None),
            P("fsdp", None),
            P("fsdp", None),
            P("fsdp", None),
            P(),
            P("fsdp", None),
            P("fsdp", None),
            P(),
            P("fsdp", None),
            P("fsdp", None),
            P("fsdp", None),
        ),
        check_vma=False,
    )
```

profile of v0, /device:TPU:0, one launch (start us, length us, event | category | flops | bytes accessed | tf_op | source)
XLA Modules:
  0.0 2965.8 jit_solution(18028929066030934375)
XLA Ops:
  11.3 38.5 %all-gather.13.cloned.1.call-done = bf16[1536,1536]{1,0:T(8,128)(2,1)} async-done(((bf16[384,1536]{1,0:T(8,128)(2,1)}), bf16[1536,1536]{1,0:T(8,128)(2,1)}) %all-gather.13.cloned.1.call-update) | async-done | bytes 4718608 | tf_op jit(solution)/shard_map/all_gather | solution.py:77
  53.9 34.9 %all-gather.19.cloned.1.call-done = bf16[1536,1536]{1,0:T(8,128)(2,1)} async-done(((bf16[384,1536]{1,0:T(8,128)(2,1)}), bf16[1536,1536]{1,0:T(8,128)(2,1)}) %all-gather.19.cloned.1.call-update) | async-done | bytes 4718608 | tf_op jit(solution)/shard_map/all_gather | solution.py:76
  104.7 21.3 all-reduce
  127.3 32.3 %all_gather.53 = f32[1024,24]{1,0:T(8,128)S(1)} all-gather(f32[128,24]{1,0:T(8,128)S(1)} %broadcast_add_fusion), channel_id=1, replica_groups=mesh['ctx'=8,'fsdp'=4] {'ctx'}, dimensions={0}, use_global_device_ids=true | all-gather | bytes 110592 | tf_op jit(solution)/shard_map/all_gather | solution.py:126
  166.2 26.6 all-gather.15.cloned.1.call-done
  195.9 58.5 %all-gather.21.cloned.1.call-done = bf16[1024,1536]{1,0:T(8,128)(2,1)} async-done(((bf16[128,1536]{1,0:T(8,128)(2,1)}), bf16[1024,1536]{1,0:T(8,128)(2,1)}) %all-gather.21.cloned.1.call-update) | async-done | bytes 3145744 | tf_op jit(solution)/shard_map/all_gather | solution.py:128
  259.6 142.1 %while.63 = (s32[]{:T(128)}, f32[12,128,128]{1,2,0:T(8,128)}, f32[12,2,128]{2,1,0:T(2,128)}, s32[12]{0:T(128)}, bf16[1024,1536]{0,1:T(8,128)(2,1)S(1)}, /*index=...) while((s32[]{:T(128)}, f32[12,128,128]{1,2,0:T(8,128)}, ...), condition=%wide.region_8.9_spmd.clone, body=%wide.region_5.8_spmd.clone.sunk | while | flops 70123272 | bytes 5316909 | solution.py:167
  414.8 7.7 fusion.77
  422.5 76.0 %all-gather.29.cloned.1.call-done = bf16[1536,4096]{1,0:T(8,128)(2,1)} async-done(((bf16[384,4096]{1,0:T(8,128)(2,1)}), bf16[1536,4096]{1,0:T(8,128)(2,1)}) %all-gather.29.cloned.1.call-update) | async-done | bytes 12582928 | tf_op jit(solution)/shard_map/all_gather | solution.py:82
  498.5 7.7 fusion.78
  506.2 75.9 %all-gather.31.cloned.1.call-done = bf16[4096,1536]{1,0:T(8,128)(2,1)} async-done(((bf16[1024,1536]{1,0:T(8,128)(2,1)}), bf16[4096,1536]{1,0:T(8,128)(2,1)}) %all-gather.31.cloned.1.call-update) | async-done | bytes 12582928 | tf_op jit(solution)/shard_map/all_gather | solution.py:83
  582.1 11.7 multiply_convert_fusion.1
  593.8 10.2 fusion.79
  626.1 118.0 %while.64 = (s32[]{:T(128)}, bf16[128,1536]{0,1:T(8,128)(2,1)}, f32[1024,1536]{0,1:T(8,128)}, f32[1024,1536]{0,1:T(8,128)}, f32[128,24]{0,1:T(8,128)S(1)}, /*ind...) while((s32[]{:T(128)}, bf16[128,1536]{0,1:T(8,128)(2,1)}, ...), condition=%wide.region_15.16_spmd.clone, body=%wide.region_11.15_spmd.clone.sunk | while | flops 171998720 | bytes 13599061 | solution.py:262
  763.0 99.6 %reduce-scatter.13.cloned.1.call-done = f32[128,1536]{0,1:T(8,128)} async-done(((f32[1024,1536]{0,1:T(8,128)}), f32[128,1536]{0,1:T(8,128)}) %reduce-scatter.13.cloned.1.call-update) | async-done | bytes 786448 | tf_op jit(solution)/shard_map/reduce_scatter | solution.py:266
  869.4 114.9 %reduce-scatter.15.cloned.1.call-done = f32[128,1536]{0,1:T(8,128)} async-done(((f32[1024,1536]{0,1:T(8,128)}), f32[128,1536]{0,1:T(8,128)}) %reduce-scatter.15.cloned.1.call-update) | async-done | bytes 786448 | tf_op jit(solution)/shard_map/reduce_scatter | solution.py:267
  990.5 11.4 fusion.81
  1001.9 11.4 fusion.82
  1014.3 11.5 fusion.42
  1025.9 19.3 reduce-scatter.17.cloned.1.call-done
  1046.7 19.5 all-reduce.1
  1067.7 57.4 %reduce-scatter.19.cloned.1.call-done = f32[384,1536]{1,0:T(8,128)} async-done(((f32[1536,1536]{1,0:T(8,128)}), f32[384,1536]{1,0:T(8,128)}) %reduce-scatter.19.cloned.1.call-update) | async-done | bytes 2359312 | tf_op jit(solution)/shard_map/reduce_scatter | solution.py:291
  1125.1 80.9 %reduce-scatter.27.cloned.1.call-done = f32[384,1536]{1,0:T(8,128)} async-done(((f32[1536,1536]{1,0:T(8,128)}), f32[384,1536]{1,0:T(8,128)}) %reduce-scatter.27.cloned.1.call-update) | async-done | bytes 2359312 | tf_op jit(solution)/shard_map/reduce_scatter | solution.py:303
  1206.0 80.9 %reduce-scatter.29.cloned.1.call-done = f32[384,1536]{1,0:T(8,128)} async-done(((f32[1536,1536]{1,0:T(8,128)}), f32[384,1536]{1,0:T(8,128)}) %reduce-scatter.29.cloned.1.call-update) | async-done | bytes 2359312 | tf_op jit(solution)/shard_map/reduce_scatter | solution.py:306
  1286.9 80.9 %reduce-scatter.21.cloned.1.call-done = f32[384,1536]{1,0:T(8,128)} async-done(((f32[1536,1536]{1,0:T(8,128)}), f32[384,1536]{1,0:T(8,128)}) %reduce-scatter.21.cloned.1.call-update) | async-done | bytes 2359312 | tf_op jit(solution)/shard_map/reduce_scatter | solution.py:294
  1367.8 80.9 %reduce-scatter.23.cloned.1.call-done = f32[384,1536]{1,0:T(8,128)} async-done(((f32[1536,1536]{1,0:T(8,128)}), f32[384,1536]{1,0:T(8,128)}) %reduce-scatter.23.cloned.1.call-update) | async-done | bytes 2359312 | tf_op jit(solution)/shard_map/reduce_scatter | solution.py:297
  1448.7 183.1 %reduce-scatter.31.cloned.1.call-done = f32[384,4096]{1,0:T(8,128)} async-done(((f32[1536,4096]{1,0:T(8,128)}), f32[384,4096]{1,0:T(8,128)}) %reduce-scatter.31.cloned.1.call-update) | async-done | bytes 6291472 | tf_op jit(solution)/shard_map/reduce_scatter | solution.py:193
  1631.8 183.1 %reduce-scatter.33.cloned.1.call-done = f32[384,4096]{1,0:T(8,128)} async-done(((f32[1536,4096]{1,0:T(8,128)}), f32[384,4096]{1,0:T(8,128)}) %reduce-scatter.33.cloned.1.call-update) | async-done | bytes 6291472 | tf_op jit(solution)/shard_map/reduce_scatter | solution.py:196
  1814.9 183.1 %reduce-scatter.35.cloned.1.call-done = f32[1024,1536]{1,0:T(8,128)} async-done(((f32[4096,1536]{1,0:T(8,128)}), f32[1024,1536]{1,0:T(8,128)}) %reduce-scatter.35.cloned.1.call-update) | async-done | bytes 6291472 | tf_op jit(solution)/shard_map/reduce_scatter | solution.py:199
  2020.8 40.6 %psum.88 = f32[384,24]{0,1:T(8,128)} all-reduce(f32[384,24]{0,1:T(8,128)} %reduce-scatter.25.cloned.1.call-done), channel_id=1, replica_groups=mesh['ctx'=8,'fsdp'=4] {'ctx'}, use_global_device_ids=true, to_apply=%region_33.34 | all-reduce | flops 9216 | bytes 73728 | tf_op jit(solution)/shard_map/psum | solution.py:310
  2070.5 40.4 %all-reduce.2 = (f32[1536]{0:T(1024)}, f32[24]{0:T(128)}, f32[1536]{0:T(1024)}) all-reduce(f32[1536]{0:T(1024)S(1)} %get-tuple-element.623, f32[24]{0:T(128)S(1)} %get-tuple-element.709, f32[1536]{0:T(1024)S(1)} %copy-done.23), channel_id=1, replica_groups=mesh['ctx'=8,'fsdp'=4] {'ctx','fsdp'}, use_global_device_ids=true, to_apply=%region_25.26 | all-reduce | flops 3096 | bytes 24768 | tf_op jit(solution)/shard_map/psum | solution.py:324
  2112.0 825.1 %all-reduce.6.cloned.1.call-done = (f32[384,1536]{1,0:T(8,128)}, f32[384,1536]{1,0:T(8,128)}, f32[384,1536]{1,0:T(8,128)}, f32[384,1536]{1,0:T(8,128)}, f32[384,...) async-done(((f32[384,1536]{1,0:T(8,128)}, f32[384,1536]{1,0:T(8,128)}, f32[384,1536]{1,0:T(8,128)}, f32[384,1536]{1,0:T(8,128)}, ...) | async-done | bytes 30670864 | tf_op jit(solution)/shard_map/psum | solution.py:310
  (575 shorter events, 408.5 us)
Async XLA Ops:
  7.2 81.7 %copy-start.1 = (bf16[1,128,1536]{2,1,0:T(8,128)(2,1)S(1)}, bf16[1,128,1536]{2,1,0:T(8,128)(2,1)}, u32[]{:S(2)}) copy-start(bf16[1,128,1536]{2,1,0:T(8,128)(2,1)} %param.23) | copy-start | bytes 1179652
  7.2 42.6 %all-gather.13.cloned.1.call-start = ((), (), s32[]{:S(2)}) async-start(), calls=%async_computation.12 | async-start | bytes 5898240 | tf_op jit(solution)/shard_map/all_gather | solution.py:77
  7.9 80.9 %all-gather.19.cloned.1.call-start = ((), (), s32[]{:S(2)}) async-start(), calls=%async_computation.15 | async-start | bytes 5898240 | tf_op jit(solution)/shard_map/all_gather | solution.py:76
  8.7 153.4 %all-gather.17.cloned.1.call-start = ((), (), s32[]{:S(2)}) async-start(), calls=%async_computation.14 | async-start | bytes 5898240 | tf_op jit(solution)/shard_map/all_gather | solution.py:75
  9.4 183.3 %all-gather.15.cloned.1.call-start = ((), (), s32[]{:S(2)}) async-start(), calls=%async_computation.13 | async-start | bytes 3538944 | tf_op jit(solution)/shard_map/all_gather | solution.py:129
  53.9 200.6 %all-gather.21.cloned.1.call-start = ((), (), s32[]{:S(2)}) async-start(), calls=%async_computation.16 | async-start | bytes 3538944 | tf_op jit(solution)/shard_map/all_gather | solution.py:128
  92.8 311.7 %all-gather.23.cloned.1.call-start = ((), (), s32[]{:S(2)}) async-start(), calls=%async_computation.17 | async-start | bytes 5898240 | tf_op jit(solution)/shard_map/all_gather | solution.py:79
  93.4 315.8 %all-gather.25.cloned.1.call-start = ((), (), s32[]{:S(2)}) async-start(), calls=%async_computation.18 | async-start | bytes 5898240 | tf_op jit(solution)/shard_map/all_gather | solution.py:80
  94.1 320.6 %all-gather.27.cloned.1.call-start = ((), (), s32[]{:S(2)}) async-start(), calls=%async_computation.19 | async-start | bytes 15728640 | tf_op jit(solution)/shard_map/all_gather | solution.py:81
  94.9 66.0 %copy-start.26 = (bf16[1536]{0:T(1024)(128)(2,1)S(1)}, bf16[1536]{0:T(1024)(128)(2,1)}, u32[]{:S(2)}) copy-start(bf16[1536]{0:T(1024)(128)(2,1)} %param.33) | copy-start | bytes 9220
  94.9 66.6 %copy-start.16 = (s32[1,1024]{1,0:T(1,128)S(1)}, s32[1,1024]{1,0:T(1,128)}, u32[]{:S(2)}) copy-start(s32[1,1024]{1,0:T(1,128)} %param.24) | copy-start | bytes 12292
  94.9 403.5 %all-gather.29.cloned.1.call-start = ((), (), s32[]{:S(2)}) async-start(), calls=%async_computation.20 | async-start | bytes 15728640 | tf_op jit(solution)/shard_map/all_gather | solution.py:82
  95.6 486.4 %all-gather.31.cloned.1.call-start = ((), (), s32[]{:S(2)}) async-start(), calls=%async_computation.21 | async-start | bytes 15728640 | tf_op jit(solution)/shard_map/all_gather | solution.py:83
  96.2 766.4 %reduce-scatter.13.cloned.1.call-start = ((), (), s32[]{:S(2)}) async-start(), calls=%async_computation.22 | async-start | bytes 7077888 | tf_op jit(solution)/shard_map/reduce_scatter | solution.py:266
  422.5 159.6 %copy-start.14 = (bf16[1,128,1536]{2,1,0:T(8,128)(2,1)S(1)}, bf16[1,128,1536]{2,1,0:T(8,128)(2,1)}, u32[]{:S(2)}) copy-start(bf16[1,128,1536]{2,1,0:T(8,128)(2,1)} %param.37) | copy-start | bytes 1179652
  593.8 10.2 copy-start
  744.2 240.0 %reduce-scatter.15.cloned.1.call-start = ((), (), s32[]{:S(2)}) async-start(), calls=%async_computation.23 | async-start | bytes 7077888 | tf_op jit(solution)/shard_map/reduce_scatter | solution.py:267
  744.8 300.4 %reduce-scatter.17.cloned.1.call-start = ((), (), s32[]{:S(2)}) async-start(), calls=%async_computation.24 | async-start | bytes 110592 | tf_op jit(solution)/shard_map/reduce_scatter | solution.py:268
  745.5 379.6 %reduce-scatter.19.cloned.1.call-start = ((), (), s32[]{:S(2)}) async-start(), calls=%async_computation.25 | async-start | bytes 11796480 | tf_op jit(solution)/shard_map/reduce_scatter | solution.py:291
  750.8 455.2 %reduce-scatter.27.cloned.1.call-start = ((), (), s32[]{:S(2)}) async-start(), calls=%async_computation.29 | async-start | bytes 11796480 | tf_op jit(solution)/shard_map/reduce_scatter | solution.py:303
  755.9 531.1 %reduce-scatter.29.cloned.1.call-start = ((), (), s32[]{:S(2)}) async-start(), calls=%async_computation.30 | async-start | bytes 11796480 | tf_op jit(solution)/shard_map/reduce_scatter | solution.py:306
  763.0 604.8 %reduce-scatter.21.cloned.1.call-start = ((), (), s32[]{:S(2)}) async-start(), calls=%async_computation.26 | async-start | bytes 11796480 | tf_op jit(solution)/shard_map/reduce_scatter | solution.py:294
  868.9 579.8 %reduce-scatter.23.cloned.1.call-start = ((), (), s32[]{:S(2)}) async-start(), calls=%async_computation.27 | async-start | bytes 11796480 | tf_op jit(solution)/shard_map/reduce_scatter | solution.py:297
  990.4 641.4 %reduce-scatter.31.cloned.1.call-start = ((), (), s32[]{:S(2)}) async-start(), calls=%async_computation.31 | async-start | bytes 31457280 | tf_op jit(solution)/shard_map/reduce_scatter | solution.py:193
  1001.9 813.0 %reduce-scatter.33.cloned.1.call-start = ((), (), s32[]{:S(2)}) async-start(), calls=%async_computation.32 | async-start | bytes 31457280 | tf_op jit(solution)/shard_map/reduce_scatter | solution.py:196
  1013.3 984.6 %reduce-scatter.35.cloned.1.call-start = ((), (), s32[]{:S(2)}) async-start(), calls=%async_computation.33 | async-start | bytes 31457280 | tf_op jit(solution)/shard_map/reduce_scatter | solution.py:199
  1025.8 40.7 %copy-start.25 = (f32[128,24]{0,1:T(8,128)S(1)}, f32[128,24]{0,1:T(8,128)}, u32[]{:S(2)}) copy-start(f32[128,24]{0,1:T(8,128)} %get-tuple-element.728) | copy-start | bytes 36868
  1025.8 995.0 %reduce-scatter.25.cloned.1.call-start = ((), (), s32[]{:S(2)}) async-start(), calls=%async_computation.28 | async-start | bytes 184320 | tf_op jit(solution)/shard_map/reduce_scatter | solution.py:300
  1067.6 1869.5 %all-reduce.6.cloned.1.call-start = ((), (), s32[]{:S(2)}) async-start(), calls=%async_computation.34 | async-start | bytes 61341696 | tf_op jit(solution)/shard_map/psum | solution.py:310
  1998.0 9.8 copy-start.5
  2007.8 53.6 %copy-start.7 = (f32[128,1536]{0,1:T(8,128)S(1)}, f32[128,1536]{0,1:T(8,128)}, u32[]{:S(2)}) copy-start(f32[128,1536]{0,1:T(8,128)} %reduce-scatter.13.cloned.1.call-done) | copy-start | bytes 2359300
  2015.0 50.7 %copy-start.8 = (f32[128,1536]{0,1:T(8,128)S(1)}, f32[128,1536]{0,1:T(8,128)}, u32[]{:S(2)}) copy-start(f32[128,1536]{0,1:T(8,128)} %reduce-scatter.15.cloned.1.call-done) | copy-start | bytes 2359300
  (26 other events, 111.4 us)
Sparse Core Ops, SparseCore 0:
  9.6 40.1 all-gather.12
  51.3 37.4 all-gather.18
  90.4 37.4 all-gather.16
  130.5 62.1 all-gather.14
  195.3 59.0 all-gather.20
  255.9 36.0 all-gather.22
  293.5 37.4 all-gather.24
  332.6 82.1 all-gather.26
  416.3 82.0 all-gather.28
  499.9 82.1 all-gather.30
  744.3 118.2 reduce-scatter.12
  866.7 117.5 reduce-scatter.14
  988.0 57.0 reduce-scatter.16
  1047.6 77.4 reduce-scatter.18
  1127.6 78.4 reduce-scatter.26
  1208.5 78.4 reduce-scatter.28
  1289.4 78.3 reduce-scatter.20
  1370.3 78.4 reduce-scatter.22
  1451.3 180.4 reduce-scatter.30
  1634.4 180.4 reduce-scatter.32
  1817.5 180.4 reduce-scatter.34
  2001.1 19.6 reduce-scatter.24
  2027.5 909.5 all-reduce.5
where the time goes:
time: 2980 us; the launch traced here: 2970 us
  waiting for transfers between devices  2310 us (78%)
  matrix products  216 us (7%)
  local copies, waits for them, and re-layouts  208 us (7%)
  blocking collectives  159 us (5%)
  other arithmetic  34.6 us (1%)
    psum x1, waiting for transfers between devices, shards(): lax.psum((ffn_parts[0], ffn_parts[1], ffn_parts[2], attn_parts[0], attn_p...  825 us
    reduce_scatter x1, waiting for transfers between devices, shards(): lax.psum_scatter(weight_grad(normed_two, grad_up_low), 'fsdp', scatter_di...  183 us
    reduce_scatter x1, waiting for transfers between devices, shards(): lax.psum_scatter(weight_grad(hidden, grad_out_low), 'fsdp', scatter_dimen...  183 us
    reduce_scatter x1, waiting for transfers between devices, shards(): lax.psum_scatter(weight_grad(normed_two, grad_gate_low), 'fsdp', scatter_...  183 us
    reduce_scatter x1, waiting for transfers between devices, shards(): lax.psum_scatter(grad_values, 'ctx', scatter_dimension=0, tiled=True)  115 us
    reduce_scatter x1, waiting for transfers between devices, shards(): lax.psum_scatter(grad_keys, 'ctx', scatter_dimension=0, tiled=True)  99.6 us
    reduce_scatter x1, waiting for transfers between devices, shards(): lax.psum_scatter(weight_grad(normed, grad_value_low), 'fsdp', scatter_dim...  80.9 us
    reduce_scatter x1, waiting for transfers between devices, shards(): lax.psum_scatter(weight_grad(gated_out, grad_branch_low), 'fsdp', scatter...  80.9 us
  transfers between devices with their start and end apart: 23, of which 20 were waited for; matrix products, arithmetic and copies ran while one was open for 9% of the time, Pallas kernels for 0%

commit v1 on v0

v1 whole, which is shorter than its diff:
```python
import jax
import jax.numpy as jnp
from jax import lax
from jax.experimental import pallas as pl
from jax.experimental.pallas import tpu as pltpu
from jax.sharding import PartitionSpec as P

EPSILON = 1e-06
NEGATIVE = -1e30
BF16, F32 = jnp.bfloat16, jnp.float32


def matmul(left, right):
    return jnp.dot(left, right, preferred_element_type=F32)


def matmul_rows(left, right):
    return lax.dot_general(left, right, (((1,), (1,)), ((), ())), preferred_element_type=F32)


def weight_grad(left, right):
    return lax.dot_general(left, right, (((0,), (0,)), ((), ())), preferred_element_type=F32)


def rms_stats(values):
    rstat = lax.rsqrt(jnp.mean(values * values, axis=-1, keepdims=True) + EPSILON)
    return (values * rstat, rstat)


def norm_back(grad_in, normed, rstat, gain):
    grad_normed = grad_in * gain
    grad_gain = jnp.sum(grad_in * normed, axis=0)
    grad_values = rstat * (
        grad_normed - normed * jnp.mean(grad_normed * normed, axis=-1, keepdims=True)
    )
    return (grad_values, grad_gain)


MESH = pl.DeviceIdType.MESH
RING_PIECES = 4


def ring_place(ctx, count):
    odd = ctx % 2
    return ctx // 2 + odd * (count - 1 - 2 * (ctx // 2))


def ring_index(place, count):
    back = place // (count // 2)
    return 2 * place + back * (2 * (count - 1 - place) + 1 - 2 * place)


class Ring:
    def __init__(self, count):
        self.count, self.half = count, count // 2
        self.ctx, self.fsdp = lax.axis_index("ctx"), lax.axis_index("fsdp")
        self.place = ring_place(self.ctx, count)

    def at(self, offset):
        return ring_index((self.place + offset + self.count) % self.count, self.count)

    def device(self, offset):
        return (self.at(offset), self.fsdp)


def greet(devices):
    barrier = pltpu.get_barrier_semaphore()
    for device in devices:
        pl.semaphore_signal(barrier, inc=1, device_id=device, device_id_type=MESH)
    pl.semaphore_wait(barrier, len(devices))


def remote(src, dst, send, recv, device):
    return pltpu.make_async_remote_copy(
        src_ref=src, dst_ref=dst, send_sem=send, recv_sem=recv, device_id=device, device_id_type=MESH
    )


def carried(step, half, pieces, way):
    if step < half - 1:
        return range(pieces)
    return range(pieces // 2) if way == 0 else range(pieces // 2, pieces)


def ring_gather(ring, own, full, local_sem, send_sem, recv_sem, pieces=RING_PIECES):
    rows = own.shape[0] // pieces

    def part(k):
        return pl.ds(k * rows, rows)

    keep = pltpu.make_async_copy(own, full.at[ring.ctx], local_sem)
    keep.start()
    copies = {}
    for step in range(ring.half):
        for k in range(pieces):
            for way, sign in ((0, 1), (1, -1)):
                if k not in carried(step, ring.half, pieces, way):
                    continue
                if step > 0:
                    copies[step - 1, k, way].wait_recv()
                block = ring.at(-sign * step)
                src = own.at[part(k)] if step == 0 else full.at[block, part(k)]
                copy = remote(
                    src,
                    full.at[block, part(k)],
                    send_sem.at[step, k, way],
                    recv_sem.at[step, k, way],
                    ring.device(sign),
                )
                copy.start()
                copies[step, k, way] = copy
        yield
    for (step, k, way), copy in copies.items():
        if step == ring.half - 1 or k not in carried(step + 1, ring.half, pieces, way):
            copy.wait_recv()
    for copy in copies.values():
        copy.wait_send()
    keep.wait()


def ring_sum(ring, parts, held, total, send_sem, recv_sem, pieces=RING_PIECES):
    rows = parts.shape[1] // pieces

    def part(k):
        return pl.ds(k * rows, rows)

    copies = {}
    for step in range(ring.half):
        for k in range(pieces):
            for way, sign in ((0, 1), (1, -1)):
                if k not in carried(ring.half - 1 - step, ring.half, pieces, way):
                    continue
                block = ring.at(sign * (ring.half - step))
                src = parts.at[block, part(k)]
                if (step - 1, k, way) in copies:
                    copies[step - 1, k, way].wait_recv()
                    slot = held.at[way, step - 1, part(k)]
                    slot[...] = (slot[...].astype(F32) + src[...].astype(F32)).astype(BF16)
                    src = slot
                copy = remote(
                    src,
                    held.at[way, step, part(k)],
                    send_sem.at[step, k, way],
                    recv_sem.at[step, k, way],
                    ring.device(sign),
                )
                copy.start()
                copies[step, k, way] = copy
    last = ring.half - 1
    for k in range(pieces):
        for way in range(2):
            copies[last, k, way].wait_recv()
        total[part(k)] = (
            parts[ring.ctx, part(k)].astype(F32)
            + held[0, last, part(k)].astype(F32)
            + held[1, last, part(k)].astype(F32)
        )
    for copy in copies.values():
        copy.wait_send()


def ring_sems(count, pieces=RING_PIECES):
    shape = (count // 2, pieces, 2)
    return [pltpu.SemaphoreType.DMA(shape), pltpu.SemaphoreType.DMA(shape)]


def gather_rows(value, ident):
    count = lax.axis_size("ctx")

    def kernel(own, full, local_sem, send_sem, recv_sem):
        ring = Ring(count)
        greet([ring.device(1), ring.device(-1)])
        for _ in ring_gather(ring, own, full, local_sem, send_sem, recv_sem):
            pass

    full = pl.pallas_call(
        kernel,
        out_shape=jax.ShapeDtypeStruct((count,) + value.shape, value.dtype),
        in_specs=[pl.BlockSpec(memory_space=pl.ANY)],
        out_specs=pl.BlockSpec(memory_space=pl.ANY),
        scratch_shapes=[pltpu.SemaphoreType.DMA] + ring_sems(count),
        compiler_params=pltpu.CompilerParams(collective_id=ident, has_side_effects=True),
        cost_estimate=pl.CostEstimate(flops=0, bytes_accessed=100_000_000, transcendentals=0),
        name="gather_rows",
    )(value)
    return full.reshape(-1, value.shape[1])


def sum_rows(partial, ident):
    count = lax.axis_size("ctx")
    rows, width = partial.shape[0] // count, partial.shape[1]

    def kernel(parts, total, held, send_sem, recv_sem):
        ring = Ring(count)
        greet([ring.device(1), ring.device(-1)])
        ring_sum(ring, parts, held, total, send_sem, recv_sem)

    return pl.pallas_call(
        kernel,
        out_shape=jax.ShapeDtypeStruct((rows, width), F32),
        in_specs=[pl.BlockSpec(memory_space=pltpu.VMEM)],
        out_specs=pl.BlockSpec(memory_space=pltpu.VMEM),
        scratch_shapes=[pltpu.VMEM((2, count // 2, rows, width), BF16)] + ring_sems(count),
        compiler_params=pltpu.CompilerParams(
            collective_id=ident, has_side_effects=True, vmem_limit_bytes=32 * 2**20
        ),
        cost_estimate=pl.CostEstimate(flops=0, bytes_accessed=100_000_000, transcendentals=0),
        name="sum_rows",
    )(partial.astype(BF16).reshape(count, rows, width))


def gather_start(value, weight):
    count, shards = lax.axis_size("ctx"), lax.axis_size("fsdp")

    def kernel(own, shard, full, whole, local_sem, send_sem, recv_sem, far_send, far_recv):
        ring = Ring(count)
        me = ring.fsdp
        pair = me + 1 - 2 * (me % 2)
        others = [(me + 2 * hop) % shards for hop in range(1, shards // 2)]
        greet(
            [ring.device(1), ring.device(-1), (ring.ctx, pair)]
            + [(ring.ctx, other) for other in others]
        )
        keep = pltpu.make_async_copy(shard, whole.at[me], local_sem.at[1])
        keep.start()
        copies = [
            remote(shard, whole.at[me], far_send.at[i], far_recv.at[i], (ring.ctx, to))
            for i, to in enumerate([pair] + others)
        ]
        for copy in copies:
            copy.start()
        walk = ring_gather(ring, own, full, local_sem.at[0], send_sem, recv_sem)
        next(walk)
        passed = []
        for i in range(1, len(copies)):
            copies[i].wait_recv()
            origin = (me - 2 * i + shards) % shards
            at = shards // 2 - 1 + i
            copy = remote(whole.at[origin], whole.at[origin], far_send.at[at], far_recv.at[at], (ring.ctx, pair))
            copy.start()
            passed.append(copy)
        for _ in walk:
            pass
        copies[0].wait_recv()
        for copy in passed:
            copy.wait_recv()
        for copy in copies + passed:
            copy.wait_send()
        keep.wait()

    full, whole = pl.pallas_call(
        kernel,
        out_shape=(
            jax.ShapeDtypeStruct((count,) + value.shape, value.dtype),
            jax.ShapeDtypeStruct((shards,) + weight.shape, weight.dtype),
        ),
        in_specs=[pl.BlockSpec(memory_space=pl.ANY)] * 2,
        out_specs=(pl.BlockSpec(memory_space=pl.ANY),) * 2,
        scratch_shapes=[pltpu.SemaphoreType.DMA((2,))]
        + ring_sems(count)
        + [pltpu.SemaphoreType.DMA((shards - 1,)), pltpu.SemaphoreType.DMA((shards - 1,))],
        compiler_params=pltpu.CompilerParams(collective_id=0, has_side_effects=True),
        cost_estimate=pl.CostEstimate(flops=0, bytes_accessed=100_000_000, transcendentals=0),
        name="gather_start",
    )(value, weight)
    return full.reshape(-1, value.shape[1]), whole.reshape(-1, weight.shape[1])


def rows_to_columns(value):
    return lax.all_to_all(value, "ctx", split_axis=1, concat_axis=0, tiled=True)


def columns_to_rows(value):
    return lax.all_to_all(value, "ctx", split_axis=0, concat_axis=1, tiled=True)


def sum_grad(partial):
    return lax.psum_scatter(partial.astype(BF16), "fsdp", scatter_dimension=0, tiled=True)


def attention_scores(queries, keys, decay, allowed, scaling):
    scores = jnp.einsum("ihd,jhd->hij", queries, keys, preferred_element_type=F32) * scaling
    scores = scores + decay.T[:, :, None] - decay.T[:, None, :]
    return jnp.where(allowed[None], scores, NEGATIVE)


def shards(
    tokens,
    segments,
    gain_attn,
    w_query,
    w_key,
    w_value,
    w_forget,
    forget_bias,
    w_outgate,
    w_out,
    gain_ffn,
    w_gate,
    w_up,
    w_down,
    cotangent,
):
    n_ctx, me = lax.axis_size("ctx"), lax.axis_index("ctx")
    n_fsdp = lax.axis_size("fsdp")
    tok_rows, width = tokens.shape[1:]
    seq_rows = tok_rows * n_ctx
    n_heads = forget_bias.shape[0]
    head_dim = width // n_heads
    scaling = head_dim ** (-0.5)
    own_heads = -(-n_heads // n_ctx)
    own_width = own_heads * head_dim
    padded = own_width * n_ctx
    ffn_rows = w_down.shape[0]
    ffn_piece = ffn_rows // n_ctx
    ffn_width = ffn_piece * n_fsdp
    shard_rows = w_query.shape[0]

    def widen(value, size):
        return jnp.pad(value, ((0, 0), (0, size - value.shape[1])))

    def own_columns(weight, size):
        return lax.dynamic_slice_in_dim(widen(weight, size * n_ctx), me * size, size, 1)

    def own_ffn(weight):
        pieces = weight.reshape(weight.shape[0], n_fsdp, n_ctx, ffn_piece)
        return lax.dynamic_slice_in_dim(pieces, me, 1, 2).reshape(weight.shape[0], ffn_width)

    def gather_weight(weight):
        return lax.all_gather(weight, "fsdp", axis=0, tiled=True)

    mixed_shard = jnp.concatenate(
        [own_columns(w, own_width) for w in (w_query, w_key, w_value, w_outgate)]
        + [own_columns(w_forget, own_heads)],
        axis=1,
    )
    full_out = gather_weight(w_out)
    ffn_in = gather_weight(jnp.concatenate([own_ffn(w_gate), own_ffn(w_up)], axis=1))
    ffn_out = gather_weight(lax.dynamic_slice_in_dim(w_down, me * ffn_piece, ffn_piece, 0))
    bias_own = lax.dynamic_slice_in_dim(
        jnp.pad(forget_bias, (0, own_heads * n_ctx - n_heads)), me * own_heads, own_heads, 0
    )

    seg = segments[0]
    places = jnp.arange(seq_rows, dtype=jnp.int32)
    allowed = (places[None, :] <= places[:, None]) & (seg[None, :] == seg[:, None])

    inputs = tokens[0].astype(F32)
    gain_one = gain_attn.astype(F32)
    normed_one, rstat_one = rms_stats(inputs)
    normed, mixed_in = gather_start((normed_one * gain_one).astype(BF16), mixed_shard)
    grad_out_low = lax.all_gather(cotangent[0], "ctx", axis=0, tiled=True)

    mixed = matmul(normed, mixed_in)
    split = [own_width * i for i in range(5)]
    queries, keys, values = [
        mixed[:, split[i] : split[i + 1]].astype(BF16).reshape(seq_rows, own_heads, head_dim)
        for i in range(3)
    ]
    gate_value = jax.nn.sigmoid(mixed[:, split[3] : split[4]])
    forget_logits = mixed[:, split[4] :] + bias_own
    decay = jnp.cumsum(jax.nn.log_sigmoid(forget_logits), axis=0)

    scores = attention_scores(queries, keys, decay, allowed, scaling)
    row_max = jnp.max(scores, axis=-1, keepdims=True)
    raised = jnp.exp(scores - row_max)
    row_total = jnp.sum(raised, axis=-1, keepdims=True)
    probabilities = raised / row_total
    attended = jnp.einsum(
        "hij,jhd->ihd", probabilities.astype(BF16), values, preferred_element_type=F32
    ).reshape(seq_rows, own_width)
    gated = columns_to_rows((attended * gate_value).astype(BF16))[:, :width]

    middle = inputs + matmul(gated, full_out)
    gain_two = gain_ffn.astype(F32)
    normed_two_f, rstat_two = rms_stats(middle)
    normed_two = gather_rows((normed_two_f * gain_two).astype(BF16), 1)
    gated_all = lax.all_gather(gated, "ctx", axis=0, tiled=True)

    ffn_mid = matmul(normed_two, ffn_in)
    gate_part, up_part = ffn_mid[:, :ffn_width], ffn_mid[:, ffn_width:]
    sig_gate = jax.nn.sigmoid(gate_part)
    silu_gate = gate_part * sig_gate
    hidden = (silu_gate * up_part).astype(BF16)
    output = middle + lax.psum_scatter(
        matmul(hidden, ffn_out).astype(BF16), "ctx", scatter_dimension=0, tiled=True
    ).astype(F32)

    grad_hidden = matmul_rows(grad_out_low, ffn_out)
    grad_gate_low = (
        grad_hidden * up_part * (sig_gate * (1.0 + gate_part * (1.0 - sig_gate)))
    ).astype(BF16)
    grad_up_low = (grad_hidden * silu_gate).astype(BF16)
    grad_mid_low = jnp.concatenate([grad_gate_low, grad_up_low], axis=1)
    grad_normed_two = sum_rows(matmul_rows(grad_mid_low, ffn_in), 2)
    back_two, grad_gain_two = norm_back(grad_normed_two, normed_two_f, rstat_two, gain_two)
    grad_middle = cotangent[0].astype(F32) + back_two
    grad_ffn_in = sum_grad(weight_grad(normed_two, grad_mid_low))
    grad_ffn_out = sum_grad(weight_grad(hidden, grad_out_low))

    grad_branch_low = grad_middle.astype(BF16)
    grad_gated = matmul_rows(grad_branch_low, full_out).astype(BF16)
    grad_gated = rows_to_columns(widen(grad_gated, padded)).astype(F32)
    grad_branch_own = rows_to_columns(widen(grad_branch_low, padded))
    grad_attn_low = (grad_gated * gate_value).astype(BF16)
    grad_gatelog_low = (grad_gated * attended * (gate_value * (1.0 - gate_value))).astype(BF16)

    grad_heads = grad_attn_low.reshape(seq_rows, own_heads, head_dim)
    grad_values = jnp.einsum(
        "hij,ihd->jhd", probabilities.astype(BF16), grad_heads, preferred_element_type=F32
    )
    grad_probs = jnp.einsum("ihd,jhd->hij", grad_heads, values, preferred_element_type=F32)
    row_inner = jnp.sum(probabilities * grad_probs, axis=-1, keepdims=True)
    grad_scores = (probabilities * (grad_probs - row_inner)).astype(BF16)
    grad_queries = (
        jnp.einsum("hij,jhd->ihd", grad_scores, keys, preferred_element_type=F32) * scaling
    )
    grad_keys = (
        jnp.einsum("hij,ihd->jhd", grad_scores, queries, preferred_element_type=F32) * scaling
    )
    score_sums = grad_scores.astype(F32)
    decay_grad = jnp.sum(score_sums, axis=2).T - jnp.sum(score_sums, axis=1).T
    later = jnp.flip(jnp.cumsum(jnp.flip(decay_grad, 0), axis=0), 0)
    grad_logits_low = (later * jax.nn.sigmoid(-forget_logits)).astype(BF16)
    bias_part = jnp.zeros((own_heads * n_ctx,), F32)
    bias_part = lax.dynamic_update_slice_in_dim(
        bias_part, jnp.sum(grad_logits_low.astype(F32), axis=0), me * own_heads, 0
    )[:n_heads]

    grad_mixed_low = jnp.concatenate(
        [
            g.astype(BF16).reshape(seq_rows, own_width)
            for g in (grad_queries, grad_keys, grad_values, grad_gatelog_low)
        ]
        + [grad_logits_low],
        axis=1,
    )
    grad_normed = sum_rows(matmul_rows(grad_mixed_low, mixed_in), 3)
    back_one, grad_gain_one = norm_back(grad_normed, normed_one, rstat_one, gain_one)
    grad_inputs = grad_middle + back_one

    grad_mixed_in = sum_grad(weight_grad(normed, grad_mixed_low))
    grad_out_part = sum_grad(weight_grad(gated_all, grad_branch_own))

    def spread(value):
        return lax.all_gather(value, "ctx", axis=0)

    def columns_of(pieces, size):
        full = jnp.moveaxis(pieces, 0, 1).reshape(pieces.shape[1], -1)
        return full[:, :size].astype(F32)

    spread_ffn_in = spread(grad_ffn_in)
    spread_ffn_out = spread(grad_ffn_out)
    grad_attn_part = jnp.concatenate([grad_mixed_in, grad_out_part], axis=1)
    spread_attn = gather_rows(grad_attn_part, 4).reshape((n_ctx,) + grad_attn_part.shape)

    def ffn_columns(pieces):
        pieces = pieces.reshape(n_ctx, shard_rows, n_fsdp, ffn_piece)
        return jnp.transpose(pieces, (1, 2, 0, 3)).reshape(shard_rows, -1).astype(F32)

    grad_weights = [
        columns_of(spread_attn[:, :, split[i] : split[i + 1]], width) for i in range(4)
    ]
    grad_forget = columns_of(spread_attn[:, :, split[4] : split[4] + own_heads], n_heads)
    grad_out_full = columns_of(spread_attn[:, :, split[4] + own_heads :], width)
    small = lax.psum((grad_gain_one, grad_gain_two, bias_part), ("ctx", "fsdp"))
    return (
        output.astype(BF16)[None],
        grad_inputs[None],
        small[0],
        grad_weights[0],
        grad_weights[1],
        grad_weights[2],
        grad_forget,
        small[2],
        grad_weights[3],
        grad_out_full,
        small[1],
        ffn_columns(spread_ffn_in[:, :, :ffn_width]),
        ffn_columns(spread_ffn_in[:, :, ffn_width:]),
        spread_ffn_out.reshape(ffn_rows, width).astype(F32),
    )


def solution(mesh):
    rows, blocks = P("fsdp", None), P("fsdp", "ctx", None)
    return jax.shard_map(
        shards,
        mesh=mesh,
        in_specs=(blocks, rows, P())
        + (rows,) * 4
        + (P(), rows, rows, P(), rows, rows, rows, blocks),
        out_specs=(blocks, blocks, P())
        + (rows,) * 4
        + (P(), rows, rows, P(), rows, rows, rows),
        check_vma=False,
    )
```

time: 2980 us -> 754 us (0.25)
  waiting for transfers between devices: 2310 us -> 92.2 us
  Pallas kernels: 0 us -> 288 us
  matrix products: 216 us -> 104 us
  blocking collectives: 159 us -> 55.7 us
  local copies, waits for them, and re-layouts: 208 us -> 131 us
    reduce_scatter x12 -> x5, waiting for transfers between devices: 1170 us -> 0.04 us  [the longest x4 0.04 us: sum_grad(): lax.psum_scatter(partial.astype(BF16), 'fsdp', scatter_dimension=0, tiled...]
    psum x1 -> x0, waiting for transfers between devices: 825 us -> none  [shards(): lax.psum((ffn_parts[0], ffn_parts[1], ffn_parts[2], attn_parts[0], attn_p...]
    pallas_call x0 -> x5, Pallas kernels: none -> 288 us  [the longest x2 140 us: gather_rows(): pl.pallas_call(kernel, out_shape=jax.ShapeDtypeStruct((count,) + value.sh...]
    all_gather x10 -> x7, waiting for transfers between devices: 312 us -> 88.1 us  [the longest x2 88.1 us: spread(): return lax.all_gather(value, 'ctx', axis=0)]
    dynamic_slice x96 -> x6, local copies, waits for them, and re-layouts: 88.6 us -> 6.04 us  [the longest x3 3.19 us: own_columns(): lax.dynamic_slice_in_dim(widen(weight, size * n_ctx), me * size, size, 1)]
    convert_element_type x0 -> x15, local copies, waits for them, and re-layouts: none -> 67.9 us  [the longest x4 28.3 us: ffn_columns(): jnp.transpose(pieces, (1, 2, 0, 3)).reshape(shard_rows, -1).astype(F32)]
    dot_general x93 -> x9, matrix products: 98.7 us -> 51.7 us  [the longest x4 22.7 us: matmul(): return jnp.dot(left, right, preferred_element_type=F32)]
    dot_general x9 -> x4, matrix products: 63.8 us -> 21 us  [weight_grad(): lax.dot_general(left, right, (((0,), (0,)), ((), ())), preferred_element_...]
  transfers between devices with their start and end apart: 23 -> 14, of which waited for: 20 -> 2; matrix products, arithmetic and copies ran while one was open for 9% -> 30% of each run, Pallas kernels for 0% -> 39%
where the time goes in v1:
time: 754 us; the launch traced here: 747 us
  Pallas kernels  288 us (38%)
  local copies, waits for them, and re-layouts  131 us (17%)
  matrix products  104 us (14%)
  waiting for transfers between devices  92.2 us (12%)
  blocking collectives  55.7 us (7%)
  other arithmetic  50.5 us (7%)
  between operations  15 us (2%)
  starting transfers between devices  9.95 us (1%)
    pallas_call x2, Pallas kernels, gather_rows(): pl.pallas_call(kernel, out_shape=jax.ShapeDtypeStruct((count,) + value.sh...  140 us
    all_gather x2, waiting for transfers between devices, spread(): return lax.all_gather(value, 'ctx', axis=0)  88.1 us
    pallas_call x2, Pallas kernels, sum_rows(): pl.pallas_call(kernel, out_shape=jax.ShapeDtypeStruct((rows, width), F32)...  87.6 us
    pallas_call x1, Pallas kernels, gather_start(): pl.pallas_call(kernel, out_shape=(jax.ShapeDtypeStruct((count,) + value.s...  60.1 us
    unnamed x80, local copies, waits for them, and re-layouts  51.3 us
    psum x1, blocking collectives, shards(): small = lax.psum((grad_gain_one, grad_gain_two, bias_part), ('ctx', 'fsdp'))  41.5 us
    convert_element_type x4, local copies, waits for them, and re-layouts, ffn_columns(): jnp.transpose(pieces, (1, 2, 0, 3)).reshape(shard_rows, -1).astype(F32)  28.3 us
    dot_general x4, matrix products, matmul_rows(): lax.dot_general(left, right, (((1,), (1,)), ((), ())), preferred_element_...  24 us
  transfers between devices with their start and end apart: 14, of which 2 were waited for; matrix products, arithmetic and copies ran while one was open for 30% of the time, Pallas kernels for 39%

profile of v1, /device:TPU:0, one launch (start us, length us, event | category | flops | bytes accessed | tf_op | source)
XLA Modules:
  0.0 746.7 jit_solution(10936953590525985408)
XLA Ops:
  8.0 4.8 copy.95
  27.6 60.1 %gather_start.1 = (bf16[8,128,1536]{2,1,0:T(8,128)(2,1)}, bf16[4,384,771]{2,1,0:T(8,128)(2,1)}) custom-call(bf16[128,1536]{1,0:T(8,128)(2,1)} %fusion.36.own, bf16[384,771]{1,0:T(8,128)(2,1)} %concatenate.15.shard), custom_call_target="tpu_custom_call" | custom-call | bytes 100000000 | tf_op jit(solution)/shard_map/gather_start/pallas_call | solution.py:251
  87.8 5.5 fusion.62
  97.1 7.6 %fusion.63 = (f32[3,1024]{1,0:T(4,128)S(1)}, f32[3,1024,1024]{1,2,0:T(8,128)}) fusion(f32[3,1024]{1,0:T(4,128)S(1)} %bitcast.225, pred[1024,1024]{0,1:T(8,128)(4,1)S(1)} %fusion.7, bf16[1024,3,64]{0,2,1:T(8,128)(2,1)S(1)} %bitcast.207, bf16[1024,3,64]{0,2,1:T(8,128)(2,1)S(1)} %bitcast.209), kind=kOutput, calls=%fused_computation.137 | convolution fusion | flops 421528576 | bytes 14442496 | tf_op jit(solution)/shard_map/sub | solution.py:366
  104.8 6.1 fusion.14
  112.3 14.2 %all_to_all.51 = bf16[8,128,192]{1,2,0:T(8,128)(2,1)} all-to-all(bf16[8,128,192]{1,2,0:T(8,128)(2,1)S(1)} %copy_bitcast_fusion.2), channel_id=1, replica_groups=mesh['ctx'=8,'fsdp'=4] {'ctx'}, dimensions={0} | all-to-all | bytes 786432 | tf_op jit(solution)/shard_map/all_to_all | solution.py:274
  131.4 61.9 %gather_rows.2 = bf16[8,128,1536]{2,1,0:T(8,128)(2,1)} custom-call(bf16[128,1536]{1,0:T(8,128)(2,1)} %multiply_convert_fusion.2.own), custom_call_target="tpu_custom_call" | custom-call | bytes 100000000 | tf_op jit(solution)/shard_map/gather_rows/pallas_call | solution.py:176
  193.3 8.3 %fusion.64 = f32[1024,1024]{0,1:T(8,128)} fusion(bf16[1024,1536]{1,0:T(8,128)(2,1)} %bitcast.205, bf16[1536,1024]{0,1:T(8,128)(2,1)} %all-gather.13.cloned.1.call-done), kind=kOutput, calls=%fused_computation.138 | convolution fusion | flops 3221225472 | bytes 10485760 | tf_op jit(solution)/shard_map/dot_general | solution.py:14
  201.6 7.5 %fusion.20 = (bf16[1024,512]{0,1:T(8,128)(2,1)}, bf16[1024,512]{0,1:T(8,128)(2,1)}, bf16[1024,512]{0,1:T(8,128)(2,1)S(1)}) fusion(f32[1024,1024]{0,1:T(8,128)} %fusion.64, bf16[512,1536]{1,0:T(8,128)(2,1)} %all-gather.15.cloned.1.call-done, bf16[1,1024,1536]{2,1,0:T(8,128)(2,1)} %all-gather.19.cloned.1.call-done), kind=kOutput, calls=%fused_computation.46 | convolution fusion | flops 1618477056 | bytes 12058624 | tf_op jit(solution)/shard_map/dot_general | solution.py:18
  213.1 6.0 convolution_convert_fusion.3
  219.1 56.9 %sum_rows.2 = f32[128,1536]{1,0:T(8,128)S(1)} custom-call(bf16[8,128,1536]{2,1,0:T(8,128)(2,1)S(1)} %bitcast.188), custom_call_target="tpu_custom_call" | custom-call | bytes 100000000 | tf_op jit(solution)/shard_map/sum_rows/pallas_call | solution.py:198
  283.9 12.6 %copy.96 = bf16[128,1536]{0,1:T(8,128)(2,1)} copy(bf16[128,1536]{1,0:T(8,128)(2,1)} %convolution_convert_fusion.6) | data formatting | bytes 786432 | tf_op jit(solution)/shard_map/convert_element_type | solution.py:402
  301.1 7.6 %convolution_convert_fusion.2 = bf16[1536,1024]{1,0:T(8,128)(2,1)} fusion(bf16[1024,1536]{1,0:T(8,128)(2,1)} %bitcast.206, bf16[1024,512]{0,1:T(8,128)(2,1)} %get-tuple-element.80, bf16[1024,512]{0,1:T(8,128)(2,1)} %get-tuple-element.79), kind=kOutput, calls=%fused_computation.20 | convolution fusion | flops 3226992640 | bytes 8388608 | tf_op jit(solution)/shard_map/dot_general | solution.py:22
  317.2 7.4 multiply_reduce_fusion
  347.7 4.9 fusion.26
  353.4 6.6 fusion.27
  363.3 6.4 convolution_convert_fusion.4
  374.4 5.2 convolution_convert_fusion.1
  381.0 5.8 convolution_convert_fusion
  386.8 30.6 %sum_rows.3 = f32[128,1536]{1,0:T(8,128)S(1)} custom-call(bf16[8,128,1536]{2,1,0:T(8,128)(2,1)S(1)} %bitcast.187), custom_call_target="tpu_custom_call" | custom-call | bytes 100000000 | tf_op jit(solution)/shard_map/sum_rows/pallas_call | solution.py:198
  418.0 41.5 %all-reduce = (f32[1536]{0:T(1024)}, f32[24]{0:T(128)}, f32[1536]{0:T(1024)}) all-reduce(f32[1536]{0:T(1024)S(1)} %get-tuple-element.64, f32[24]{0:T(128)S(1)} %dynamic_update_slice.3, f32[1536]{0:T(1024)S(1)} %copy-done.12), channel_id=1, replica_groups=mesh['ctx'=8,'fsdp'=4] {'ctx','fsdp'}, use_global_device_ids=true, to_apply=%region_15.16 | all-reduce | flops 3096 | bytes 24768 | tf_op jit(solution)/shard_map/psum | solution.py:466
  461.8 78.4 %gather_rows.3 = bf16[8,384,963]{2,1,0:T(8,128)(2,1)} custom-call(bf16[384,963]{1,0:T(8,128)(2,1)} %pad_maximum_fusion.4.own), custom_call_target="tpu_custom_call" | custom-call | bytes 100000000 | tf_op jit(solution)/shard_map/gather_rows/pallas_call | solution.py:176
  540.2 11.4 %convert_bitcast_fusion = (f32[384,8,192]{2,0,1:T(8,128)}, f32[384,8,192]{2,0,1:T(8,128)}, f32[384,8,192]{2,0,1:T(8,128)}, f32[384,8,192]{2,0,1:T(8,128)}, f32[384,8,192]{2,0,1:T(8,128)}) fusion(bf16[8,384,963]{2,1,0:T(8,128)(2,1)} %gather_rows.3), kind=kLoop, calls=%fused_computation.29 | loop fusion | flops 2949120 | bytes 17694720 | tf_op jit(solution)/shard_map/convert_element_type | solution.py:450
  590.9 5.6 convert_element_type.291
  596.5 88.1 %all-gather.21.cloned.1.call-done = bf16[3072,1024]{1,0:T(8,128)(2,1)} async-done(((bf16[384,1024]{1,0:T(8,128)(2,1)}), bf16[3072,1024]{1,0:T(8,128)(2,1)}) %all-gather.21.cloned.1.call-update) | async-done | bytes 6291472 | tf_op jit(solution)/shard_map/all_gather | solution.py:446
  684.5 9.3 %slice_convert_fusion = (f32[8,384,512]{2,1,0:T(8,128)}, f32[8,384,512]{2,1,0:T(8,128)}) fusion(bf16[8,384,1024]{2,1,0:T(8,128)(2,1)} %bitcast.200), kind=kLoop, calls=%fused_computation.23 | loop fusion | flops 3145728 | bytes 18874368 | tf_op jit(solution)/shard_map/convert_element_type | solution.py:459
  693.9 7.7 %reshape.271 = f32[8,384,4,128]{3,2,1,0:T(4,128)} reshape(f32[8,384,512]{2,1,0:T(8,128)} %get-tuple-element.73) | data formatting | bytes 12582912 | tf_op jit(solution)/shard_map/convert_element_type | solution.py:459
  701.6 6.4 copy.111
  708.0 8.7 %copy.146 = f32[48,8,32,128]{3,1,2,0:T(8,128)} copy(f32[48,8,32,128]{3,2,1,0:T(8,128)S(1)} %bitcast.189) | data formatting | bytes 12582912
  716.7 7.8 %reshape.272 = f32[8,384,4,128]{3,2,1,0:T(4,128)} reshape(f32[8,384,512]{2,1,0:T(8,128)} %get-tuple-element.72) | data formatting | bytes 12582912 | tf_op jit(solution)/shard_map/convert_element_type | solution.py:459
  724.5 6.4 copy.112
  730.9 8.7 %copy.145 = f32[48,8,32,128]{3,1,2,0:T(8,128)} copy(f32[48,8,32,128]{3,2,1,0:T(8,128)S(1)} %bitcast.190) | data formatting | bytes 12582912
  (177 shorter events, 125.6 us)
Async XLA Ops:
  7.2 12.6 %copy-start = (bf16[1024,1536]{1,0:T(8,128)(2,1)S(1)}, bf16[1024,1536]{1,0:T(8,128)(2,1)}, u32[]{:S(2)}) copy-start(bf16[1024,1536]{1,0:T(8,128)(2,1)} %param.28) | copy-start | bytes 9437188
  7.2 119.7 %all-gather.11.cloned.1.call-start = ((), (), s32[]{:S(2)}) async-start(), calls=%async_computation.8 | async-start | bytes 5898240 | tf_op jit(solution)/shard_map/all_gather | solution.py:330
  7.9 185.4 %all-gather.13.cloned.1.call-start = ((), (), s32[]{:S(2)}) async-start(), calls=%async_computation.9 | async-start | bytes 3932160 | tf_op jit(solution)/shard_map/all_gather | solution.py:330
  19.7 181.9 %all-gather.15.cloned.1.call-start = ((), (), s32[]{:S(2)}) async-start(), calls=%async_computation.10 | async-start | bytes 1966080 | tf_op jit(solution)/shard_map/all_gather | solution.py:330
  20.6 181.0 %all-gather.19.cloned.1.call-start = ((), (), s32[]{:S(2)}) async-start(), calls=%async_computation.17 | async-start | bytes 3538944 | tf_op jit(solution)/shard_map/all_gather | solution.py:352
  21.2 315.4 %all-gather.17.cloned.1.call-start = ((), (), s32[]{:S(2)}) async-start(), calls=%async_computation.13 | async-start | bytes 3538944 | tf_op jit(solution)/shard_map/all_gather | solution.py:378
  21.4 71.9 %copy-start.19 = (f32[128]{0:T(128)}, f32[128]{0:T(128)S(1)}, u32[]{:S(2)}) copy-start(f32[128]{0:T(128)S(1)} %add_rsqrt_fusion.1) | copy-start | bytes 1540
  23.1 70.2 %copy-start.25 = (f32[3]{0:T(128)}, f32[3]{0:T(128)S(1)}, u32[]{:S(2)}) copy-start(f32[3]{0:T(128)S(1)} %dynamic_slice.32) | copy-start | bytes 40
  87.7 8.8 %copy-start.16 = (s32[1,1024]{1,0:T(1,128)S(1)}, s32[1,1024]{1,0:T(1,128)}, u32[]{:S(2)}) copy-start(s32[1,1024]{1,0:T(1,128)} %param.16) | copy-start | bytes 12292
  96.5 8.3 %copy-start.4 = (bf16[1024,192]{0,1:T(8,128)(2,1)}, bf16[1024,192]{0,1:T(8,128)(2,1)S(1)}, u32[]{:S(2)}) copy-start(bf16[1024,192]{0,1:T(8,128)(2,1)S(1)} %get-tuple-element.85) | copy-start | bytes 1179652
  96.5 8.3 %copy-start.6 = (bf16[1024,192]{0,1:T(8,128)(2,1)}, bf16[1024,192]{0,1:T(8,128)(2,1)S(1)}, u32[]{:S(2)}) copy-start(bf16[1024,192]{0,1:T(8,128)(2,1)S(1)} %get-tuple-element.84) | copy-start | bytes 1179652
  96.5 8.3 %copy-start.10 = (bf16[1024,192]{0,1:T(8,128)(2,1)}, bf16[1024,192]{0,1:T(8,128)(2,1)S(1)}, u32[]{:S(2)}) copy-start(bf16[1024,192]{0,1:T(8,128)(2,1)S(1)} %get-tuple-element.86) | copy-start | bytes 1179652
  110.8 16.0 %copy-start.22 = (bf16[1536]{0:T(1024)(128)(2,1)S(1)}, bf16[1536]{0:T(1024)(128)(2,1)}, u32[]{:S(2)}) copy-start(bf16[1536]{0:T(1024)(128)(2,1)} %param.25) | copy-start | bytes 9220
  126.5 253.2 %reduce-scatter.14.cloned.1.call-start = ((), (), s32[]{:S(2)}) async-start(), calls=%async_computation.16 | async-start | bytes 1966080 | tf_op jit(solution)/shard_map/reduce_scatter | solution.py:278
  130.5 145.5 %copy-start.17 = (f32[128]{0:T(128)}, f32[128]{0:T(128)S(1)}, u32[]{:S(2)}) copy-start(f32[128]{0:T(128)S(1)} %add_rsqrt_fusion) | copy-start | bytes 1540
  201.6 8.5 %copy-start.26 = (bf16[1,1024,1536]{2,1,0:T(8,128)(2,1)S(1)}, bf16[1,1024,1536]{2,1,0:T(8,128)(2,1)}, u32[]{:S(2)}) copy-start(bf16[1,1024,1536]{2,1,0:T(8,128)(2,1)} %all-gather.19.cloned.1.call-done) | copy-start | bytes 9437188
  219.1 58.3 %copy-start.3 = (bf16[1,128,1536]{2,1,0:T(8,128)(2,1)S(1)}, bf16[1,128,1536]{2,1,0:T(8,128)(2,1)}, u32[]{:S(2)}) copy-start(bf16[1,128,1536]{2,1,0:T(8,128)(2,1)} %param.29) | copy-start | bytes 1179652
  296.6 13.7 %all-to-all-start.1 = ((bf16[128,8,192]{0,2,1:T(8,128)(2,1)}), bf16[128,8,192]{0,2,1:T(8,128)(2,1)S(1)}, u32[]{:S(2)}, u32[]{:S(2)}) async-start(bf16[128,8,192]{0,2,1:T(8,128)(2,1)} %bitcast.23), calls=%async_computation.2 | async-start | bytes 786432 | tf_op jit(solution)/shard_map/all_to_all | solution.py:270
  301.1 79.4 %reduce-scatter.12.cloned.1.call-start = ((), (), s32[]{:S(2)}) async-start(), calls=%async_computation.15 | async-start | bytes 3932160 | tf_op jit(solution)/shard_map/reduce_scatter | solution.py:278
  310.3 26.3 %all-to-all-start.2 = ((bf16[128,8,192]{0,2,1:T(8,128)(2,1)}), bf16[128,8,192]{0,2,1:T(8,128)(2,1)}, u32[]{:S(2)}, u32[]{:S(2)}) async-start(bf16[128,8,192]{0,2,1:T(8,128)(2,1)} %bitcast.39), calls=%async_computation.4 | async-start | bytes 786432 | tf_op jit(solution)/shard_map/all_to_all | solution.py:270
  314.8 144.7 %reduce-scatter.10.cloned.1.call-start = ((), (), s32[]{:S(2)}) async-start(), calls=%async_computation.14 | async-start | bytes 983040 | tf_op jit(solution)/shard_map/reduce_scatter | solution.py:278
  317.2 8.8 %slice-start.1 = ((s8[12582912]{0:T(1024)(128)(4,1)}), s8[4194304]{0:T(1024)(128)(4,1)S(1)}, s32[]{:S(2)}) async-start(s8[12582912]{0:T(1024)(128)(4,1)} %bitcast.191), calls=%async_computation.21 | async-start | bytes 8388608
  317.2 10.1 %slice-start.2 = ((s8[12582912]{0:T(1024)(128)(4,1)}), s8[4194304]{0:T(1024)(128)(4,1)S(1)}, s32[]{:S(2)}) async-start(s8[12582912]{0:T(1024)(128)(4,1)} %bitcast.191), calls=%async_computation.22 | async-start | bytes 8388608
  317.2 10.1 %copy-start.14 = (f32[3,1024]{1,0:T(4,128)S(1)}, f32[3,1024]{1,0:T(4,128)}, u32[]{:S(2)}) copy-start(f32[3,1024]{1,0:T(4,128)} %copy-done.13) | copy-start | bytes 36868
  353.4 7.5 %copy-start.8 = (bf16[1024,192]{0,1:T(8,128)(2,1)S(1)}, bf16[1024,192]{0,1:T(8,128)(2,1)}, u32[]{:S(2)}) copy-start(bf16[1024,192]{0,1:T(8,128)(2,1)} %get-tuple-element.82) | copy-start | bytes 1179652
  360.1 99.4 %reduce-scatter.8.cloned.1.call-start = ((), (), s32[]{:S(2)}) async-start(), calls=%async_computation.12 | async-start | bytes 3440640 | tf_op jit(solution)/shard_map/reduce_scatter | solution.py:278
  374.2 214.4 %reduce-scatter.6.cloned.1.call-start = ((), (), s32[]{:S(2)}) async-start(), calls=%async_computation.11 | async-start | bytes 3538944 | tf_op jit(solution)/shard_map/reduce_scatter | solution.py:385
  379.7 211.2 %all-gather.23.cloned.1.call-start = ((), (), s32[]{:S(2)}) async-start(), calls=%async_computation.19 | async-start | bytes 3538944 | tf_op jit(solution)/shard_map/all_gather | solution.py:446
  380.4 304.1 %all-gather.21.cloned.1.call-start = ((), (), s32[]{:S(2)}) async-start(), calls=%async_computation.18 | async-start | bytes 7077888 | tf_op jit(solution)/shard_map/all_gather | solution.py:446
  386.8 30.9 %copy-start.20 = (f32[128]{0:T(128)S(1)}, f32[128]{0:T(128)}, u32[]{:S(2)}) copy-start(f32[128]{0:T(128)} %copy-done.19) | copy-start | bytes 1540
  386.8 31.2 %copy-start.12 = (f32[1536]{0:T(1024)S(1)}, f32[1536]{0:T(1024)}, u32[]{:S(2)}) copy-start(f32[1536]{0:T(1024)} %get-tuple-element.62) | copy-start | bytes 18436
  730.9 8.7 %copy-start.1 = (bf16[1024,1536]{1,0:T(8,128)(2,1)S(1)}, bf16[1024,1536]{1,0:T(8,128)(2,1)}, u32[]{:S(2)}) copy-start(bf16[1024,1536]{1,0:T(8,128)(2,1)} %param.28) | copy-start | bytes 9437188
  (13 other events, 52.9 us)
Sparse Core Ops, SparseCore 0:
  9.6 55.5 all-gather.10
  67.3 28.5 all-gather.12
  98.0 19.6 all-gather.14
  119.8 78.8 all-gather.18
  200.6 81.8 all-gather.16
  285.5 26.4 reduce-scatter.13
  315.3 38.0 reduce-scatter.11
  360.2 24.5 reduce-scatter.9
  388.1 35.4 reduce-scatter.7
  427.6 92.3 reduce-scatter.5
  522.2 62.5 all-gather.22
  586.9 97.6 all-gather.20

commit v2 on v1

v2 whole, which is shorter than its diff:
```python
import jax
import jax.numpy as jnp
from jax import lax
from jax.experimental import pallas as pl
from jax.experimental.pallas import tpu as pltpu
from jax.sharding import PartitionSpec as P

EPSILON = 1e-06
NEGATIVE = -1e30
BF16, F32 = jnp.bfloat16, jnp.float32


def matmul(left, right):
    return jnp.dot(left, right, preferred_element_type=F32)


def matmul_rows(left, right):
    return lax.dot_general(left, right, (((1,), (1,)), ((), ())), preferred_element_type=F32)


def weight_grad(left, right):
    return lax.dot_general(left, right, (((0,), (0,)), ((), ())), preferred_element_type=F32)


def rms_stats(values):
    rstat = lax.rsqrt(jnp.mean(values * values, axis=-1, keepdims=True) + EPSILON)
    return (values * rstat, rstat)


def norm_back(grad_in, normed, rstat, gain):
    grad_normed = grad_in * gain
    grad_gain = jnp.sum(grad_in * normed, axis=0)
    grad_values = rstat * (
        grad_normed - normed * jnp.mean(grad_normed * normed, axis=-1, keepdims=True)
    )
    return (grad_values, grad_gain)


MESH = pl.DeviceIdType.MESH
RING_PIECES = 4


def ring_place(ctx, count):
    odd = ctx % 2
    return ctx // 2 + odd * (count - 1 - 2 * (ctx // 2))


def ring_index(place, count):
    back = place // (count // 2)
    return 2 * place + back * (2 * (count - 1 - place) + 1 - 2 * place)


class Ring:
    def __init__(self, count):
        self.count, self.half = count, count // 2
        self.ctx, self.fsdp = lax.axis_index("ctx"), lax.axis_index("fsdp")
        self.place = ring_place(self.ctx, count)

    def at(self, offset):
        return ring_index((self.place + offset + self.count) % self.count, self.count)

    def device(self, offset):
        return (self.at(offset), self.fsdp)


def greet(devices):
    barrier = pltpu.get_barrier_semaphore()
    for device in devices:
        pl.semaphore_signal(barrier, inc=1, device_id=device, device_id_type=MESH)
    pl.semaphore_wait(barrier, len(devices))


def remote(src, dst, send, recv, device):
    return pltpu.make_async_remote_copy(
        src_ref=src, dst_ref=dst, send_sem=send, recv_sem=recv, device_id=device, device_id_type=MESH
    )


def carried(step, half, pieces, way):
    if step < half - 1:
        return range(pieces)
    return range(pieces // 2) if way == 0 else range(pieces // 2, pieces)


def ring_gather(ring, own, full, local_sem, send_sem, recv_sem, absolute=False, pieces=RING_PIECES):
    rows = own.shape[0] // pieces

    def part(k):
        return pl.ds(k * rows, rows)

    def slot(step, sign, holder=0):
        if absolute:
            return ring.at(-sign * step)
        return (sign * (step + holder)) % ring.count

    keep = pltpu.make_async_copy(own, full.at[slot(0, 1)], local_sem)
    keep.start()
    copies = {}
    for step in range(ring.half):
        for k in range(pieces):
            for way, sign in ((0, 1), (1, -1)):
                if k not in carried(step, ring.half, pieces, way):
                    continue
                if step > 0:
                    copies[step - 1, k, way].wait_recv()
                src = own.at[part(k)] if step == 0 else full.at[slot(step, sign), part(k)]
                copy = remote(
                    src,
                    full.at[slot(step, sign, 1), part(k)],
                    send_sem.at[step, k, way],
                    recv_sem.at[step, k, way],
                    ring.device(sign),
                )
                copy.start()
                copies[step, k, way] = copy
            yield
    for (step, k, way), copy in copies.items():
        if step == ring.half - 1 or k not in carried(step + 1, ring.half, pieces, way):
            copy.wait_recv()
    for copy in copies.values():
        copy.wait_send()
    keep.wait()


def ring_sum(ring, parts, held, total, send_sem, recv_sem, absolute, pieces=RING_PIECES):
    rows = parts.shape[1] // pieces

    def place(offset):
        return ring.at(offset) if absolute else -offset % ring.count

    def part(k):
        return pl.ds(k * rows, rows)

    copies = {}
    for step in range(ring.half):
        for k in range(pieces):
            for way, sign in ((0, 1), (1, -1)):
                if k not in carried(ring.half - 1 - step, ring.half, pieces, way):
                    continue
                block = place(sign * (ring.half - step))
                src = parts.at[block, part(k)]
                if (step - 1, k, way) in copies:
                    copies[step - 1, k, way].wait_recv()
                    slot = held.at[way, step - 1, part(k)]
                    slot[...] = (slot[...].astype(F32) + src[...].astype(F32)).astype(BF16)
                    src = slot
                copy = remote(
                    src,
                    held.at[way, step, part(k)],
                    send_sem.at[step, k, way],
                    recv_sem.at[step, k, way],
                    ring.device(sign),
                )
                copy.start()
                copies[step, k, way] = copy
            yield
    last = ring.half - 1
    for k in range(pieces):
        for way in range(2):
            copies[last, k, way].wait_recv()
        total[part(k)] = (
            parts[place(0), part(k)].astype(F32)
            + held[0, last, part(k)].astype(F32)
            + held[1, last, part(k)].astype(F32)
        )
    for copy in copies.values():
        copy.wait_send()


def ring_sems(count, pieces=RING_PIECES):
    shape = (count // 2, pieces, 2)
    return [pltpu.SemaphoreType.DMA(shape), pltpu.SemaphoreType.DMA(shape)]


def sems(*counts):
    return [pltpu.SemaphoreType.DMA((max(count, 1),)) for count in counts]


ANYWHERE, VMEM = pl.BlockSpec(memory_space=pl.ANY), pl.BlockSpec(memory_space=pltpu.VMEM)


class RingGather:
    def __init__(self, value, absolute=False):
        self.absolute = absolute
        count = lax.axis_size("ctx")
        self.ins, self.in_specs = [value], [ANYWHERE]
        self.outs, self.out_specs = (
            [jax.ShapeDtypeStruct((count,) + value.shape, value.dtype)],
            [ANYWHERE],
        )
        self.scratch = [pltpu.SemaphoreType.DMA] + ring_sems(count)

    def peers(self, ring):
        return [ring.device(1), ring.device(-1)]

    def run(self, ring, ins, outs, scratch):
        return ring_gather(ring, ins[0], outs[0], *scratch, absolute=self.absolute)


class RingSum:
    def __init__(self, partial, absolute=False):
        self.absolute = absolute
        count = lax.axis_size("ctx")
        rows, width = partial.shape[0] // count, partial.shape[1]
        self.ins, self.in_specs = [partial.astype(BF16).reshape(count, rows, width)], [VMEM]
        self.outs, self.out_specs = [jax.ShapeDtypeStruct((rows, width), F32)], [VMEM]
        self.scratch = [pltpu.VMEM((2, count // 2, rows, width), BF16)] + ring_sems(count)

    def peers(self, ring):
        return [ring.device(1), ring.device(-1)]

    def run(self, ring, ins, outs, scratch):
        return ring_sum(ring, ins[0], scratch[0], outs[0], *scratch[1:], self.absolute)


def shard_pair(ring, shards):
    me = ring.fsdp
    pair = me + 1 - 2 * (me % 2)
    return pair, [(me + 2 * hop) % shards for hop in range(1, shards // 2)]


def idle(turns):
    for _ in range(turns):
        yield


class ShardGather:
    def __init__(self, sources, piece=None):
        shards = lax.axis_size("fsdp")
        starts = None if piece is None else range(shards)
        self.starts, self.piece = starts, piece
        rows = sources[0].shape[0]
        width = sources[0].shape[1] if starts is None else len(sources) * len(starts) * piece
        self.ins, self.in_specs = list(sources), [ANYWHERE] * len(sources)
        self.outs = [jax.ShapeDtypeStruct((shards, rows, width), BF16)]
        self.out_specs = [ANYWHERE]
        parts = 1 if starts is None else len(sources) * len(starts)
        self.scratch = sems(parts, shards - 1, shards - 1)

    def peers(self, ring):
        pair, others = shard_pair(ring, lax.axis_size("fsdp"))
        return [(ring.ctx, to) for to in [pair] + others]

    def run(self, ring, ins, outs, scratch):
        whole, (local_sem, send_sem, recv_sem) = outs[0], scratch
        shards, me = lax.axis_size("fsdp"), ring.fsdp
        pair, others = shard_pair(ring, shards)
        local = []
        if self.starts is None:
            local.append(pltpu.make_async_copy(ins[0], whole.at[me], local_sem.at[0]))
        else:
            for i, source in enumerate(ins):
                for j, start in enumerate(self.starts):
                    at = i * len(self.starts) + j
                    start = (start * ring.count + ring.ctx) * self.piece
                    start = pl.multiple_of(start, self.piece)
                    local.append(
                        pltpu.make_async_copy(
                            source.at[:, pl.ds(start, self.piece)],
                            whole.at[me, :, pl.ds(at * self.piece, self.piece)],
                            local_sem.at[at],
                        )
                    )
        for copy in local:
            copy.start()
        yield
        if self.starts is None:
            block = ins[0]
        else:
            for copy in local:
                copy.wait()
            block = whole.at[me]
        copies = [
            remote(block, whole.at[me], send_sem.at[i], recv_sem.at[i], (ring.ctx, to))
            for i, to in enumerate([pair] + others)
        ]
        for copy in copies:
            copy.start()
        yield from idle(3 * RING_PIECES)
        passed = []
        for i in range(1, len(copies)):
            copies[i].wait_recv()
            origin = (me - 2 * i + shards) % shards
            at = shards // 2 - 1 + i
            copy = remote(
                whole.at[origin], whole.at[origin], send_sem.at[at], recv_sem.at[at], (ring.ctx, pair)
            )
            copy.start()
            passed.append(copy)
        yield from idle(2)
        copies[0].wait_recv()
        for copy in passed:
            copy.wait_recv()
        for copy in copies + passed:
            copy.wait_send()
        if self.starts is None:
            local[0].wait()


class ShardSum:
    def __init__(self, partial):
        shards = lax.axis_size("fsdp")
        rows, width = partial.shape[0] // shards, partial.shape[1]
        self.ins, self.in_specs = [partial.astype(BF16).reshape(shards, rows, width)], [VMEM]
        self.outs, self.out_specs = [jax.ShapeDtypeStruct((rows, width), BF16)], [VMEM]
        half = shards // 2
        self.scratch = [
            pltpu.VMEM((half, rows, width), BF16),
            pltpu.VMEM((max(half - 1, 1), rows, width), BF16),
        ] + sems(half, half, half - 1, half - 1)

    def peers(self, ring):
        pair, others = shard_pair(ring, lax.axis_size("fsdp"))
        return [(ring.ctx, to) for to in [pair] + others]

    def run(self, ring, ins, outs, scratch):
        parts, (near, far, near_send, near_recv, far_send, far_recv) = ins[0], scratch
        shards, me = lax.axis_size("fsdp"), ring.fsdp
        half, core, chip = shards // 2, me % 2, me // 2
        pair, others = shard_pair(ring, shards)
        first = [
            remote(
                parts.at[2 * i + 1 - core],
                near.at[i],
                near_send.at[i],
                near_recv.at[i],
                (ring.ctx, pair),
            )
            for i in range(half)
        ]
        for copy in first:
            copy.start()
        yield from idle(2)
        for copy in first:
            copy.wait_recv()
        second = []
        for hop in range(1, half):
            to = (chip + hop) % half
            near[to] = (near[to].astype(F32) + parts[2 * to + core].astype(F32)).astype(BF16)
            copy = remote(
                near.at[to],
                far.at[hop - 1],
                far_send.at[hop - 1],
                far_recv.at[hop - 1],
                (ring.ctx, others[hop - 1]),
            )
            copy.start()
            second.append(copy)
        yield from idle(3 * RING_PIECES)
        total = parts[me].astype(F32) + near[chip].astype(F32)
        for hop, copy in enumerate(second):
            copy.wait_recv()
            total = total + far[hop].astype(F32)
        outs[0][...] = total.astype(BF16)
        for copy in first + second:
            copy.wait_send()


class SmallSum:
    def __init__(self, small):
        count, shards = lax.axis_size("ctx"), lax.axis_size("fsdp")
        self.ins, self.in_specs = [small], [VMEM]
        self.outs, self.out_specs = [jax.ShapeDtypeStruct(small.shape, F32)], [VMEM]
        self.scratch = [
            pltpu.VMEM((shards,) + small.shape, F32),
            pltpu.VMEM((count,) + small.shape, F32),
        ] + sems(shards - 1, shards - 1, count - 1, count - 1)

    def devices(self, ring):
        count, shards = lax.axis_size("ctx"), lax.axis_size("fsdp")
        siblings = [(ring.ctx, (ring.fsdp + hop) % shards) for hop in range(1, shards)]
        return siblings, [((ring.ctx + hop) % count, ring.fsdp) for hop in range(1, count)]

    def peers(self, ring):
        return sum(self.devices(ring), [])

    def run(self, ring, ins, outs, scratch):
        near, far, near_send, near_recv, far_send, far_recv = scratch
        siblings, peers = self.devices(ring)
        me, row = ring.fsdp, ring.ctx
        near[me] = ins[0][...]
        first = [
            remote(ins[0], near.at[me], near_send.at[i], near_recv.at[i], to)
            for i, to in enumerate(siblings)
        ]
        for copy in first:
            copy.start()
        yield
        for copy in first:
            copy.wait()
        far[row] = sum([near[i] for i in range(len(siblings) + 1)])
        second = [
            remote(far.at[row], far.at[row], far_send.at[i], far_recv.at[i], to)
            for i, to in enumerate(peers)
        ]
        for copy in second:
            copy.start()
        yield
        yield
        for copy in second:
            copy.wait()
        outs[0][...] = sum([far[i] for i in range(len(peers) + 1)])


class Attention:
    def __init__(self, qkv, decay, seg, own_heads):
        self.rows, self.heads = qkv.shape[0], own_heads
        self.dim = qkv.shape[1] // 3 // own_heads
        self.scaling = self.dim ** (-0.5)
        self.tall = min(256, self.rows)
        self.ins = [qkv, decay, decay.T, seg[:, None], seg[None, :]]

    def block(self, index):
        rows = slice(index * self.tall, (index + 1) * self.tall)
        return rows, (index + 1) * self.tall

    def allowed(self, rows, wide, seg_rows, seg_cols):
        shape = (self.tall, wide)
        here = lax.broadcasted_iota(jnp.int32, shape, 0) + rows.start
        there = lax.broadcasted_iota(jnp.int32, shape, 1)
        return (there <= here) & (seg_rows[rows] == seg_cols[:, :wide])

    def part(self, qkv, which, head, rows):
        start = (which * self.heads + head) * self.dim
        return qkv[rows, start : start + self.dim]

    def scores(self, refs, head, rows, wide, allowed):
        qkv, decay, decay_cols = refs[:3]
        queries = self.part(qkv, 0, head, rows)
        keys = self.part(qkv, 1, head, slice(0, wide))
        scores = matmul_rows(queries, keys) * self.scaling
        scores = scores + decay[rows, head : head + 1] - decay_cols[head : head + 1, :wide]
        return queries, keys, jnp.where(allowed, scores, NEGATIVE)

    def peers(self, ring):
        return []


class AttentionForward(Attention):
    def __init__(self, qkv, decay, seg, own_heads):
        super().__init__(qkv, decay, seg, own_heads)
        self.in_specs = [VMEM] * 5
        self.outs = [
            jax.ShapeDtypeStruct((self.rows, own_heads * self.dim), F32),
            jax.ShapeDtypeStruct((self.rows, own_heads), F32),
        ]
        self.out_specs, self.scratch = [VMEM] * 2, []

    def run(self, ring, ins, outs, scratch):
        for index in range(self.rows // self.tall):
            rows, wide = self.block(index)
            allowed = self.allowed(rows, wide, *ins[3:])
            mixed, totals = [], []
            for head in range(self.heads):
                _, _, scores = self.scores(ins, head, rows, wide, allowed)
                row_max = jnp.max(scores, axis=1, keepdims=True)
                raised = jnp.exp(scores - row_max)
                row_total = jnp.sum(raised, axis=1, keepdims=True)
                probabilities = (raised * (1.0 / row_total)).astype(BF16)
                mixed.append(matmul(probabilities, self.part(ins[0], 2, head, slice(0, wide))))
                totals.append(row_max + jnp.log(row_total))
                if head < self.heads - 1:
                    yield
            outs[0][rows] = jnp.concatenate(mixed, axis=1)
            outs[1][rows] = jnp.concatenate(totals, axis=1)
            yield


class AttentionBackward(Attention):
    def __init__(self, qkv, decay, seg, own_heads, log_totals, grad_attn):
        super().__init__(qkv, decay, seg, own_heads)
        self.ins = self.ins + [log_totals, grad_attn]
        self.in_specs = [VMEM] * 7
        self.outs = [
            jax.ShapeDtypeStruct(qkv.shape, BF16),
            jax.ShapeDtypeStruct((self.rows, own_heads), F32),
            jax.ShapeDtypeStruct((own_heads, self.rows), F32),
        ]
        self.out_specs = [VMEM] * 3
        self.scratch = [pltpu.VMEM((3, own_heads, self.rows, self.dim), F32)]

    def run(self, ring, ins, outs, scratch):
        log_totals, grad_attn = ins[5:]
        grads, (sums,) = scratch, outs[2:]
        grad_q, grad_k, grad_v = [grads[0].at[i] for i in range(3)]
        blocks = self.rows // self.tall
        for index in reversed(range(blocks)):
            rows, wide = self.block(index)
            allowed = self.allowed(rows, wide, *ins[3:5])
            own = slice(0, wide)
            row_sums = []
            for head in range(self.heads):
                queries, keys, scores = self.scores(ins, head, rows, wide, allowed)
                probabilities = jnp.exp(scores - log_totals[rows, head : head + 1])
                grad_part = grad_attn[rows, head * self.dim : (head + 1) * self.dim]
                grad_probs = matmul_rows(grad_part, self.part(ins[0], 2, head, own))
                row_inner = jnp.sum(probabilities * grad_probs, axis=1, keepdims=True)
                grad_scores = (probabilities * (grad_probs - row_inner)).astype(BF16)
                grad_q[head, rows] = matmul(grad_scores, keys) * self.scaling
                from_k = weight_grad(grad_scores, queries) * self.scaling
                from_v = weight_grad(probabilities.astype(BF16), grad_part)
                wide_sums = grad_scores.astype(F32)
                row_sums.append(jnp.sum(wide_sums, axis=1, keepdims=True))
                column_sums = jnp.sum(wide_sums, axis=0, keepdims=True)
                if index == blocks - 1:
                    grad_k[head], grad_v[head] = from_k, from_v
                    sums[head : head + 1] = column_sums
                else:
                    grad_k[head, own] += from_k
                    grad_v[head, own] += from_v
                    sums[head : head + 1, own] += column_sums
                if head < self.heads - 1:
                    yield
            outs[1][rows] = jnp.concatenate(row_sums, axis=1)
            yield
        for index in range(blocks):
            rows, _ = self.block(index)
            outs[0][rows] = jnp.concatenate(
                [g[head, rows] for g in (grad_q, grad_k, grad_v) for head in range(self.heads)],
                axis=1,
            ).astype(BF16)


def running_sum(values, backward=False):
    tall = 128 if values.shape[0] % 128 == 0 else values.shape[0]
    blocks = values.reshape(-1, tall, values.shape[1])
    ones = jnp.ones((tall, tall), F32)
    wedge = jnp.triu(ones) if backward else jnp.tril(ones)
    inside = jnp.einsum("st,btk->bsk", wedge, blocks, precision=lax.Precision.HIGHEST)
    totals = jnp.sum(blocks, axis=1)
    count = totals.shape[0]
    before = jnp.tril(jnp.ones((count, count), F32), -1)
    before = before.T if backward else before
    return (inside + jnp.sum(before[:, :, None] * totals[None], axis=1)[:, None]).reshape(values.shape)


def exchange(ident, name, *tasks):
    count = lax.axis_size("ctx")

    def take(refs, sizes):
        groups, at = [], 0
        for size in sizes:
            groups.append(refs[at : at + size])
            at += size
        return groups

    ins = [len(task.ins) for task in tasks]
    outs = [len(task.outs) for task in tasks]
    scratch = [len(task.scratch) for task in tasks]

    def kernel(*refs):
        ring = Ring(count)
        greeted = []
        for kind in {type(task).__name__: task for task in tasks}.values():
            greeted.append(kind)
        near, along, small = [], [], []
        for task in greeted:
            if isinstance(task, SmallSum):
                small = task.peers(ring)
            elif isinstance(task, (RingGather, RingSum)):
                near = task.peers(ring)
            elif isinstance(task, (ShardGather, ShardSum)):
                along = task.peers(ring)
        greet(small if small else near + along)
        groups = [
            take(refs[: sum(ins)], ins),
            take(refs[sum(ins) : sum(ins) + sum(outs)], outs),
            take(refs[sum(ins) + sum(outs) :], scratch),
        ]
        walks = [task.run(ring, *parts) for task, *parts in zip(tasks, *groups)]
        while walks:
            walks = [walk for walk in walks if next(walk, walks) is None]

    results = pl.pallas_call(
        kernel,
        out_shape=sum([task.outs for task in tasks], []),
        in_specs=sum([task.in_specs for task in tasks], []),
        out_specs=sum([task.out_specs for task in tasks], []),
        scratch_shapes=sum([task.scratch for task in tasks], []),
        compiler_params=pltpu.CompilerParams(
            collective_id=ident, has_side_effects=True, vmem_limit_bytes=48 * 2**20
        ),
        cost_estimate=pl.CostEstimate(flops=0, bytes_accessed=100_000_000, transcendentals=0),
        name=name,
    )(*sum([task.ins for task in tasks], []))
    return take(list(results), outs)


def flat(blocks):
    return blocks.reshape(-1, blocks.shape[-1])


def ffn_columns(blocks, n_fsdp):
    count, rows, both = blocks.shape
    width, piece = both // 2, both // 2 // n_fsdp
    steps = 4
    tall = rows // steps

    def kernel(block_ref, *outs):
        for j in range(count):
            for half in range(2):
                for group in range(n_fsdp):
                    start, to = half * width + group * piece, (group * count + j) * piece
                    outs[half][:, to : to + piece] = block_ref[j, :, start : start + piece].astype(F32)

    wide = jax.ShapeDtypeStruct((rows, width * count), F32)
    spec = pl.BlockSpec((tall, width * count), lambda i: (i, 0))
    return pl.pallas_call(
        kernel,
        out_shape=(wide, wide),
        grid=(steps,),
        in_specs=[pl.BlockSpec((count, tall, both), lambda i: (0, i, 0))],
        out_specs=(spec, spec),
        compiler_params=pltpu.CompilerParams(vmem_limit_bytes=40 * 2**20),
        cost_estimate=pl.CostEstimate(
            flops=0, bytes_accessed=rows * both * count * 6, transcendentals=0
        ),
        name="ffn_columns",
    )(blocks)


def head_columns(blocks, sizes, widths):
    count, rows, total = blocks.shape
    steps = 4
    tall = rows // steps
    starts = [sum(sizes[:i]) for i in range(len(sizes))]

    def kernel(block_ref, *outs):
        for start, size, out in zip(starts, sizes, outs):
            for i in range(0, count, 2):
                pair = jnp.concatenate(
                    [block_ref[i + k][:, start : start + size].astype(F32) for k in range(2)], axis=1
                )
                at = i * size
                keep = min(2 * size, out.shape[1] - at)
                if keep > 0:
                    out[:, at : at + keep] = pair[:, :keep]

    return pl.pallas_call(
        kernel,
        out_shape=tuple(jax.ShapeDtypeStruct((rows, w), F32) for w in widths),
        grid=(steps,),
        in_specs=[pl.BlockSpec((count, tall, total), lambda i: (0, i, 0))],
        out_specs=tuple(pl.BlockSpec((tall, w), lambda i: (i, 0)) for w in widths),
        compiler_params=pltpu.CompilerParams(vmem_limit_bytes=40 * 2**20),
        cost_estimate=pl.CostEstimate(
            flops=0, bytes_accessed=count * rows * total * 6, transcendentals=0
        ),
        name="head_columns",
    )(blocks)


def rows_to_columns(value):
    return lax.all_to_all(value, "ctx", split_axis=1, concat_axis=0, tiled=True)


def columns_to_rows(value):
    return lax.all_to_all(value, "ctx", split_axis=0, concat_axis=1, tiled=True)


def shards(
    tokens,
    segments,
    gain_attn,
    w_query,
    w_key,
    w_value,
    w_forget,
    forget_bias,
    w_outgate,
    w_out,
    gain_ffn,
    w_gate,
    w_up,
    w_down,
    cotangent,
):
    n_ctx, me = lax.axis_size("ctx"), lax.axis_index("ctx")
    n_fsdp = lax.axis_size("fsdp")
    tok_rows, width = tokens.shape[1:]
    seq_rows = tok_rows * n_ctx
    n_heads = forget_bias.shape[0]
    head_dim = width // n_heads
    own_heads = -(-n_heads // n_ctx)
    own_width = own_heads * head_dim
    padded = own_width * n_ctx
    ffn_rows = w_down.shape[0]
    ffn_piece = ffn_rows // n_ctx
    ffn_width = ffn_piece * n_fsdp
    shard_rows = w_query.shape[0]

    def widen(value, size):
        return jnp.pad(value, ((0, 0), (0, size - value.shape[1])))

    def own_columns(weight, size):
        return lax.dynamic_slice_in_dim(widen(weight, size * n_ctx), me * size, size, 1)

    def own_ffn(weight):
        return [
            lax.dynamic_slice_in_dim(weight, (group * n_ctx + me) * ffn_piece, ffn_piece, 1)
            for group in range(n_fsdp)
        ]

    mixed_shard = jnp.concatenate(
        [own_columns(w, own_width) for w in (w_query, w_key, w_value, w_outgate)]
        + [own_columns(w_forget, own_heads)],
        axis=1,
    )
    bias_own = lax.dynamic_slice_in_dim(
        jnp.pad(forget_bias, (0, own_heads * n_ctx - n_heads)), me * own_heads, own_heads, 0
    )

    seg = segments[0]
    inputs = tokens[0].astype(F32)
    gain_one = gain_attn.astype(F32)
    normed_one, rstat_one = rms_stats(inputs)
    (normed,), (mixed_in,) = exchange(
        0,
        "gather_start",
        RingGather((normed_one * gain_one).astype(BF16), absolute=True),
        ShardGather([mixed_shard]),
    )
    normed, mixed_in = flat(normed), flat(mixed_in)
    normed, out_shard = lax.optimization_barrier((normed, w_out))
    full_out = lax.all_gather(out_shard, "fsdp", axis=0, tiled=True)

    split = [own_width * i for i in range(5)]
    qkv = matmul(normed, mixed_in[:, : split[3]]).astype(BF16)
    mixed = matmul(normed, mixed_in[:, split[3] :])
    gate_value = jax.nn.sigmoid(mixed[:, :own_width])
    forget_logits = mixed[:, own_width:] + bias_own
    decay = running_sum(jax.nn.log_sigmoid(forget_logits))

    (grad_out_low,), (attended, log_totals) = exchange(
        5,
        "attend",
        RingGather(cotangent[0], absolute=True),
        AttentionForward(qkv, decay, seg, own_heads),
    )
    grad_out_low = flat(grad_out_low)
    gated = columns_to_rows((attended * gate_value).astype(BF16))[:, :width]

    middle = inputs + matmul(gated, full_out)
    gain_two = gain_ffn.astype(F32)
    normed_two_f, rstat_two = rms_stats(middle)
    if ffn_piece % 128 == 0:
        ffn_in_task = ShardGather([w_gate, w_up], ffn_piece)
    else:
        ffn_in_task = ShardGather([jnp.concatenate(own_ffn(w_gate) + own_ffn(w_up), axis=1)])
    (normed_two,), (ffn_in,), (ffn_out,) = exchange(
        1,
        "gather_middle",
        RingGather((normed_two_f * gain_two).astype(BF16), absolute=True),
        ffn_in_task,
        ShardGather([lax.dynamic_slice_in_dim(w_down, me * ffn_piece, ffn_piece, 0)]),
    )
    normed_two, ffn_in, ffn_out = flat(normed_two), flat(ffn_in), flat(ffn_out)

    ffn_mid = matmul(normed_two, ffn_in)
    gate_part, up_part = ffn_mid[:, :ffn_width], ffn_mid[:, ffn_width:]
    sig_gate = jax.nn.sigmoid(gate_part)
    silu_gate = gate_part * sig_gate
    hidden = (silu_gate * up_part).astype(BF16)
    out_part = matmul(hidden, ffn_out).astype(BF16)

    grad_hidden = matmul_rows(grad_out_low, ffn_out)
    grad_gate_low = (
        grad_hidden * up_part * (sig_gate * (1.0 + gate_part * (1.0 - sig_gate)))
    ).astype(BF16)
    grad_up_low = (grad_hidden * silu_gate).astype(BF16)
    grad_mid_low = jnp.concatenate([grad_gate_low, grad_up_low], axis=1)
    (grad_normed_two,), (grad_ffn_in,), (grad_ffn_out,) = exchange(
        2,
        "sum_middle",
        RingSum(matmul_rows(grad_mid_low, ffn_in), absolute=True),
        ShardSum(weight_grad(normed_two, grad_mid_low)),
        ShardSum(weight_grad(hidden, grad_out_low)),
    )
    back_two, grad_gain_two = norm_back(grad_normed_two, normed_two_f, rstat_two, gain_two)
    grad_middle = cotangent[0].astype(F32) + back_two

    grad_branch_low = grad_middle.astype(BF16)
    grad_gated = matmul_rows(grad_branch_low, full_out).astype(BF16)
    grad_gated = rows_to_columns(widen(grad_gated, padded)).astype(F32)
    grad_branch_own = rows_to_columns(widen(grad_branch_low, padded))
    grad_attn_low = (grad_gated * gate_value).astype(BF16)
    grad_gatelog_low = (grad_gated * attended * (gate_value * (1.0 - gate_value))).astype(BF16)

    (spread_ffn_in,), (spread_ffn_out,), (out_sum,), (gated_all,), (grad_qkv, row_sums, column_sums) = exchange(
        6,
        "attend_back",
        RingGather(grad_ffn_in, absolute=True),
        RingGather(grad_ffn_out, absolute=True),
        RingSum(out_part, absolute=True),
        RingGather(gated, absolute=True),
        AttentionBackward(qkv, decay, seg, own_heads, log_totals, grad_attn_low),
    )
    output, gated_all = middle + out_sum, flat(gated_all)
    later = running_sum(row_sums - column_sums.T, backward=True)
    grad_logits_low = (later * jax.nn.sigmoid(-forget_logits)).astype(BF16)
    bias_part = jnp.zeros((own_heads * n_ctx,), F32)
    bias_part = lax.dynamic_update_slice_in_dim(
        bias_part, jnp.sum(grad_logits_low.astype(F32), axis=0), me * own_heads, 0
    )[:n_heads]

    grad_mixed_low = jnp.concatenate([grad_qkv, grad_gatelog_low, grad_logits_low], axis=1)
    (grad_normed,), (grad_mixed_in,), (grad_out_part,) = exchange(
        3,
        "sum_end",
        RingSum(matmul_rows(grad_mixed_low, mixed_in), absolute=True),
        ShardSum(weight_grad(normed, grad_mixed_low)),
        ShardSum(weight_grad(gated_all, grad_branch_own)),
    )
    back_one, grad_gain_one = norm_back(grad_normed, normed_one, rstat_one, gain_one)
    grad_inputs = grad_middle + back_one

    def pad_rows(rows):
        rows = [jnp.pad(row, (0, width - row.shape[0])) for row in rows]
        return jnp.stack(rows + [jnp.zeros((width,), F32)] * (8 - len(rows)))

    grad_attn_part = jnp.concatenate([grad_mixed_in, grad_out_part], axis=1)
    (spread_attn,), (small,) = exchange(
        4,
        "gather_end",
        RingGather(grad_attn_part, absolute=True),
        SmallSum(pad_rows([grad_gain_one, grad_gain_two, bias_part])),
    )
    sizes = [own_width] * 4 + [own_heads, own_width]
    if ffn_piece % 128 == 0:
        grad_gate, grad_up = ffn_columns(spread_ffn_in, n_fsdp)
    else:
        whole = spread_ffn_in.reshape(n_ctx, shard_rows, 2, n_fsdp, ffn_piece)
        whole = jnp.transpose(whole, (2, 1, 3, 0, 4)).reshape(2, shard_rows, -1).astype(F32)
        grad_gate, grad_up = whole[0], whole[1]
    grad_weights = head_columns(spread_attn, sizes, [width] * 4 + [n_heads, width])
    return (
        output.astype(BF16)[None],
        grad_inputs[None],
        small[0],
        grad_weights[0],
        grad_weights[1],
        grad_weights[2],
        grad_weights[4],
        small[2, :n_heads],
        grad_weights[3],
        grad_weights[5],
        small[1],
        grad_gate,
        grad_up,
        spread_ffn_out.reshape(ffn_rows, width).astype(F32),
    )


def solution(mesh):
    rows, blocks = P("fsdp", None), P("fsdp", "ctx", None)
    return jax.shard_map(
        shards,
        mesh=mesh,
        in_specs=(blocks, rows, P())
        + (rows,) * 4
        + (P(), rows, rows, P(), rows, rows, rows, blocks),
        out_specs=(blocks, blocks, P())
        + (rows,) * 4
        + (P(), rows, rows, P(), rows, rows, rows),
        check_vma=False,
    )
```

time: 754 us -> 613 us (0.81)
  Pallas kernels: 288 us -> 443 us
  local copies, waits for them, and re-layouts: 131 us -> 44.5 us
  waiting for transfers between devices: 92.2 us -> 11.3 us
  blocking collectives: 55.7 us -> 0 us
  matrix products: 104 us -> 54.3 us
  other arithmetic: 50.5 us -> 21.1 us
    pallas_call x5 -> x9, Pallas kernels: 288 us -> 443 us  [the longest x7 431 us: exchange(): pl.pallas_call(kernel, out_shape=sum([task.outs for task in tasks], []),...]
    all_gather x7 -> x1, waiting for transfers between devices: 88.1 us -> 0.01 us  [shards(): full_out = lax.all_gather(out_shard, 'fsdp', axis=0, tiled=True)]
    convert_element_type x13 -> x3, local copies, waits for them, and re-layouts: 54.3 us -> 6.91 us  [the longest x2 4.36 us: __init__(): partial.astype(BF16).reshape(shards, rows, width)]
    psum x1 -> x0, blocking collectives: 41.5 us -> none  [shards(): small = lax.psum((grad_gain_one, grad_gain_two, bias_part), ('ctx', 'fsdp'))]
    unnamed x80 -> x135, local copies, waits for them, and re-layouts: 51.3 us -> 17.1 us
    dot_general x5 -> x2, matrix products: 29.1 us -> 0.46 us  [running_sum(): jnp.einsum('st,btk->bsk', wedge, blocks, precision=lax.Precision.HIGHEST)]
    convert_element_type x4 -> x2, other arithmetic: 24 us -> 1.06 us  [the longest x1 0.93 us: shards(): grad_gated = rows_to_columns(widen(grad_gated, padded)).astype(F32)]
    all_to_all x1 -> x0, blocking collectives: 14.2 us -> none  [columns_to_rows(): return lax.all_to_all(value, 'ctx', split_axis=0, concat_axis=1, tiled=True)]
  transfers between devices with their start and end apart: 14 -> 4, of which waited for: 2 -> 2; matrix products, arithmetic and copies ran while one was open for 30% -> 8% of each run, Pallas kernels for 39% -> 32%
where the time goes in v2:
time: 613 us; the launch traced here: 603 us
  Pallas kernels  443 us (72%)
  matrix products  54.3 us (9%)
  local copies, waits for them, and re-layouts  44.5 us (7%)
  other arithmetic  21.1 us (3%)
  between operations  15.3 us (2%)
  starting transfers between devices  13 us (2%)
  waiting for transfers between devices  11.3 us (2%)
    pallas_call x7, Pallas kernels, exchange(): pl.pallas_call(kernel, out_shape=sum([task.outs for task in tasks], []),...  431 us
    dot_general x5, matrix products, matmul(): return jnp.dot(left, right, preferred_element_type=F32)  22.8 us
    dot_general x4, matrix products, weight_grad(): lax.dot_general(left, right, (((0,), (0,)), ((), ())), preferred_element_...  17.1 us
    unnamed x135, local copies, waits for them, and re-layouts  17.1 us
    dot_general x4, matrix products, matmul_rows(): lax.dot_general(left, right, (((1,), (1,)), ((), ())), preferred_element_...  13.9 us
  transfers between devices with their start and end apart: 4, of which 2 were waited for; matrix products, arithmetic and copies ran while one was open for 8% of the time, Pallas kernels for 32%

profile of v2, /device:TPU:0, one launch (start us, length us, event | category | flops | bytes accessed | tf_op | source)
XLA Modules:
  0.0 602.7 jit_solution(2990941977527339315)
XLA Ops:
  15.9 2.1 concatenate.12.refs_1_
  19.2 35.9 %gather_start.1 = (bf16[8,128,1536]{2,1,0:T(8,128)(2,1)}, bf16[4,384,771]{2,1,0:T(8,128)(2,1)S(1)}) custom-call(bf16[128,1536]{1,0:T(8,128)(2,1)S(1)} %fusion.19.refs_0_, bf16[384,771]{1,0:T(8,128)(2,1)S(1)} %copy-done.17), custom_call_target="tpu_custom_call" | custom-call | bytes 100000000 | tf_op jit(solution)/shard_map/gather_start/pallas_call | solution.py:574
  56.8 3.3 fusion.27
  66.7 5.2 fusion.4.refs_1_.refs_4_
  71.9 34.9 %attend.1 = (bf16[8,128,1536]{2,1,0:T(8,128)(2,1)}, f32[1024,192]{1,0:T(8,128)S(1)}, f32[1024,3]{1,0:T(8,128)S(1)}) custom-call(bf16[128,1536]{1,0:T(8,128)(2,1)S(1)} %bitcast.120, bf16[1024,576]{1,0:T(8,128)(2,1)S(1)} %fusion.4.refs_1_.refs_4_, f32[1024,3]{1,0:T(8,128)S(1)} %copy-done.7, f32[3,1024]{1,0:T(4,128)S(1)} %bitcast.124, s32[1024,1]{1,0:T(8,128)S(1)} %copy-done.9, ...), custom_call_target="tpu_custom_call" | custom-call | bytes 100000000 | tf_op jit(solution)/shard_map/attend/pallas_call | solution.py:574
  112.0 4.4 all-to-all-start
  118.5 7.2 %all-to-all-done = bf16[8,128,192]{1,2,0:T(8,128)(2,1)} async-done(((bf16[8,128,192]{1,2,0:T(8,128)(2,1)}), bf16[8,128,192]{1,2,0:T(8,128)(2,1)}, u32[]{:S(2)}, u32[]{:S(2)}) %all-to-all-start) | async-done | bytes 393248 | tf_op jit(solution)/shard_map/all_to_all | solution.py:658
  125.7 3.5 multiply_reduce_fusion.2
  129.3 59.1 %gather_middle.1 = (bf16[8,128,1536]{2,1,0:T(8,128)(2,1)S(1)}, bf16[4,384,1024]{2,1,0:T(8,128)(2,1)}, bf16[4,128,1536]{2,1,0:T(8,128)(2,1)S(1)}) custom-call(bf16[128,1536]{1,0:T(8,128)(2,1)S(1)} %multiply_convert_fusion.4.refs_0_, bf16[384,4096]{1,0:T(8,128)(2,1)} %refs_1_.1, bf16[384,4096]{1,0:T(8,128)(2,1)} %refs_2_.1, bf16[128,1536]{1,0:T(8,128)(2,1)S(1)} %copy-done.18), custom_call_target="tpu_custom_call" | custom-call | bytes 100000000 | tf_op jit(solution)/shard_map/gather_middle/pallas_call | solution.py:574
  188.5 6.1 %fusion.59 = f32[1024,1024]{0,1:T(8,128)S(1)} fusion(bf16[1024,1536]{1,0:T(8,128)(2,1)S(1)} %bitcast.127, bf16[1536,1024]{1,0:T(8,128)(2,1)} %bitcast.147), kind=kOutput, calls=%fused_computation.117 | convolution fusion | flops 3221225472 | bytes 10485760 | tf_op jit(solution)/shard_map/dot_general | solution.py:14
  194.6 2.5 multiply_convert_fusion.2
  197.2 5.8 convolution_convert_fusion.2
  202.9 4.9 convolution_convert_fusion.3
  209.6 38.4 %sum_middle.1 = (f32[128,1536]{1,0:T(8,128)S(1)}, bf16[384,1024]{1,0:T(8,128)(2,1)S(1)}, bf16[128,1536]{1,0:T(8,128)(2,1)S(1)}) custom-call(bf16[8,128,1536]{2,1,0:T(8,128)(2,1)} %bitcast.139, bf16[4,384,1024]{2,1,0:T(8,128)(2,1)} %bitcast.138, bf16[4,128,1536]{2,1,0:T(8,128)(2,1)S(1)} %bitcast.122), custom_call_target="tpu_custom_call" | custom-call | bytes 100000000 | tf_op jit(solution)/shard_map/sum_middle/pallas_call | solution.py:574
  253.3 4.3 all-to-all-start.1
  260.7 4.7 convolution_convert_fusion.1
  265.4 4.1 all-to-all-done.1
  269.5 4.3 all-to-all-start.2
  274.8 2.6 copy.133
  277.3 2.8 fusion.14
  280.2 156.3 %attend_back.1 = (bf16[8,384,1024]{2,1,0:T(8,128)(2,1)}, bf16[8,128,1536]{2,1,0:T(8,128)(2,1)}, f32[128,1536]{1,0:T(8,128)S(1)}, bf16[8,128,1536]{2,1,0:T(8,128)...) custom-call(bf16[384,1024]{1,0:T(8,128)(2,1)S(1)} %copy-done.22, ...), custom_call_target="tpu_custom_call" | custom-call | bytes 100000000 | tf_op jit(solution)/shard_map/attend_back/pallas_call | solution.py:574
  440.9 6.8 %convolution_convert_fusion.4 = bf16[1536,771]{0,1:T(8,128)(2,1)} fusion(bf16[1024,1536]{1,0:T(8,128)(2,1)} %bitcast.144, bf16[1024,3]{1,0:T(8,128)(2,1)S(1)} %get-tuple-element.171, bf16[1024,192]{1,0:T(8,128)(2,1)} %get-tuple-element.177, bf16[1024,576]{1,0:T(8,128)(2,1)} %get-tuple-element.61), kind=kOutput, calls=%fused_computation.4 | convolution fusion | flops 2431277568 | bytes 7093248 | tf_op jit(solution)/shard_map/dot_general | solution.py:22
  447.7 4.9 convolution_convert_fusion
  452.6 2.8 fusion
  456.5 3.2 copy.139
  460.9 36.1 %sum_end.1 = (f32[128,1536]{1,0:T(8,128)S(1)}, bf16[384,771]{1,0:T(8,128)(2,1)S(1)}, bf16[384,192]{1,0:T(8,128)(2,1)S(1)}) custom-call(bf16[8,128,1536]{2,1,0:T(8,128)(2,1)} %bitcast.137, bf16[4,384,771]{2,1,0:T(8,128)(2,1)S(1)} %bitcast.119, bf16[4,384,192]{2,1,0:T(8,128)(2,1)S(1)} %bitcast.121), custom_call_target="tpu_custom_call" | custom-call | bytes 100000000 | tf_op jit(solution)/shard_map/sum_end/pallas_call | solution.py:574
  499.8 70.5 %gather_end.1 = (bf16[8,384,963]{2,1,0:T(8,128)(2,1)}, f32[8,1536]{1,0:T(8,128)S(1)}) custom-call(bf16[384,963]{1,0:T(8,128)(2,1)S(1)} %pad_maximum_fusion.4.refs_0_, f32[8,1536]{1,0:T(8,128)S(1)} %stack.19.refs_1_), custom_call_target="tpu_custom_call" | custom-call | bytes 100000000 | tf_op jit(solution)/shard_map/gather_end/pallas_call | solution.py:574
  571.5 2.8 copy-done.5
  574.2 6.7 %head_columns.1 = (f32[384,1536]{1,0:T(8,128)}, f32[384,1536]{1,0:T(8,128)}, f32[384,1536]{1,0:T(8,128)}, f32[384,1536]{1,0:T(8,128)}, f32[384,24]{1,0:T(8,128)S(1)}, /*index=5*/f32[384,1536]{1,0:T(8,128)}) custom-call(bf16[8,384,963]{2,1,0:T(8,128)(2,1)S(1)} %copy-done.5), custom_call_target="tpu_custom_call" | custom-call | bytes 17750016 | tf_op jit(solution)/shard_map/head_columns/pallas_call | solution.py:639
  581.7 2.8 copy-done.4
  584.5 5.3 ffn_columns.1
  589.9 4.2 bitcast_convert_fusion
  (194 shorter events, 49.0 us)
Async XLA Ops:
  7.2 110.5 %copy-start = (bf16[1024,1536]{1,0:T(8,128)(2,1)S(1)}, bf16[1024,1536]{1,0:T(8,128)(2,1)}, u32[]{:S(2)}) copy-start(bf16[1024,1536]{1,0:T(8,128)(2,1)} %param.28) | copy-start | bytes 9437188
  7.2 118.5 %all-gather.2.cloned.1.call-start = ((), (), s32[]{:S(2)}) async-start(), calls=%async_computation.3 | async-start | bytes 5898240 | tf_op jit(solution)/shard_map/all_gather | solution.py:725
  9.6 47.0 %copy-start.47 = (f32[1536]{0:T(1024)}, f32[1536]{0:T(1024)S(1)}, u32[]{:S(2)}) copy-start(f32[1536]{0:T(1024)S(1)} %convert_element_type.97) | copy-start | bytes 18436
  10.8 45.9 %copy-start.62 = (f32[24]{0:T(128)S(1)}, f32[24]{0:T(128)}, u32[]{:S(2)}) copy-start(f32[24]{0:T(128)} %param.22) | copy-start | bytes 292
  10.8 49.3 %copy-start.53 = (f32[128]{0:T(128)}, f32[128]{0:T(128)S(1)}, u32[]{:S(2)}) copy-start(f32[128]{0:T(128)S(1)} %add_rsqrt_fusion.1) | copy-start | bytes 1540
  56.8 8.9 %copy-start.29 = (s32[1,1024]{1,0:T(1,128)S(1)}, s32[1,1024]{1,0:T(1,128)}, u32[]{:S(2)}) copy-start(s32[1,1024]{1,0:T(1,128)} %refs_8_.1) | copy-start | bytes 12292
  71.9 37.0 %copy-start.41 = (f32[1024,195]{1,0:T(8,128)S(1)}, f32[1024,195]{1,0:T(8,128)}, u32[]{:S(2)}) copy-start(f32[1024,195]{1,0:T(8,128)} %copy-done.40) | copy-start | bytes 2396164
  112.0 13.7 %all-to-all-start = ((bf16[8,128,192]{1,2,0:T(8,128)(2,1)}), bf16[8,128,192]{1,2,0:T(8,128)(2,1)}, u32[]{:S(2)}, u32[]{:S(2)}) async-start(bf16[8,128,192]{1,2,0:T(8,128)(2,1)} %copy.131), calls=%async_computation | async-start | bytes 786432 | tf_op jit(solution)/shard_map/all_to_all | solution.py:658
  129.1 120.0 %copy-start.36 = (f32[128,1536]{1,0:T(8,128)}, f32[128,1536]{1,0:T(8,128)S(1)}, u32[]{:S(2)}) copy-start(f32[128,1536]{1,0:T(8,128)S(1)} %get-tuple-element.186) | copy-start | bytes 2359300
  129.2 120.0 %copy-start.51 = (f32[128]{0:T(128)}, f32[128]{0:T(128)S(1)}, u32[]{:S(2)}) copy-start(f32[128]{0:T(128)S(1)} %add_rsqrt_fusion) | copy-start | bytes 1540
  188.5 6.1 %copy-start.34 = (bf16[4,128,1536]{2,1,0:T(8,128)(2,1)}, bf16[4,128,1536]{2,1,0:T(8,128)(2,1)S(1)}, u32[]{:S(2)}) copy-start(bf16[4,128,1536]{2,1,0:T(8,128)(2,1)S(1)} %get-tuple-element.53) | copy-start | bytes 4718596
  188.5 6.1 %copy-start.59 = (bf16[8,128,1536]{2,1,0:T(8,128)(2,1)S(1)}, bf16[8,128,1536]{2,1,0:T(8,128)(2,1)}, u32[]{:S(2)}) copy-start(bf16[8,128,1536]{2,1,0:T(8,128)(2,1)} %get-tuple-element.52) | copy-start | bytes 9437188
  197.1 10.7 %copy-start.63 = (bf16[1024,512]{0,1:T(8,128)(2,1)}, bf16[1024,512]{0,1:T(8,128)(2,1)S(1)}, u32[]{:S(2)}) copy-start(bf16[1024,512]{0,1:T(8,128)(2,1)S(1)} %get-tuple-element.176) | copy-start | bytes 3145732
  197.2 5.8 copy-start.60
  207.8 42.9 %slice-start = ((s8[4718592]{0:T(1024)(128)(4,1)}), s8[4194304]{0:T(1024)(128)(4,1)S(1)}, s32[]{:S(2)}) async-start(s8[4718592]{0:T(1024)(128)(4,1)} %bitcast.134), calls=%async_computation.4 | async-start | bytes 8388608
  209.6 41.1 %slice-start.1 = ((s8[4718592]{0:T(1024)(128)(4,1)}), s8[524288]{0:T(1024)(128)(4,1)S(1)}, s32[]{:S(2)}) async-start(s8[4718592]{0:T(1024)(128)(4,1)} %bitcast.134), calls=%async_computation.5 | async-start | bytes 1048576
  250.7 10.0 %copy-start.35 = (bf16[4,128,1536]{2,1,0:T(8,128)(2,1)S(1)}, bf16[4,128,1536]{2,1,0:T(8,128)(2,1)}, u32[]{:S(2)}) copy-start(bf16[4,128,1536]{2,1,0:T(8,128)(2,1)} %copy-done.34) | copy-start | bytes 4718596
  252.4 8.3 %copy-start.49 = (f32[1536]{0:T(1024)S(1)}, f32[1536]{0:T(1024)}, u32[]{:S(2)}) copy-start(f32[1536]{0:T(1024)} %get-tuple-element.164) | copy-start | bytes 18436
  253.3 16.2 %all-to-all-start.1 = ((bf16[128,8,192]{0,2,1:T(8,128)(2,1)}), bf16[128,8,192]{0,2,1:T(8,128)(2,1)S(1)}, u32[]{:S(2)}, u32[]{:S(2)}) async-start(bf16[128,8,192]{0,2,1:T(8,128)(2,1)} %bitcast.22), calls=%async_computation.1 | async-start | bytes 786432 | tf_op jit(solution)/shard_map/all_to_all | solution.py:654
  265.4 11.9 %copy-start.12 = (f32[1024,192]{1,0:T(8,128)S(1)}, f32[1024,192]{1,0:T(8,128)}, u32[]{:S(2)}) copy-start(f32[1024,192]{1,0:T(8,128)} %copy-done.11) | copy-start | bytes 2359300
  269.5 183.0 %all-to-all-start.2 = ((bf16[128,8,192]{0,2,1:T(8,128)(2,1)}), bf16[128,8,192]{0,2,1:T(8,128)(2,1)}, u32[]{:S(2)}, u32[]{:S(2)}) async-start(bf16[128,8,192]{0,2,1:T(8,128)(2,1)} %bitcast.32), calls=%async_computation.2 | async-start | bytes 786432 | tf_op jit(solution)/shard_map/all_to_all | solution.py:654
  274.7 5.4 copy-start.31
  280.2 158.8 %copy-start.50 = (f32[8,8]{1,0:T(8,128)S(1)}, f32[8,8]{1,0:T(8,128)}, u32[]{:S(2)}) copy-start(f32[8,8]{1,0:T(8,128)} %get-tuple-element.183) | copy-start | bytes 772
  280.2 159.4 %copy-start.56 = (f32[3]{0:T(128)S(1)}, f32[3]{0:T(128)}, u32[]{:S(2)}) copy-start(f32[3]{0:T(128)} %copy-done.55) | copy-start | bytes 40
  437.3 10.3 %copy-start.19 = (f32[128,1536]{1,0:T(8,128)}, f32[128,1536]{1,0:T(8,128)S(1)}, u32[]{:S(2)}) copy-start(f32[128,1536]{1,0:T(8,128)S(1)} %get-tuple-element.60) | copy-start | bytes 2359300
  440.9 6.8 %copy-start.33 = (bf16[4,384,771]{2,1,0:T(8,128)(2,1)S(1)}, bf16[4,384,771]{2,1,0:T(8,128)(2,1)}, u32[]{:S(2)}) copy-start(bf16[4,384,771]{2,1,0:T(8,128)(2,1)} %copy-done.32) | copy-start | bytes 7105540
  440.9 6.8 %copy-start.44 = (bf16[1024,192]{1,0:T(8,128)(2,1)S(1)}, bf16[1024,192]{1,0:T(8,128)(2,1)}, u32[]{:S(2)}) copy-start(bf16[1024,192]{1,0:T(8,128)(2,1)} %get-tuple-element.177) | copy-start | bytes 1179652
  440.9 6.8 %copy-start.61 = (bf16[1024,576]{1,0:T(8,128)(2,1)S(1)}, bf16[1024,576]{1,0:T(8,128)(2,1)}, u32[]{:S(2)}) copy-start(bf16[1024,576]{1,0:T(8,128)(2,1)} %get-tuple-element.61) | copy-start | bytes 3538948
  460.9 37.0 %copy-start.38 = (bf16[1,128,1536]{2,1,0:T(8,128)(2,1)S(1)}, bf16[1,128,1536]{2,1,0:T(8,128)(2,1)}, u32[]{:S(2)}) copy-start(bf16[1,128,1536]{2,1,0:T(8,128)(2,1)} %param.15) | copy-start | bytes 1179652
  460.9 37.0 %copy-start.48 = (f32[1536]{0:T(1024)S(1)}, f32[1536]{0:T(1024)}, u32[]{:S(2)}) copy-start(f32[1536]{0:T(1024)} %copy-done.47) | copy-start | bytes 18436
  460.9 37.0 %copy-start.54 = (f32[128]{0:T(128)S(1)}, f32[128]{0:T(128)}, u32[]{:S(2)}) copy-start(f32[128]{0:T(128)} %copy-done.53) | copy-start | bytes 1540
  589.9 5.6 copy-start.1
  (38 other events, 116.0 us)
Sparse Core Ops, SparseCore 0:
  56.8 37.2 all-gather.1

commit v3 on v2

v3 whole, which is shorter than its diff:
```python
import jax
import jax.numpy as jnp
from jax import lax
from jax.experimental import pallas as pl
from jax.experimental.pallas import tpu as pltpu
from jax.sharding import PartitionSpec as P

EPSILON = 1e-06
NEGATIVE = -1e30
BF16, F32 = jnp.bfloat16, jnp.float32


def matmul(left, right):
    return jnp.dot(left, right, preferred_element_type=F32)


def matmul_rows(left, right):
    return lax.dot_general(left, right, (((1,), (1,)), ((), ())), preferred_element_type=F32)


def weight_grad(left, right):
    return lax.dot_general(left, right, (((0,), (0,)), ((), ())), preferred_element_type=F32)


def rms_stats(values):
    rstat = lax.rsqrt(jnp.mean(values * values, axis=-1, keepdims=True) + EPSILON)
    return (values * rstat, rstat)


def norm_back(grad_in, normed, rstat, gain):
    grad_normed = grad_in * gain
    grad_gain = jnp.sum(grad_in * normed, axis=0)
    grad_values = rstat * (
        grad_normed - normed * jnp.mean(grad_normed * normed, axis=-1, keepdims=True)
    )
    return (grad_values, grad_gain)


MESH = pl.DeviceIdType.MESH
RING_PIECES = 4


def ring_place(ctx, count):
    odd = ctx % 2
    return ctx // 2 + odd * (count - 1 - 2 * (ctx // 2))


def ring_index(place, count):
    back = place // (count // 2)
    return 2 * place + back * (2 * (count - 1 - place) + 1 - 2 * place)


class Ring:
    def __init__(self, count):
        self.count, self.half = count, count // 2
        self.ctx, self.fsdp = lax.axis_index("ctx"), lax.axis_index("fsdp")
        self.place = ring_place(self.ctx, count)

    def at(self, offset):
        return ring_index((self.place + offset + self.count) % self.count, self.count)

    def device(self, offset):
        return (self.at(offset), self.fsdp)


def greet(devices):
    barrier = pltpu.get_barrier_semaphore()
    for device in devices:
        pl.semaphore_signal(barrier, inc=1, device_id=device, device_id_type=MESH)
    pl.semaphore_wait(barrier, len(devices))


def remote(src, dst, send, recv, device):
    return pltpu.make_async_remote_copy(
        src_ref=src, dst_ref=dst, send_sem=send, recv_sem=recv, device_id=device, device_id_type=MESH
    )


def carried(step, half, pieces, way):
    if step < half - 1:
        return range(pieces)
    return range(pieces // 2) if way == 0 else range(pieces // 2, pieces)


def ring_slot(ring, offset, absolute):
    if absolute:
        return ring.at(offset)
    if abs(offset) == ring.half:
        return ring.count - 1
    return 2 * offset - 1 if offset > 0 else -2 * offset


def ring_gather(ring, own, full, local_sem, send_sem, recv_sem, absolute, pieces=RING_PIECES):
    rows = own.shape[0] // pieces

    def part(k):
        return pl.ds(k * rows, rows)

    def slot(offset):
        return ring_slot(ring, offset, absolute)

    keep = pltpu.make_async_copy(own, full.at[slot(0)], local_sem)
    keep.start()
    copies = {}
    for step in range(ring.half):
        for k in range(pieces):
            for way, sign in ((0, 1), (1, -1)):
                if k not in carried(step, ring.half, pieces, way):
                    continue
                if step > 0:
                    copies[step - 1, k, way].wait_recv()
                src = own.at[part(k)] if step == 0 else full.at[slot(-sign * step), part(k)]
                to = slot(-sign * step if absolute else -sign * (step + 1))
                copy = remote(
                    src,
                    full.at[to, part(k)],
                    send_sem.at[step, k, way],
                    recv_sem.at[step, k, way],
                    ring.device(sign),
                )
                copy.start()
                copies[step, k, way] = copy
            yield
    for (step, k, way), copy in copies.items():
        if step == ring.half - 1 or k not in carried(step + 1, ring.half, pieces, way):
            copy.wait_recv()
    for copy in copies.values():
        copy.wait_send()
    keep.wait()


def ring_sum(ring, parts, held, total, send_sem, recv_sem, absolute, pieces=RING_PIECES):
    rows = parts.shape[1] // pieces

    def place(offset):
        return ring_slot(ring, offset, absolute)

    def part(k):
        return pl.ds(k * rows, rows)

    copies = {}
    for step in range(ring.half):
        for k in range(pieces):
            for way, sign in ((0, 1), (1, -1)):
                if k not in carried(ring.half - 1 - step, ring.half, pieces, way):
                    continue
                block = place(sign * (ring.half - step))
                src = parts.at[block, part(k)]
                if (step - 1, k, way) in copies:
                    copies[step - 1, k, way].wait_recv()
                    slot = held.at[way, step - 1, part(k)]
                    slot[...] = (slot[...].astype(F32) + src[...].astype(F32)).astype(BF16)
                    src = slot
                copy = remote(
                    src,
                    held.at[way, step, part(k)],
                    send_sem.at[step, k, way],
                    recv_sem.at[step, k, way],
                    ring.device(sign),
                )
                copy.start()
                copies[step, k, way] = copy
            yield
    last = ring.half - 1
    for k in range(pieces):
        for way in range(2):
            copies[last, k, way].wait_recv()
        total[part(k)] = (
            parts[place(0), part(k)].astype(F32)
            + held[0, last, part(k)].astype(F32)
            + held[1, last, part(k)].astype(F32)
        )
    for copy in copies.values():
        copy.wait_send()


def ring_sems(count, pieces=RING_PIECES):
    shape = (count // 2, pieces, 2)
    return [pltpu.SemaphoreType.DMA(shape), pltpu.SemaphoreType.DMA(shape)]


def sems(*counts):
    return [pltpu.SemaphoreType.DMA((max(count, 1),)) for count in counts]


ANYWHERE, VMEM = pl.BlockSpec(memory_space=pl.ANY), pl.BlockSpec(memory_space=pltpu.VMEM)


class RingGather:
    kinds = ("ring",)

    def __init__(self, value, absolute=False):
        self.absolute = absolute
        count = lax.axis_size("ctx")
        self.ins, self.in_specs = [value], [ANYWHERE]
        self.outs, self.out_specs = (
            [jax.ShapeDtypeStruct((count,) + value.shape, value.dtype)],
            [ANYWHERE],
        )
        self.scratch = [pltpu.SemaphoreType.DMA] + ring_sems(count)

    def run(self, ring, ins, outs, scratch):
        return ring_gather(ring, ins[0], outs[0], *scratch, absolute=self.absolute)


def shard_pair(ring, shards):
    me = ring.fsdp
    pair = me + 1 - 2 * (me % 2)
    return pair, [(me + 2 * hop) % shards for hop in range(1, shards // 2)]


def all_peers(ring):
    count, shards = lax.axis_size("ctx"), lax.axis_size("fsdp")
    siblings = [(ring.ctx, (ring.fsdp + hop) % shards) for hop in range(1, shards)]
    return siblings, [((ring.ctx + hop) % count, ring.fsdp) for hop in range(1, count)]


def idle(turns):
    for _ in range(turns):
        yield


def together(*walks):
    walks = list(walks)
    while walks:
        walks = [walk for walk in walks if next(walk, walks) is None]
        yield


def shard_gather(ring, fill, whole, local_sem, send_sem, recv_sem):
    shards, me = lax.axis_size("fsdp"), ring.fsdp
    rows = whole.shape[0] // shards
    pair, others = shard_pair(ring, shards)

    def shard(index):
        return whole.at[pl.ds(pl.multiple_of(index * rows, rows), rows)]

    local, source = fill(shard(me), local_sem)
    for copy in local:
        copy.start()
    yield
    if source is None:
        for copy in local:
            copy.wait()
    sent = shard(me) if source is None else source
    copies = [
        remote(sent, shard(me), send_sem.at[i], recv_sem.at[i], (ring.ctx, to))
        for i, to in enumerate([pair] + others)
    ]
    for copy in copies:
        copy.start()
    yield from idle(3 * RING_PIECES)
    passed = []
    for i in range(1, len(copies)):
        copies[i].wait_recv()
        origin = (me - 2 * i + shards) % shards
        at = shards // 2 - 1 + i
        copy = remote(
            shard(origin), shard(origin), send_sem.at[at], recv_sem.at[at], (ring.ctx, pair)
        )
        copy.start()
        passed.append(copy)
    yield from idle(2)
    copies[0].wait_recv()
    for copy in passed:
        copy.wait_recv()
    for copy in copies + passed:
        copy.wait_send()
    if source is not None:
        for copy in local:
            copy.wait()


def shard_gather_sems(parts):
    shards = lax.axis_size("fsdp")
    return sems(parts, shards - 1, shards - 1)


class ShardGather:
    kinds = ("shard",)

    def __init__(self, shard):
        shards = lax.axis_size("fsdp")
        self.ins, self.in_specs = [shard], [ANYWHERE]
        self.outs = [jax.ShapeDtypeStruct((shards * shard.shape[0], shard.shape[1]), BF16)]
        self.out_specs, self.scratch = [ANYWHERE], shard_gather_sems(1)

    def run(self, ring, ins, outs, scratch):
        def fill(shard, local_sem):
            return [pltpu.make_async_copy(ins[0], shard, local_sem.at[0])], ins[0]

        return shard_gather(ring, fill, outs[0], *scratch)


def shard_sum(ring, parts, total, near, far, near_send, near_recv, far_send, far_recv):
    shards, me = lax.axis_size("fsdp"), ring.fsdp
    half, core, chip = shards // 2, me % 2, me // 2
    pair, others = shard_pair(ring, shards)
    rows = parts.shape[0] // shards

    def shard(index):
        return pl.ds(pl.multiple_of(index * rows, rows), rows)

    first = [
        remote(
            parts.at[shard(2 * i + 1 - core)],
            near.at[i],
            near_send.at[i],
            near_recv.at[i],
            (ring.ctx, pair),
        )
        for i in range(half)
    ]
    for copy in first:
        copy.start()
    yield from idle(2)
    for copy in first:
        copy.wait_recv()
    second = []
    for hop in range(1, half):
        to = (chip + hop) % half
        near[to] = (near[to].astype(F32) + parts[shard(2 * to + core)].astype(F32)).astype(BF16)
        copy = remote(
            near.at[to],
            far.at[hop - 1],
            far_send.at[hop - 1],
            far_recv.at[hop - 1],
            (ring.ctx, others[hop - 1]),
        )
        copy.start()
        second.append(copy)
    yield from idle(3 * RING_PIECES)
    sums = parts[shard(me)].astype(F32) + near[chip].astype(F32)
    for hop, copy in enumerate(second):
        copy.wait_recv()
        sums = sums + far[hop].astype(F32)
    total[...] = sums.astype(BF16)
    for copy in first + second:
        copy.wait_send()


def shard_sum_scratch(rows, width):
    half = lax.axis_size("fsdp") // 2
    return [
        pltpu.VMEM((half, rows, width), BF16),
        pltpu.VMEM((max(half - 1, 1), rows, width), BF16),
    ] + sems(half, half, half - 1, half - 1)


class Ffn:
    kinds = ("ring", "shard")

    def __init__(self, normed, grad_out, w_in, w_out, piece):
        count, shards = lax.axis_size("ctx"), lax.axis_size("fsdp")
        rows, width = normed.shape
        self.aligned = len(w_in) == 2
        self.piece, self.inner = piece, piece * shards
        inner, both = self.inner, 2 * self.inner
        shard_rows = width // shards
        self.ins = [normed, grad_out, w_out] + list(w_in)
        self.in_specs = [ANYWHERE, VMEM] + [ANYWHERE] * (1 + len(w_in))
        self.outs = [
            jax.ShapeDtypeStruct((rows, width), F32),
            jax.ShapeDtypeStruct((rows, width), F32),
            jax.ShapeDtypeStruct((shard_rows, both), BF16),
            jax.ShapeDtypeStruct((piece, width), BF16),
        ]
        self.out_specs = [VMEM] * 4
        held = pltpu.VMEM((2, count // 2, rows, width), BF16)
        groups = [
            [pltpu.VMEM((count, rows, width), BF16), pltpu.SemaphoreType.DMA] + ring_sems(count),
            [pltpu.VMEM((width, both), BF16)] + shard_gather_sems(2 * shards),
            [pltpu.VMEM((inner, width), BF16)] + shard_gather_sems(1),
            [pltpu.VMEM((count, rows, inner), BF16), pltpu.VMEM((count, rows, both), BF16)],
            [pltpu.VMEM((count, rows, width), BF16), held] + ring_sems(count),
            [pltpu.VMEM((count, rows, width), BF16), held] + ring_sems(count),
            [pltpu.VMEM((width, both), BF16)] + shard_sum_scratch(shard_rows, both),
            [pltpu.VMEM((inner, width), BF16)] + shard_sum_scratch(piece, width),
        ]
        self.sizes = [len(group) for group in groups]
        self.scratch = sum(groups, [])

    def run(self, ring, ins, outs, scratch):
        normed, grad_out, w_out_rows = ins[:3]
        inner, piece = self.inner, self.piece
        groups, at = [], 0
        for size in self.sizes:
            groups.append(scratch[at : at + size])
            at += size
        (rows_all, *rows_sems), (w_in, *w_in_sems), (w_out, *w_out_sems) = groups[:3]
        hidden, grad_mid = groups[3]
        (out_part, out_held, *out_sems), (in_part, in_held, *in_sems) = groups[4:6]
        (grad_w_in, *grad_in_rest), (grad_w_out, *grad_out_rest) = groups[6:]
        count, tall = rows_all.shape[:2]
        width = rows_all.shape[2]

        def fill_in(shard, local_sem):
            if not self.aligned:
                return [pltpu.make_async_copy(ins[3], shard, local_sem.at[0])], ins[3]
            copies = []
            for i in range(2):
                for group in range(inner // piece):
                    at = i * (inner // piece) + group
                    start = pl.multiple_of((group * count + ring.ctx) * piece, piece)
                    copies.append(
                        pltpu.make_async_copy(
                            ins[3 + i].at[:, pl.ds(start, piece)],
                            shard.at[:, pl.ds(at * piece, piece)],
                            local_sem.at[at],
                        )
                    )
            return copies, None

        def fill_out(shard, local_sem):
            start = pl.multiple_of(ring.ctx * piece, piece)
            own = w_out_rows.at[pl.ds(start, piece)]
            return [pltpu.make_async_copy(own, shard, local_sem.at[0])], own

        def compute(slots):
            size = (slots.stop - slots.start) * tall

            def load(ref):
                return ref[slots].reshape(size, ref.shape[2])

            def store(ref, columns, value):
                ref[slots, :, columns] = value.astype(BF16).reshape(-1, tall, value.shape[1])

            tile = min(256, inner)

            @pl.loop(0, inner // tile)
            def _(index):
                def columns(start):
                    return pl.ds(pl.multiple_of(start + index * tile, tile), tile)

                gate = matmul(load(rows_all), w_in[:, columns(0)])
                up = matmul(load(rows_all), w_in[:, columns(inner)])
                grad_hidden = matmul_rows(load(grad_out), w_out[columns(0)])
                sig = jax.nn.sigmoid(gate)
                silu = gate * sig
                store(hidden, columns(0), silu * up)
                store(
                    grad_mid, columns(0), grad_hidden * up * (sig * (1.0 + gate * (1.0 - sig)))
                )
                store(grad_mid, columns(inner), grad_hidden * silu)

            wide = 256 if width % 256 == 0 else width

            @pl.loop(0, width // wide)
            def _(index):
                columns = pl.ds(pl.multiple_of(index * wide, wide), wide)
                store(in_part, columns, matmul_rows(load(grad_mid), w_in[columns]))
                store(out_part, columns, matmul(load(hidden), w_out[:, columns]))

        def weight_grads(left, right, grads):
            tile = 128 if left.shape[2] % 128 == 0 else left.shape[2]

            @pl.loop(0, left.shape[2] // tile)
            def _(index):
                columns = pl.ds(pl.multiple_of(index * tile, tile), tile)
                grads[columns] = weight_grad(
                    left[:, :, columns].reshape(count * tall, tile),
                    right[...].reshape(count * tall, right.shape[2]),
                ).astype(BF16)

        yield from together(
            ring_gather(ring, normed, rows_all, *rows_sems, False),
            shard_gather(ring, fill_in, w_in, *w_in_sems),
            shard_gather(ring, fill_out, w_out, *w_out_sems),
        )
        compute(slice(count - 1, count))
        sums = together(
            ring_sum(ring, in_part, in_held, outs[1], *in_sems, False),
            ring_sum(ring, out_part, out_held, outs[0], *out_sems, False),
        )
        for _ in range(RING_PIECES):
            next(sums)
        for pair in range(count // 2 - 1, 0, -1):
            compute(slice(2 * pair - 1, 2 * pair + 1))
            if pair == 2:
                for _ in range(RING_PIECES):
                    next(sums)
        compute(slice(0, 1))
        weight_grads(rows_all, grad_mid, grad_w_in)
        weight_grads(hidden, grad_out, grad_w_out)
        yield from together(
            sums,
            shard_sum(ring, grad_w_in, outs[2], *grad_in_rest),
            shard_sum(ring, grad_w_out, outs[3], *grad_out_rest),
        )


def small_sum_scratch(shape):
    count, shards = lax.axis_size("ctx"), lax.axis_size("fsdp")
    return [
        pltpu.VMEM((shards,) + shape, F32),
        pltpu.VMEM((count,) + shape, F32),
    ] + sems(shards - 1, shards - 1, count - 1, count - 1)


def small_sum(ring, small, total, near, far, near_send, near_recv, far_send, far_recv):
    siblings, peers = all_peers(ring)
    me, row = ring.fsdp, ring.ctx
    near[me] = small[...]
    first = [
        remote(small, near.at[me], near_send.at[i], near_recv.at[i], to)
        for i, to in enumerate(siblings)
    ]
    for copy in first:
        copy.start()
    yield from idle(RING_PIECES)
    for copy in first:
        copy.wait()
    far[row] = sum([near[i] for i in range(len(siblings) + 1)])
    second = [
        remote(far.at[row], far.at[row], far_send.at[i], far_recv.at[i], to)
        for i, to in enumerate(peers)
    ]
    for copy in second:
        copy.start()
    yield from idle(2 * RING_PIECES)
    for copy in second:
        copy.wait()
    total[...] = sum([far[i] for i in range(len(peers) + 1)])


class Attention:
    kinds = ()

    def __init__(self, qkv, decay, seg, own_heads):
        self.rows, self.heads = qkv.shape[0], own_heads
        self.dim = qkv.shape[1] // 3 // own_heads
        self.scaling = self.dim ** (-0.5)
        self.tall = min(256, self.rows)
        self.ins = [qkv, decay, decay.T, seg[:, None], seg[None, :]]

    def block(self, index):
        rows = slice(index * self.tall, (index + 1) * self.tall)
        return rows, (index + 1) * self.tall

    def allowed(self, rows, wide, seg_rows, seg_cols):
        shape = (self.tall, wide)
        here = lax.broadcasted_iota(jnp.int32, shape, 0) + rows.start
        there = lax.broadcasted_iota(jnp.int32, shape, 1)
        return (there <= here) & (seg_rows[rows] == seg_cols[:, :wide])

    def part(self, qkv, which, head, rows):
        start = (which * self.heads + head) * self.dim
        return qkv[rows, start : start + self.dim]

    def scores(self, refs, head, rows, wide, allowed):
        qkv, decay, decay_cols = refs[:3]
        queries = self.part(qkv, 0, head, rows)
        keys = self.part(qkv, 1, head, slice(0, wide))
        scores = matmul_rows(queries, keys) * self.scaling
        scores = scores + decay[rows, head : head + 1] - decay_cols[head : head + 1, :wide]
        return queries, keys, jnp.where(allowed, scores, NEGATIVE)


class AttentionForward(Attention):
    def __init__(self, qkv, decay, seg, own_heads):
        super().__init__(qkv, decay, seg, own_heads)
        self.in_specs = [VMEM] * 5
        self.outs = [
            jax.ShapeDtypeStruct((self.rows, own_heads * self.dim), F32),
            jax.ShapeDtypeStruct((self.rows, own_heads), F32),
        ]
        self.out_specs, self.scratch = [VMEM] * 2, []

    def run(self, ring, ins, outs, scratch):
        for index in range(self.rows // self.tall):
            rows, wide = self.block(index)
            allowed = self.allowed(rows, wide, *ins[3:])
            mixed, totals = [], []
            for head in range(self.heads):
                _, _, scores = self.scores(ins, head, rows, wide, allowed)
                row_max = jnp.max(scores, axis=1, keepdims=True)
                raised = jnp.exp(scores - row_max)
                row_total = jnp.sum(raised, axis=1, keepdims=True)
                probabilities = (raised * (1.0 / row_total)).astype(BF16)
                mixed.append(matmul(probabilities, self.part(ins[0], 2, head, slice(0, wide))))
                totals.append(row_max + jnp.log(row_total))
                if head < self.heads - 1:
                    yield
            outs[0][rows] = jnp.concatenate(mixed, axis=1)
            outs[1][rows] = jnp.concatenate(totals, axis=1)
            yield


def slow(walk, turns):
    for _ in walk:
        yield from idle(turns)


class Backward(Attention):
    kinds = ("all",)

    def __init__(self, qkv, decay, seg, own_heads, named):
        super().__init__(qkv, decay, seg, own_heads)
        self.names = list(named)
        hbm = ("gated", "grad_ffn_in", "grad_ffn_out")
        self.ins = self.ins + [named[name] for name in self.names]
        self.in_specs = [VMEM] * 5 + [ANYWHERE if name in hbm else VMEM for name in self.names]
        count, shards = lax.axis_size("ctx"), lax.axis_size("fsdp")
        tall, width = named["gated"].shape
        hidden = own_heads * self.dim
        self.main = 4 * hidden
        both = -(-(5 * hidden + own_heads) // 128) * 128
        ffn = [named["grad_ffn_in"], named["grad_ffn_out"]]
        shard_rows = width // shards
        self.outs = (
            [jax.ShapeDtypeStruct((tall, width), F32)]
            + [jax.ShapeDtypeStruct((count,) + grad.shape, BF16) for grad in ffn]
            + [jax.ShapeDtypeStruct((count, shard_rows, both), BF16)]
            + [jax.ShapeDtypeStruct((8, width), F32)]
        )
        self.out_specs = [VMEM] + [ANYWHERE] * 3 + [VMEM]
        ring = [pltpu.SemaphoreType.DMA] + ring_sems(count)
        groups = [
            [pltpu.VMEM((3, own_heads, self.rows, self.dim), F32)],
            [pltpu.VMEM((self.rows, 128), F32), pltpu.VMEM((8, self.rows), F32)],
            [pltpu.VMEM((self.rows, self.main + 128), BF16)],
            [pltpu.VMEM((count, tall, width), BF16)] + ring,
            [
                pltpu.VMEM((count, tall, width), BF16),
                pltpu.VMEM((2, count // 2, tall, width), BF16),
                pltpu.VMEM((tall, width), F32),
            ]
            + ring_sems(count),
            [pltpu.VMEM((width, both), BF16), pltpu.VMEM((shard_rows, both), BF16)]
            + shard_sum_scratch(shard_rows, both),
            ring,
            ring,
            ring,
            [pltpu.VMEM((8, width), F32)] + small_sum_scratch((8, width)),
        ]
        self.sizes = [len(group) for group in groups]
        self.scratch = sum(groups, [])

    def run(self, ring, ins, outs, scratch):
        groups, at = [], 0
        for size in self.sizes:
            groups.append(scratch[at : at + size])
            at += size
        named = dict(zip(self.names, ins[5:]))
        gated_all, *gated_sems = groups[3]
        rows_part, rows_held, rows_sum, *rows_sems = groups[4]
        grad_mixed = groups[2][0]
        grads_part, grads_sum, *grads_rest = groups[5]
        small, *small_rest = groups[9]
        count, tall, width = gated_all.shape

        def main():
            yield from together(
                self.attention(ins, named, *groups[0], *groups[1]),
                ring_gather(ring, named["gated"], gated_all, *gated_sems, True),
            )
            self.join(named, *groups[0], *groups[1], grad_mixed, small)
            block = 256 if width % 256 == 0 else width

            @pl.loop(0, width // block)
            def _(index):
                columns = pl.ds(pl.multiple_of(index * block, block), block)
                part = matmul_rows(grad_mixed[...], named["mixed_in"][columns])
                rows_part[:, :, columns] = part.astype(BF16).reshape(count, tall, block)

            yield from together(
                ring_sum(ring, rows_part, rows_held, rows_sum, *rows_sems, True),
                weights(),
            )

        def weights():
            yield from idle(RING_PIECES)
            self.weight_grads(named, gated_all, grad_mixed, grads_part)
            yield from shard_sum(ring, grads_part, grads_sum, *grads_rest)

        yield from together(
            main(),
            slow(ring_gather(ring, named["grad_ffn_in"], outs[1], *groups[6], True), 2),
            slow(ring_gather(ring, named["grad_ffn_out"], outs[2], *groups[7], True), 2),
        )
        self.norm_back(named, rows_sum, outs[0], small)
        yield from together(
            ring_gather(ring, grads_sum, outs[3], *groups[8], True),
            small_sum(ring, small, outs[4], *small_rest),
        )

    def attention(self, ins, named, grads, sums_rows, sums_columns):
        log_totals, grad_attn = named["log_totals"], named["grad_attn"]
        grad_q, grad_k, grad_v = [grads.at[i] for i in range(3)]
        blocks = self.rows // self.tall
        sums_columns[...] = jnp.zeros_like(sums_columns)
        pad = jnp.zeros((self.tall, 128 - self.heads), F32)
        for index in reversed(range(blocks)):
            rows, wide = self.block(index)
            allowed = self.allowed(rows, wide, *ins[3:5])
            own = slice(0, wide)
            row_sums = []
            for head in range(self.heads):
                queries, keys, scores = self.scores(ins, head, rows, wide, allowed)
                probabilities = jnp.exp(scores - log_totals[rows, head : head + 1])
                grad_part = grad_attn[rows, head * self.dim : (head + 1) * self.dim]
                grad_probs = matmul_rows(grad_part, self.part(ins[0], 2, head, own))
                row_inner = jnp.sum(probabilities * grad_probs, axis=1, keepdims=True)
                grad_scores = (probabilities * (grad_probs - row_inner)).astype(BF16)
                grad_q[head, rows] = matmul(grad_scores, keys) * self.scaling
                from_k = weight_grad(grad_scores, queries) * self.scaling
                from_v = weight_grad(probabilities.astype(BF16), grad_part)
                wide_sums = grad_scores.astype(F32)
                row_sums.append(jnp.sum(wide_sums, axis=1, keepdims=True))
                column_sums = jnp.sum(wide_sums, axis=0, keepdims=True)
                if index == blocks - 1:
                    grad_k[head], grad_v[head] = from_k, from_v
                    sums_columns[head : head + 1] = column_sums
                else:
                    grad_k[head, own] += from_k
                    grad_v[head, own] += from_v
                    sums_columns[head : head + 1, own] += column_sums
            sums_rows[rows] = jnp.concatenate(row_sums + [pad], axis=1)
            yield

    def join(self, named, grads, sums_rows, sums_columns, grad_mixed, small):
        for index in range(self.rows // self.tall):
            rows, _ = self.block(index)
            grad_mixed[rows, : self.main] = jnp.concatenate(
                [grads[i, head, rows].astype(BF16) for i in range(3) for head in range(self.heads)]
                + [named["grad_gatelog"][rows]],
                axis=1,
            )
        tall = 128
        here = lax.broadcasted_iota(jnp.int32, (tall, tall), 0)
        there = lax.broadcasted_iota(jnp.int32, (tall, tall), 1)
        wedge = (here <= there).astype(F32)
        later, bias = jnp.zeros((1, 8), F32), jnp.zeros((1, 8), F32)
        exact = dict(preferred_element_type=F32, precision=lax.Precision.HIGHEST)
        pad = jnp.zeros((tall, 120), BF16)
        for index in reversed(range(self.rows // tall)):
            rows = slice(index * tall, (index + 1) * tall)
            inside = jnp.dot(wedge, sums_rows[rows], **exact)[:, :8] - lax.dot_general(
                wedge, sums_columns[:, rows], (((1,), (1,)), ((), ())), **exact
            )
            logits = named["forget_logits"][rows]
            grad_logits = ((inside + later) * jax.nn.sigmoid(-logits)).astype(BF16)
            later = later + inside[:1]
            bias = bias + jnp.sum(grad_logits.astype(F32), axis=0, keepdims=True)
            grad_mixed[rows, self.main :] = jnp.concatenate([grad_logits, pad], axis=1)
        small[...] = named["small"][...]
        small[2:3] = sum(
            bias[:, head : head + 1] * named["places"][head : head + 1]
            for head in range(self.heads)
        )

    def weight_grads(self, named, gated_all, grad_mixed, parts):
        count, tall, width = gated_all.shape
        tile = 128
        hidden = named["grad_branch"].shape[1]
        tail = parts.shape[1] - self.main

        @pl.loop(0, width // tile)
        def _(index):
            columns = pl.ds(pl.multiple_of(index * tile, tile), tile)
            normed = named["normed"][:, :, columns].reshape(count * tall, tile)
            gated = gated_all[:, :, columns].reshape(count * tall, tile)
            parts[columns, : self.main] = weight_grad(normed, grad_mixed[:, : self.main]).astype(BF16)
            forget = weight_grad(normed, grad_mixed[:, self.main :])
            out = weight_grad(gated, named["grad_branch"][...])
            parts[columns, self.main :] = jnp.concatenate(
                [out, forget[:, : tail - hidden]], axis=1
            ).astype(BF16)

    def norm_back(self, named, rows_sum, grad_tokens, small):
        grad, normed = rows_sum[...], named["normed_one"][...]
        small[0:1] = jnp.sum(grad * normed, axis=0, keepdims=True)
        grad_normed = grad * named["gain_one"][...]
        inner = jnp.mean(grad_normed * normed, axis=1, keepdims=True)
        grad_tokens[...] = named["grad_middle"][...] + named["rstat_one"][...] * (
            grad_normed - normed * inner
        )


def running_sum(values):
    tall = 128 if values.shape[0] % 128 == 0 else values.shape[0]
    blocks = values.reshape(-1, tall, values.shape[1])
    wedge = jnp.tril(jnp.ones((tall, tall), F32))
    inside = jnp.einsum("st,btk->bsk", wedge, blocks, precision=lax.Precision.HIGHEST)
    totals = jnp.sum(blocks, axis=1)
    before = jnp.tril(jnp.ones((totals.shape[0],) * 2, F32), -1)
    before = jnp.sum(before[:, :, None] * totals[None], axis=1)
    return (inside + before[:, None]).reshape(values.shape)


def exchange(ident, name, *tasks):
    count = lax.axis_size("ctx")

    def take(refs, sizes):
        groups, at = [], 0
        for size in sizes:
            groups.append(refs[at : at + size])
            at += size
        return groups

    ins = [len(task.ins) for task in tasks]
    outs = [len(task.outs) for task in tasks]
    scratch = [len(task.scratch) for task in tasks]

    def kernel(*refs):
        ring = Ring(count)
        kinds = sum([task.kinds for task in tasks], ())
        peers = []
        if "all" in kinds:
            peers = sum(all_peers(ring), [])
        else:
            if "ring" in kinds:
                peers += [ring.device(1), ring.device(-1)]
            if "shard" in kinds:
                pair, others = shard_pair(ring, lax.axis_size("fsdp"))
                peers += [(ring.ctx, to) for to in [pair] + others]
        greet(peers)
        groups = [
            take(refs[: sum(ins)], ins),
            take(refs[sum(ins) : sum(ins) + sum(outs)], outs),
            take(refs[sum(ins) + sum(outs) :], scratch),
        ]
        for _ in together(*[task.run(ring, *parts) for task, *parts in zip(tasks, *groups)]):
            pass

    results = pl.pallas_call(
        kernel,
        out_shape=sum([task.outs for task in tasks], []),
        in_specs=sum([task.in_specs for task in tasks], []),
        out_specs=sum([task.out_specs for task in tasks], []),
        scratch_shapes=sum([task.scratch for task in tasks], []),
        compiler_params=pltpu.CompilerParams(
            collective_id=ident, has_side_effects=True, vmem_limit_bytes=58 * 2**20
        ),
        cost_estimate=pl.CostEstimate(flops=0, bytes_accessed=100_000_000, transcendentals=0),
        name=name,
    )(*sum([task.ins for task in tasks], []))
    return take(list(results), outs)


def flat(blocks):
    return blocks.reshape(-1, blocks.shape[-1])


def ffn_columns(blocks, n_fsdp):
    count, rows, both = blocks.shape
    width, piece = both // 2, both // 2 // n_fsdp
    steps = 4
    tall = rows // steps

    def kernel(block_ref, *outs):
        for j in range(count):
            for half in range(2):
                for group in range(n_fsdp):
                    start, to = half * width + group * piece, (group * count + j) * piece
                    outs[half][:, to : to + piece] = block_ref[j, :, start : start + piece].astype(F32)

    wide = jax.ShapeDtypeStruct((rows, width * count), F32)
    spec = pl.BlockSpec((tall, width * count), lambda i: (i, 0))
    return pl.pallas_call(
        kernel,
        out_shape=(wide, wide),
        grid=(steps,),
        in_specs=[pl.BlockSpec((count, tall, both), lambda i: (0, i, 0))],
        out_specs=(spec, spec),
        compiler_params=pltpu.CompilerParams(vmem_limit_bytes=40 * 2**20),
        cost_estimate=pl.CostEstimate(
            flops=0, bytes_accessed=rows * both * count * 6, transcendentals=0
        ),
        name="ffn_columns",
    )(blocks)


def head_columns(blocks, sizes, widths):
    count, rows, total = blocks.shape
    steps = 4
    tall = rows // steps
    starts = [sum(sizes[:i]) for i in range(len(sizes))]

    def kernel(block_ref, *outs):
        for start, size, out in zip(starts, sizes, outs):
            for i in range(0, count, 2):
                pair = jnp.concatenate(
                    [block_ref[i + k][:, start : start + size].astype(F32) for k in range(2)], axis=1
                )
                at = i * size
                keep = min(2 * size, out.shape[1] - at)
                if keep > 0:
                    out[:, at : at + keep] = pair[:, :keep]

    return pl.pallas_call(
        kernel,
        out_shape=tuple(jax.ShapeDtypeStruct((rows, w), F32) for w in widths),
        grid=(steps,),
        in_specs=[pl.BlockSpec((count, tall, total), lambda i: (0, i, 0))],
        out_specs=tuple(pl.BlockSpec((tall, w), lambda i: (i, 0)) for w in widths),
        compiler_params=pltpu.CompilerParams(vmem_limit_bytes=40 * 2**20),
        cost_estimate=pl.CostEstimate(
            flops=0, bytes_accessed=count * rows * total * 6, transcendentals=0
        ),
        name="head_columns",
    )(blocks)


def rows_to_columns(value):
    return lax.all_to_all(value, "ctx", split_axis=1, concat_axis=0, tiled=True)


def columns_to_rows(value):
    return lax.all_to_all(value, "ctx", split_axis=0, concat_axis=1, tiled=True)


def shards(
    tokens,
    segments,
    gain_attn,
    w_query,
    w_key,
    w_value,
    w_forget,
    forget_bias,
    w_outgate,
    w_out,
    gain_ffn,
    w_gate,
    w_up,
    w_down,
    cotangent,
):
    n_ctx, me = lax.axis_size("ctx"), lax.axis_index("ctx")
    n_fsdp = lax.axis_size("fsdp")
    tok_rows, width = tokens.shape[1:]
    seq_rows = tok_rows * n_ctx
    n_heads = forget_bias.shape[0]
    head_dim = width // n_heads
    own_heads = -(-n_heads // n_ctx)
    own_width = own_heads * head_dim
    padded = own_width * n_ctx
    ffn_rows = w_down.shape[0]
    ffn_piece = ffn_rows // n_ctx
    ffn_width = ffn_piece * n_fsdp
    shard_rows = w_query.shape[0]

    def widen(value, size):
        return jnp.pad(value, ((0, 0), (0, size - value.shape[1])))

    def own_columns(weight, size):
        return lax.dynamic_slice_in_dim(widen(weight, size * n_ctx), me * size, size, 1)

    def own_ffn(weight):
        return [
            lax.dynamic_slice_in_dim(weight, (group * n_ctx + me) * ffn_piece, ffn_piece, 1)
            for group in range(n_fsdp)
        ]

    mixed_shard = jnp.concatenate(
        [own_columns(w, own_width) for w in (w_query, w_key, w_value, w_outgate)]
        + [widen(own_columns(w_forget, own_heads), 128)],
        axis=1,
    )
    bias_own = lax.dynamic_slice_in_dim(
        jnp.pad(forget_bias, (0, own_heads * n_ctx - n_heads)), me * own_heads, own_heads, 0
    )
    bias_own = jnp.pad(bias_own, (0, 8 - own_heads))

    seg = segments[0]
    inputs = tokens[0].astype(F32)
    gain_one = gain_attn.astype(F32)
    normed_one, rstat_one = rms_stats(inputs)
    (normed,), (mixed_in,) = exchange(
        0,
        "gather_start",
        RingGather((normed_one * gain_one).astype(BF16), absolute=True),
        ShardGather(mixed_shard),
    )
    normed_rows = flat(normed)
    normed_rows, out_shard = lax.optimization_barrier((normed_rows, w_out))
    full_out = lax.all_gather(out_shard, "fsdp", axis=0, tiled=True)

    split = [own_width * i for i in range(5)]
    qkv = matmul(normed_rows, mixed_in[:, : split[3]]).astype(BF16)
    mixed = matmul(normed_rows, mixed_in[:, split[3] :])
    gate_value = jax.nn.sigmoid(mixed[:, :own_width])
    forget_logits = mixed[:, own_width : own_width + 8] + bias_own
    decay = running_sum(jax.nn.log_sigmoid(forget_logits))

    (grad_out_low,), (attended, log_totals) = exchange(
        5,
        "attend",
        RingGather(cotangent[0]),
        AttentionForward(qkv, decay, seg, own_heads),
    )
    gated = columns_to_rows((attended * gate_value).astype(BF16))[:, :width]

    middle = inputs + matmul(gated, full_out)
    gain_two = gain_ffn.astype(F32)
    normed_two_f, rstat_two = rms_stats(middle)
    w_in = [w_gate, w_up]
    if ffn_piece % 128 != 0:
        w_in = [jnp.concatenate(own_ffn(w_gate) + own_ffn(w_up), axis=1)]
    ((out_sum, grad_normed_two, grad_ffn_in, grad_ffn_out),) = exchange(
        1,
        "ffn",
        Ffn((normed_two_f * gain_two).astype(BF16), grad_out_low, w_in, w_down, ffn_piece),
    )
    output = middle + out_sum
    back_two, grad_gain_two = norm_back(grad_normed_two, normed_two_f, rstat_two, gain_two)
    grad_middle = cotangent[0].astype(F32) + back_two

    grad_branch_low = grad_middle.astype(BF16)
    grad_gated = matmul_rows(grad_branch_low, full_out).astype(BF16)
    grad_gated = rows_to_columns(widen(grad_gated, padded)).astype(F32)
    grad_branch_own = rows_to_columns(widen(grad_branch_low, padded))
    grad_attn_low = (grad_gated * gate_value).astype(BF16)
    grad_gatelog_low = (grad_gated * attended * (gate_value * (1.0 - gate_value))).astype(BF16)

    spots = jnp.arange(own_heads, dtype=jnp.int32)[:, None] + me * own_heads
    places = (spots == jnp.arange(width, dtype=jnp.int32)[None, :]).astype(F32)
    ((grad_inputs, spread_ffn_in, spread_ffn_out, spread_attn, small),) = exchange(
        2,
        "backward",
        Backward(
            qkv,
            decay,
            seg,
            own_heads,
            {
                "log_totals": log_totals,
                "grad_attn": grad_attn_low,
                "grad_gatelog": grad_gatelog_low,
                "forget_logits": forget_logits,
                "grad_branch": grad_branch_own,
                "gated": gated,
                "grad_ffn_in": grad_ffn_in,
                "grad_ffn_out": grad_ffn_out,
                "normed": normed,
                "mixed_in": mixed_in,
                "normed_one": normed_one,
                "rstat_one": rstat_one,
                "gain_one": gain_one[None],
                "grad_middle": grad_middle,
                "places": places,
                "small": jnp.pad(grad_gain_two[None], ((1, 6), (0, 0))),
            },
        ),
    )
    sizes = [own_width] * 5 + [own_heads]
    if ffn_piece % 128 == 0:
        grad_gate, grad_up = ffn_columns(spread_ffn_in, n_fsdp)
    else:
        whole = spread_ffn_in.reshape(n_ctx, shard_rows, 2, n_fsdp, ffn_piece)
        whole = jnp.transpose(whole, (2, 1, 3, 0, 4)).reshape(2, shard_rows, -1).astype(F32)
        grad_gate, grad_up = whole[0], whole[1]
    grad_weights = head_columns(spread_attn, sizes, [width] * 5 + [n_heads])
    return (
        output.astype(BF16)[None],
        grad_inputs[None],
        small[0],
        grad_weights[0],
        grad_weights[1],
        grad_weights[2],
        grad_weights[5],
        small[2, :n_heads],
        grad_weights[3],
        grad_weights[4],
        small[1],
        grad_gate,
        grad_up,
        spread_ffn_out.reshape(ffn_rows, width).astype(F32),
    )


def solution(mesh):
    rows, blocks = P("fsdp", None), P("fsdp", "ctx", None)
    return jax.shard_map(
        shards,
        mesh=mesh,
        in_specs=(blocks, rows, P())
        + (rows,) * 4
        + (P(), rows, rows, P(), rows, rows, rows, blocks),
        out_specs=(blocks, blocks, P())
        + (rows,) * 4
        + (P(), rows, rows, P(), rows, rows, rows),
        check_vma=False,
    )
```

time: 613 us -> 545 us (0.89)
  matrix products: 54.3 us -> 18.5 us
  Pallas kernels: 443 us -> 421 us
  local copies, waits for them, and re-layouts: 44.5 us -> 26 us
  waiting for transfers between devices: 11.3 us -> 21.8 us
    pallas_call x7 -> x4, Pallas kernels: 431 us -> 409 us  [exchange(): pl.pallas_call(kernel, out_shape=sum([task.outs for task in tasks], []),...]
    dot_general x4 -> x0, matrix products: 17.1 us -> none  [weight_grad(): lax.dot_general(left, right, (((0,), (0,)), ((), ())), preferred_element_...]
    dot_general x4 -> x1, matrix products: 13.9 us -> 3.37 us  [matmul_rows(): lax.dot_general(left, right, (((1,), (1,)), ((), ())), preferred_element_...]
    unnamed x135 -> x35, local copies, waits for them, and re-layouts: 17.1 us -> 7.42 us
    dot_general x5 -> x3, matrix products: 22.8 us -> 14.2 us  [matmul(): return jnp.dot(left, right, preferred_element_type=F32)]
    all_to_all x2, waiting for transfers between devices: 4.11 us -> 11.8 us  [rows_to_columns(): return lax.all_to_all(value, 'ctx', split_axis=1, concat_axis=0, tiled=True)]
  transfers between devices with their start and end apart: 4 -> 4, of which waited for: 2 -> 3; matrix products, arithmetic and copies ran while one was open for 8% -> 5% of each run, Pallas kernels for 32% -> 7%
where the time goes in v3:
time: 545 us; the launch traced here: 535 us
  Pallas kernels  421 us (77%)
  local copies, waits for them, and re-layouts  26 us (5%)
  waiting for transfers between devices  21.8 us (4%)
  other arithmetic  19.8 us (4%)
  matrix products  18.5 us (3%)
  between operations  14.5 us (3%)
  starting transfers between devices  12.9 us (2%)
    pallas_call x4, Pallas kernels, exchange(): pl.pallas_call(kernel, out_shape=sum([task.outs for task in tasks], []),...  409 us
    dot_general x3, matrix products, matmul(): return jnp.dot(left, right, preferred_element_type=F32)  14.2 us
    all_to_all x2, waiting for transfers between devices, rows_to_columns(): return lax.all_to_all(value, 'ctx', split_axis=1, concat_axis=0, tiled=True)  11.8 us
  transfers between devices with their start and end apart: 4, of which 3 were waited for; matrix products, arithmetic and copies ran while one was open for 5% of the time, Pallas kernels for 7%

profile of v3, /device:TPU:0, one launch (start us, length us, event | category | flops | bytes accessed | tf_op | source)
XLA Modules:
  0.0 534.5 jit_solution(8379040860175232375)
XLA Ops:
  9.3 2.2 convert_multiply_fusion
  11.5 1.2 constant_dynamic-slice_fusion.3
  12.7 1.2 constant_dynamic-slice_fusion.1
  15.2 37.6 %gather_start.1 = (bf16[8,128,1536]{2,1,0:T(8,128)(2,1)}, bf16[1536,896]{1,0:T(8,128)(2,1)}) custom-call(bf16[128,1536]{1,0:T(8,128)(2,1)} %get-tuple-element.131.refs_0_, bf16[384,896]{1,0:T(8,128)(2,1)} %concatenate.3.refs_1_), custom_call_target="tpu_custom_call" | custom-call | bytes 100000000 | tf_op jit(solution)/shard_map/gather_start/pallas_call | solution.py:826
  52.9 4.1 fusion.5
  57.0 1.3 bitcast_reduce_fusion
  61.5 6.9 %fusion.2.refs_1_.refs_0_ = bf16[1024,576]{1,0:T(8,128)(2,1)} fusion(bf16[1024,1536]{1,0:T(8,128)(2,1)} %bitcast.61, bf16[1536,896]{1,0:T(8,128)(2,1)} %get-tuple-element.40.refs_14_), kind=kOutput, calls=%fused_computation.5 | convolution fusion | flops 1812529152 | bytes 6291456 | tf_op jit(solution)/shard_map/dot_general | solution.py:14
  68.3 37.6 %attend.1 = (bf16[8,128,1536]{2,1,0:T(8,128)(2,1)}, f32[1024,192]{1,0:T(8,128)}, f32[1024,3]{1,0:T(8,128)}) custom-call(bf16[128,1536]{1,0:T(8,128)(2,1)} %bitcast.65, bf16[1024,576]{1,0:T(8,128)(2,1)} %fusion.2.refs_1_.refs_0_, f32[1024,8]{1,0:T(8,128)} %copy.80.refs_2_.refs_1_, f32[8,1024]{1,0:T(8,128)} %bitcast.68, s32[1024,1]{1,0:T(8,128)} %copy.81.refs_4_.refs_3_, ...), custom_call_target="tpu_custom_call" | custom-call | bytes 100000000 | tf_op jit(solution)/shard_map/attend/pallas_call | solution.py:826
  105.9 1.9 multiply_convert_fusion
  108.8 4.3 all-to-all-start
  113.1 10.1 %all-to-all-done = bf16[8,128,192]{1,2,0:T(8,128)(2,1)S(1)} async-done(((bf16[8,128,192]{1,2,0:T(8,128)(2,1)}), bf16[8,128,192]{1,2,0:T(8,128)(2,1)S(1)}, u32[]{:S(2)}, u32[]{:S(2)}) %all-to-all-start) | async-done | bytes 393248 | tf_op jit(solution)/shard_map/all_to_all | solution.py:910
  123.1 3.2 multiply_reduce_fusion.2
  127.3 102.7 %ffn.1 = (f32[128,1536]{1,0:T(8,128)}, f32[128,1536]{1,0:T(8,128)}, bf16[384,1024]{1,0:T(8,128)(2,1)}, bf16[128,1536]{1,0:T(8,128)(2,1)}) custom-call(bf16[128,1536]{1,0:T(8,128)(2,1)} %multiply_convert_fusion.1.refs_0_, bf16[8,128,1536]{2,1,0:T(8,128)(2,1)} %get-tuple-element.43.refs_1_, bf16[1024,1536]{1,0:T(8,128)(2,1)} %refs_2_.1, ...), custom_call_target="tpu_custom_call" | custom-call | bytes 100000000 | tf_op jit(solution)/shard_map/ffn/pallas_call | solution.py:826
  230.0 1.5 multiply_reduce_fusion
  231.4 3.0 fusion.25
  234.4 3.4 convolution_convert_fusion
  237.8 1.9 copy.84
  239.7 4.3 all-to-all-start.1
  244.0 2.0 copy.86
  246.0 8.1 %all-to-all-done.1 = bf16[128,8,192]{0,2,1:T(8,128)(2,1)S(1)} async-done(((bf16[128,8,192]{0,2,1:T(8,128)(2,1)}), bf16[128,8,192]{0,2,1:T(8,128)(2,1)S(1)}, u32[]{:S(2)}, u32[]{:S(2)}) %all-to-all-start.1) | async-done | bytes 393248 | tf_op jit(solution)/shard_map/all_to_all | solution.py:906
  254.1 4.3 all-to-all-start.2
  262.4 2.6 fusion.8
  265.0 3.7 all-to-all-done.2
  268.7 2.0 copy.87
  270.7 231.0 %backward.1 = (f32[128,1536]{1,0:T(8,128)}, bf16[8,384,1024]{2,1,0:T(8,128)(2,1)}, bf16[8,128,1536]{2,1,0:T(8,128)(2,1)}, bf16[8,384,1024]{2,1,0:T(8,128)(2,1)}, f32[8,1536]{1,0:T(8,128)}) custom-call(bf16[1024,576]{1,0:T(8,128)(2,1)} %fusion.2.refs_1_.refs_0_, f32[1024,8]{1,0:T(8,128)} %copy.80.refs_2_.refs_1_, f32[8,1024]{1,0:T(8,128)} %bitcast.69, ...), custom_call_target="tpu_custom_call" | custom-call | bytes 100000000 | tf_op jit(solution)/shard_map/backward/pallas_call | solution.py:826
  501.7 1.5 slice_reduce_fusion
  503.2 1.2 slice_bitcast_fusion
  504.4 2.8 copy-done.3
  507.2 6.8 %head_columns.1 = (f32[384,1536]{1,0:T(8,128)}, f32[384,1536]{1,0:T(8,128)}, f32[384,1536]{1,0:T(8,128)}, f32[384,1536]{1,0:T(8,128)}, f32[384,1536]{1,0:T(8,128)}, /*index=5*/f32[384,24]{1,0:T(8,128)S(1)}) custom-call(bf16[8,384,1024]{2,1,0:T(8,128)(2,1)S(1)} %copy-done.3), custom_call_target="tpu_custom_call" | custom-call | bytes 18874368 | tf_op jit(solution)/shard_map/head_columns/pallas_call | solution.py:891
  514.7 2.8 copy-done.2
  517.4 5.3 ffn_columns.1
  522.8 3.8 bitcast_convert_fusion
  (65 shorter events, 14.0 us)
Async XLA Ops:
  7.2 1.9 copy-start
  7.2 115.9 %all-gather.2.cloned.1.call-start = ((), (), s32[]{:S(2)}) async-start(), calls=%async_computation.3 | async-start | bytes 5898240 | tf_op jit(solution)/shard_map/all_gather | solution.py:978
  11.5 41.3 %copy-start.13 = (f32[24]{0:T(128)S(1)}, f32[24]{0:T(128)}, u32[]{:S(2)}) copy-start(f32[24]{0:T(128)} %param.22) | copy-start | bytes 292
  52.9 7.6 %copy-start.10 = (s32[1,1024]{1,0:T(1,128)S(1)}, s32[1,1024]{1,0:T(1,128)}, u32[]{:S(2)}) copy-start(s32[1,1024]{1,0:T(1,128)} %refs_4_.3) | copy-start | bytes 12292
  57.0 48.9 %copy-start.4 = (f32[1024,320]{1,0:T(8,128)}, f32[1024,320]{1,0:T(8,128)S(1)}, u32[]{:S(2)}) copy-start(f32[1024,320]{1,0:T(8,128)S(1)} %fusion.5) | copy-start | bytes 3932164
  59.4 8.9 %copy-start.9 = (f32[8,8,128]{2,1,0:T(8,128)}, f32[8,8,128]{2,1,0:T(8,128)S(1)}, u32[]{:S(2)}) copy-start(f32[8,8,128]{2,1,0:T(8,128)S(1)} %convolution_add_fusion.1) | copy-start | bytes 98308
  105.9 7.2 %copy-start.12 = (bf16[1536]{0:T(1024)(128)(2,1)S(1)}, bf16[1536]{0:T(1024)(128)(2,1)}, u32[]{:S(2)}) copy-start(bf16[1536]{0:T(1024)(128)(2,1)} %param.25) | copy-start | bytes 9220
  105.9 17.2 %copy-start.6 = (bf16[1,128,1536]{2,1,0:T(8,128)(2,1)S(1)}, bf16[1,128,1536]{2,1,0:T(8,128)(2,1)}, u32[]{:S(2)}) copy-start(bf16[1,128,1536]{2,1,0:T(8,128)(2,1)} %param.15) | copy-start | bytes 1179652
  108.8 14.4 %all-to-all-start = ((bf16[8,128,192]{1,2,0:T(8,128)(2,1)}), bf16[8,128,192]{1,2,0:T(8,128)(2,1)S(1)}, u32[]{:S(2)}, u32[]{:S(2)}) async-start(bf16[8,128,192]{1,2,0:T(8,128)(2,1)} %copy.83), calls=%async_computation | async-start | bytes 786432 | tf_op jit(solution)/shard_map/all_to_all | solution.py:910
  127.3 107.1 %slice-start = ((s8[4718592]{0:T(1024)(128)(4,1)}), s8[4194304]{0:T(1024)(128)(4,1)S(1)}, s32[]{:S(2)}) async-start(s8[4718592]{0:T(1024)(128)(4,1)} %bitcast.56), calls=%async_computation.4 | async-start | bytes 8388608
  127.3 107.1 %slice-start.1 = ((s8[4718592]{0:T(1024)(128)(4,1)}), s8[524288]{0:T(1024)(128)(4,1)S(1)}, s32[]{:S(2)}) async-start(s8[4718592]{0:T(1024)(128)(4,1)} %bitcast.56), calls=%async_computation.5 | async-start | bytes 1048576
  237.8 21.3 %copy-start.11 = (bf16[1536]{0:T(1024)(128)(2,1)S(1)}, bf16[1536]{0:T(1024)(128)(2,1)}, u32[]{:S(2)}) copy-start(bf16[1536]{0:T(1024)(128)(2,1)} %param.17) | copy-start | bytes 9220
  239.7 14.4 %all-to-all-start.1 = ((bf16[128,8,192]{0,2,1:T(8,128)(2,1)}), bf16[128,8,192]{0,2,1:T(8,128)(2,1)S(1)}, u32[]{:S(2)}, u32[]{:S(2)}) async-start(bf16[128,8,192]{0,2,1:T(8,128)(2,1)} %bitcast.16), calls=%async_computation.1 | async-start | bytes 786432 | tf_op jit(solution)/shard_map/all_to_all | solution.py:906
  244.0 18.4 %copy-start.5 = (f32[1024,320]{1,0:T(8,128)S(1)}, f32[1024,320]{1,0:T(8,128)}, u32[]{:S(2)}) copy-start(f32[1024,320]{1,0:T(8,128)} %copy-done.4) | copy-start | bytes 3932164
  254.1 14.6 %all-to-all-start.2 = ((bf16[128,8,192]{0,2,1:T(8,128)(2,1)}), bf16[128,8,192]{0,2,1:T(8,128)(2,1)}, u32[]{:S(2)}, u32[]{:S(2)}) async-start(bf16[128,8,192]{0,2,1:T(8,128)(2,1)} %bitcast.19), calls=%async_computation.2 | async-start | bytes 786432 | tf_op jit(solution)/shard_map/all_to_all | solution.py:906
  504.4 2.8 copy-start.3
  514.6 2.8 copy-start.2
  517.4 5.3 copy-start.7
  522.8 3.8 copy-start.8
  522.8 4.7 copy-start.1
Sparse Core Ops, SparseCore 0:
  52.9 37.6 all-gather.1

commit v4 on v3

--- a/solution.py
+++ b/solution.py
@@ -25,15 +25,6 @@
 def rms_stats(values):
     rstat = lax.rsqrt(jnp.mean(values * values, axis=-1, keepdims=True) + EPSILON)
     return (values * rstat, rstat)
-
-
-def norm_back(grad_in, normed, rstat, gain):
-    grad_normed = grad_in * gain
-    grad_gain = jnp.sum(grad_in * normed, axis=0)
-    grad_values = rstat * (
-        grad_normed - normed * jnp.mean(grad_normed * normed, axis=-1, keepdims=True)
-    )
-    return (grad_values, grad_gain)
 
 
 MESH = pl.DeviceIdType.MESH
@@ -186,23 +177,6 @@
 ANYWHERE, VMEM = pl.BlockSpec(memory_space=pl.ANY), pl.BlockSpec(memory_space=pltpu.VMEM)
 
 
-class RingGather:
-    kinds = ("ring",)
-
-    def __init__(self, value, absolute=False):
-        self.absolute = absolute
-        count = lax.axis_size("ctx")
-        self.ins, self.in_specs = [value], [ANYWHERE]
-        self.outs, self.out_specs = (
-            [jax.ShapeDtypeStruct((count,) + value.shape, value.dtype)],
-            [ANYWHERE],
-        )
-        self.scratch = [pltpu.SemaphoreType.DMA] + ring_sems(count)
-
-    def run(self, ring, ins, outs, scratch):
-        return ring_gather(ring, ins[0], outs[0], *scratch, absolute=self.absolute)
-
-
 def shard_pair(ring, shards):
     me = ring.fsdp
     pair = me + 1 - 2 * (me % 2)
@@ -276,22 +250,6 @@
     return sems(parts, shards - 1, shards - 1)
 
 
-class ShardGather:
-    kinds = ("shard",)
-
-    def __init__(self, shard):
-        shards = lax.axis_size("fsdp")
-        self.ins, self.in_specs = [shard], [ANYWHERE]
-        self.outs = [jax.ShapeDtypeStruct((shards * shard.shape[0], shard.shape[1]), BF16)]
-        self.out_specs, self.scratch = [ANYWHERE], shard_gather_sems(1)
-
-    def run(self, ring, ins, outs, scratch):
-        def fill(shard, local_sem):
-            return [pltpu.make_async_copy(ins[0], shard, local_sem.at[0])], ins[0]
-
-        return shard_gather(ring, fill, outs[0], *scratch)
-
-
 def shard_sum(ring, parts, total, near, far, near_send, near_recv, far_send, far_recv):
     shards, me = lax.axis_size("fsdp"), ring.fsdp
     half, core, chip = shards // 2, me % 2, me // 2
@@ -350,22 +308,24 @@
 class Ffn:
     kinds = ("ring", "shard")
 
-    def __init__(self, normed, grad_out, w_in, w_out, piece):
+    def __init__(self, tokens, gated, full_out, gain, grad_out, w_in, w_out, piece):
         count, shards = lax.axis_size("ctx"), lax.axis_size("fsdp")
-        rows, width = normed.shape
+        rows, width = tokens.shape
         self.aligned = len(w_in) == 2
         self.piece, self.inner = piece, piece * shards
         inner, both = self.inner, 2 * self.inner
         shard_rows = width // shards
-        self.ins = [normed, grad_out, w_out] + list(w_in)
-        self.in_specs = [ANYWHERE, VMEM] + [ANYWHERE] * (1 + len(w_in))
+        self.ins = [grad_out, tokens, gated, full_out, gain, w_out] + list(w_in)
+        self.in_specs = [VMEM] * 5 + [ANYWHERE] * (1 + len(w_in))
         self.outs = [
+            jax.ShapeDtypeStruct((rows, width), BF16),
             jax.ShapeDtypeStruct((rows, width), F32),
             jax.ShapeDtypeStruct((rows, width), F32),
+            jax.ShapeDtypeStruct((rows, 1), F32),
             jax.ShapeDtypeStruct((shard_rows, both), BF16),
             jax.ShapeDtypeStruct((piece, width), BF16),
         ]
-        self.out_specs = [VMEM] * 4
+        self.out_specs = [VMEM] * 6
         held = pltpu.VMEM((2, count // 2, rows, width), BF16)
         groups = [
             [pltpu.VMEM((count, rows, width), BF16), pltpu.SemaphoreType.DMA] + ring_sems(count),
@@ -376,27 +336,31 @@
             [pltpu.VMEM((count, rows, width), BF16), held] + ring_sems(count),
             [pltpu.VMEM((width, both), BF16)] + shard_sum_scratch(shard_rows, both),
             [pltpu.VMEM((inner, width), BF16)] + shard_sum_scratch(piece, width),
+            [
+                pltpu.VMEM((rows, width), F32),
+                pltpu.VMEM((rows, width), BF16),
+                pltpu.VMEM((rows, width), F32),
+            ],
         ]
         self.sizes = [len(group) for group in groups]
         self.scratch = sum(groups, [])
 
     def run(self, ring, ins, outs, scratch):
-        normed, grad_out, w_out_rows = ins[:3]
+        grad_out, tokens, gated, full_out, gain, w_out_rows = ins[:6]
+        w_in_rows = ins[6:]
         inner, piece = self.inner, self.piece
-        groups, at = [], 0
-        for size in self.sizes:
-            groups.append(scratch[at : at + size])
-            at += size
+        groups = split_refs(scratch, self.sizes)
         (rows_all, *rows_sems), (w_in, *w_in_sems), (w_out, *w_out_sems) = groups[:3]
         hidden, grad_mid = groups[3]
         (out_part, out_held, *out_sems), (in_part, in_held, *in_sems) = groups[4:6]
-        (grad_w_in, *grad_in_rest), (grad_w_out, *grad_out_rest) = groups[6:]
+        (grad_w_in, *grad_in_rest), (grad_w_out, *grad_out_rest) = groups[6:8]
+        middle, normed, out_sum = groups[8]
         count, tall = rows_all.shape[:2]
         width = rows_all.shape[2]
 
         def fill_in(shard, local_sem):
             if not self.aligned:
-                return [pltpu.make_async_copy(ins[3], shard, local_sem.at[0])], ins[3]
+                return [pltpu.make_async_copy(w_in_rows[0], shard, local_sem.at[0])], w_in_rows[0]
             copies = []
             for i in range(2):
                 for group in range(inner // piece):
@@ -404,7 +368,7 @@
                     start = pl.multiple_of((group * count + ring.ctx) * piece, piece)
                     copies.append(
                         pltpu.make_async_copy(
-                            ins[3 + i].at[:, pl.ds(start, piece)],
+                            w_in_rows[i].at[:, pl.ds(start, piece)],
                             shard.at[:, pl.ds(at * piece, piece)],
                             local_sem.at[at],
                         )
@@ -462,15 +426,33 @@
                     right[...].reshape(count * tall, right.shape[2]),
                 ).astype(BF16)
 
-        yield from together(
-            ring_gather(ring, normed, rows_all, *rows_sems, False),
+        def first():
+            block = 256 if width % 256 == 0 else width
+
+            @pl.loop(0, width // block)
+            def _(index):
+                columns = pl.ds(pl.multiple_of(index * block, block), block)
+                middle[:, columns] = tokens[:, columns].astype(F32) + matmul(
+                    gated[:, :width], full_out[:, columns]
+                )
+
+            value = middle[...]
+            rstat = lax.rsqrt(jnp.mean(value * value, axis=1, keepdims=True) + EPSILON)
+            outs[2][...] = value * rstat
+            outs[3][...] = rstat
+            normed[...] = (outs[2][...] * gain[...]).astype(BF16)
+
+        weights = together(
             shard_gather(ring, fill_in, w_in, *w_in_sems),
             shard_gather(ring, fill_out, w_out, *w_out_sems),
         )
+        next(weights)
+        first()
+        yield from together(weights, ring_gather(ring, normed, rows_all, *rows_sems, False))
         compute(slice(count - 1, count))
         sums = together(
             ring_sum(ring, in_part, in_held, outs[1], *in_sems, False),
-            ring_sum(ring, out_part, out_held, outs[0], *out_sems, False),
+            ring_sum(ring, out_part, out_held, out_sum, *out_sems, False),
         )
         for _ in range(RING_PIECES):
             next(sums)
@@ -484,9 +466,28 @@
         weight_grads(hidden, grad_out, grad_w_out)
         yield from together(
             sums,
-            shard_sum(ring, grad_w_in, outs[2], *grad_in_rest),
-            shard_sum(ring, grad_w_out, outs[3], *grad_out_rest),
-        )
+            shard_sum(ring, grad_w_in, outs[4], *grad_in_rest),
+            shard_sum(ring, grad_w_out, outs[5], *grad_out_rest),
+        )
+        outs[0][...] = (middle[...] + out_sum[...]).astype(BF16)
+
+
+def swap_sems(count):
+    return sems(count - 1, count - 1)
+
+
+def swap(ring, sent, received, send_sem, recv_sem):
+    _, peers = all_peers(ring)
+    copies = [
+        remote(sent.at[to[0]], received.at[ring.ctx], send_sem.at[i], recv_sem.at[i], to)
+        for i, to in enumerate(peers)
+    ]
+    for copy in copies:
+        copy.start()
+    received[ring.ctx] = sent[ring.ctx]
+    yield from idle(RING_PIECES)
+    for copy in copies:
+        copy.wait()
 
 
 def small_sum_scratch(shape):
@@ -524,65 +525,171 @@
 
 
 class Attention:
-    kinds = ()
-
-    def __init__(self, qkv, decay, seg, own_heads):
-        self.rows, self.heads = qkv.shape[0], own_heads
-        self.dim = qkv.shape[1] // 3 // own_heads
-        self.scaling = self.dim ** (-0.5)
-        self.tall = min(256, self.rows)
-        self.ins = [qkv, decay, decay.T, seg[:, None], seg[None, :]]
+    kinds = ("all",)
+
+    def __init__(self, rows, heads, dim):
+        self.rows, self.heads, self.dim = rows, heads, dim
+        self.scaling = dim ** (-0.5)
+        self.tall = min(256 if rows <= 1024 else 128, rows)
 
     def block(self, index):
         rows = slice(index * self.tall, (index + 1) * self.tall)
         return rows, (index + 1) * self.tall
 
-    def allowed(self, rows, wide, seg_rows, seg_cols):
+    def allowed(self, rows, wide, info, across):
         shape = (self.tall, wide)
         here = lax.broadcasted_iota(jnp.int32, shape, 0) + rows.start
         there = lax.broadcasted_iota(jnp.int32, shape, 1)
-        return (there <= here) & (seg_rows[rows] == seg_cols[:, :wide])
+        return (there <= here) & (info[rows, 24:25] == across[8:9, :wide])
 
     def part(self, qkv, which, head, rows):
         start = (which * self.heads + head) * self.dim
         return qkv[rows, start : start + self.dim]
 
-    def scores(self, refs, head, rows, wide, allowed):
-        qkv, decay, decay_cols = refs[:3]
+    def scores(self, qkv, info, across, head, rows, wide, allowed):
         queries = self.part(qkv, 0, head, rows)
         keys = self.part(qkv, 1, head, slice(0, wide))
         scores = matmul_rows(queries, keys) * self.scaling
-        scores = scores + decay[rows, head : head + 1] - decay_cols[head : head + 1, :wide]
+        scores = scores + info[rows, head : head + 1] - across[head : head + 1, :wide]
         return queries, keys, jnp.where(allowed, scores, NEGATIVE)
 
 
-class AttentionForward(Attention):
-    def __init__(self, qkv, decay, seg, own_heads):
-        super().__init__(qkv, decay, seg, own_heads)
-        self.in_specs = [VMEM] * 5
+def split_refs(refs, sizes):
+    groups, at = [], 0
+    for size in sizes:
+        groups.append(list(refs[at : at + size]))
+        at += size
+    return groups
+
+
+EXACT = dict(preferred_element_type=F32, precision=lax.Precision.HIGHEST)
+
+
+class Forward(Attention):
+    def __init__(self, normed, cotangent, mixed_shard, w_out, bias, seg, heads, dim):
+        count, shards = lax.axis_size("ctx"), lax.axis_size("fsdp")
+        tall, width = normed.shape
+        rows = tall * count
+        super().__init__(rows, heads, dim)
+        hidden = heads * dim
+        self.hidden = hidden
+        documents = seg.astype(F32)
+        self.ins = [normed, cotangent, mixed_shard, w_out, bias]
+        self.in_specs = [ANYWHERE] * 4 + [VMEM] * 3
+        self.ins += [documents[:, None], documents[None, :]]
+        everyone = jax.ShapeDtypeStruct((count, tall, width), BF16)
         self.outs = [
-            jax.ShapeDtypeStruct((self.rows, own_heads * self.dim), F32),
-            jax.ShapeDtypeStruct((self.rows, own_heads), F32),
+            everyone,
+            everyone,
+            jax.ShapeDtypeStruct((width, mixed_shard.shape[1]), BF16),
+            jax.ShapeDtypeStruct((width, width), BF16),
+            jax.ShapeDtypeStruct((rows, 3 * hidden), BF16),
+            jax.ShapeDtypeStruct((rows, hidden), F32),
+            jax.ShapeDtypeStruct((rows, hidden), F32),
+            jax.ShapeDtypeStruct((rows, 128), F32),
+            jax.ShapeDtypeStruct((16, rows), F32),
+            jax.ShapeDtypeStruct((tall, count * hidden), BF16),
         ]
-        self.out_specs, self.scratch = [VMEM] * 2, []
+        self.out_specs = [VMEM, ANYWHERE, VMEM, ANYWHERE] + [VMEM] * 6
+        ring = [pltpu.SemaphoreType.DMA] + ring_sems(count)
+        swapped = pltpu.VMEM((count, tall, hidden), BF16)
+        groups = [
+            ring,
+            ring,
+            shard_gather_sems(1),
+            shard_gather_sems(1),
+            [swapped, swapped] + swap_sems(count),
+        ]
+        self.sizes = [len(group) for group in groups]
+        self.scratch = sum(groups, [])
 
     def run(self, ring, ins, outs, scratch):
+        rows_sems, cotangent_sems, mixed_sems, out_sems, swapping = split_refs(scratch, self.sizes)
+        own, cotangent, mixed_shard, w_out, bias, seg_rows, seg_columns = ins
+        normed, grad_out, mixed_in, full_out, qkv, attended, gate, info, across, gated = outs
+        sent, received = swapping[:2]
+        count, tall, _ = normed.shape
+
+        def filled_from(source):
+            def fill(shard, local_sem):
+                return [pltpu.make_async_copy(source, shard, local_sem.at[0])], source
+
+            return fill
+
+        def later(turns, walk):
+            yield from idle(turns)
+            yield from walk
+
+        def main():
+            yield from together(
+                ring_gather(ring, own, normed, *rows_sems, True),
+                shard_gather(ring, filled_from(mixed_shard), mixed_in, *mixed_sems),
+            )
+            self.project(normed, mixed_in, bias, qkv, gate, info)
+            self.decay(info, across, seg_rows, seg_columns)
+            yield
+            yield from self.attend(qkv, info, across, attended)
+            for i in range(count):
+                rows = slice(i * tall, (i + 1) * tall)
+                sent[i] = (attended[rows] * gate[rows]).astype(BF16)
+            yield from swap(ring, *swapping)
+            gated[...] = jnp.concatenate([received[i] for i in range(count)], axis=1)
+
+        turns = count // 2 * RING_PIECES
+        yield from together(
+            main(),
+            later(turns - 1, ring_gather(ring, cotangent, grad_out, *cotangent_sems, False)),
+            later(turns // 2, shard_gather(ring, filled_from(w_out), full_out, *out_sems)),
+        )
+
+    def project(self, normed, mixed_in, bias, qkv, gate, info):
+        count, tall, width = normed.shape
+        pair = 2 if count % 2 == 0 else 1
+        hidden = self.hidden
+
+        @pl.loop(0, count // pair)
+        def _(index):
+            block = normed[pl.ds(index * pair, pair)].reshape(pair * tall, width)
+            rows = pl.ds(pl.multiple_of(index * pair * tall, pair * tall), pair * tall)
+            mixed = matmul(block, mixed_in[...])
+            qkv[rows] = mixed[:, : 3 * hidden].astype(BF16)
+            gate[rows] = jax.nn.sigmoid(mixed[:, 3 * hidden : 4 * hidden])
+            info[rows] = mixed[:, 4 * hidden : 4 * hidden + 128]
+            info[rows, 8:16] = info[rows, 0:8] + bias[...]
+
+    def decay(self, info, across, seg_rows, seg_columns):
+        tall = 128
+        here = lax.broadcasted_iota(jnp.int32, (tall, tall), 0)
+        there = lax.broadcasted_iota(jnp.int32, (tall, tall), 1)
+        wedge = (there <= here).astype(F32)
+        before = jnp.zeros((1, 8), F32)
+        pad = jnp.zeros((tall, 120), F32)
+        for index in range(self.rows // tall):
+            rows = slice(index * tall, (index + 1) * tall)
+            logs = jax.nn.log_sigmoid(info[rows, 8:16])
+            sums = jnp.dot(wedge, jnp.concatenate([logs, pad], axis=1), **EXACT)[:, :8] + before
+            before = sums[tall - 1 :]
+            info[rows, 0:8] = sums
+            across[0:8, rows] = jnp.concatenate([sums, pad], axis=1).T[:8]
+        info[:, 24:25] = seg_rows[...]
+        across[8:9] = seg_columns[...]
+
+    def attend(self, qkv, info, across, attended):
         for index in range(self.rows // self.tall):
             rows, wide = self.block(index)
-            allowed = self.allowed(rows, wide, *ins[3:])
-            mixed, totals = [], []
+            allowed = self.allowed(rows, wide, info, across)
+            mixed = []
             for head in range(self.heads):
-                _, _, scores = self.scores(ins, head, rows, wide, allowed)
+                _, _, scores = self.scores(qkv, info, across, head, rows, wide, allowed)
                 row_max = jnp.max(scores, axis=1, keepdims=True)
                 raised = jnp.exp(scores - row_max)
                 row_total = jnp.sum(raised, axis=1, keepdims=True)
                 probabilities = (raised * (1.0 / row_total)).astype(BF16)
-                mixed.append(matmul(probabilities, self.part(ins[0], 2, head, slice(0, wide))))
-                totals.append(row_max + jnp.log(row_total))
+                mixed.append(matmul(probabilities, self.part(qkv, 2, head, slice(0, wide))))
+                info[rows, 16 + head : 17 + head] = row_max + jnp.log(row_total)
                 if head < self.heads - 1:
                     yield
-            outs[0][rows] = jnp.concatenate(mixed, axis=1)
-            outs[1][rows] = jnp.concatenate(totals, axis=1)
+            attended[rows] = jnp.concatenate(mixed, axis=1)
             yield
 
 
@@ -592,14 +699,13 @@
 
 
 class Backward(Attention):
-    kinds = ("all",)
-
-    def __init__(self, qkv, decay, seg, own_heads, named):
-        super().__init__(qkv, decay, seg, own_heads)
+    def __init__(self, own_heads, named):
+        rows = named["qkv"].shape[0]
+        super().__init__(rows, own_heads, named["qkv"].shape[1] // 3 // own_heads)
         self.names = list(named)
         hbm = ("gated", "grad_ffn_in", "grad_ffn_out")
-        self.ins = self.ins + [named[name] for name in self.names]
-        self.in_specs = [VMEM] * 5 + [ANYWHERE if name in hbm else VMEM for name in self.names]
+        self.ins = [named[name] for name in self.names]
+        self.in_specs = [ANYWHERE if name in hbm else VMEM for name in self.names]
         count, shards = lax.axis_size("ctx"), lax.axis_size("fsdp")
         tall, width = named["gated"].shape
         hidden = own_heads * self.dim
@@ -607,6 +713,8 @@
         both = -(-(5 * hidden + own_heads) // 128) * 128
         ffn = [named["grad_ffn_in"], named["grad_ffn_out"]]
         shard_rows = width // shards
+        swapped = pltpu.VMEM((count, tall, 2 * hidden), BF16)
+        heads = pltpu.VMEM((self.rows, hidden), BF16)
         self.outs = (
             [jax.ShapeDtypeStruct((tall, width), F32)]
             + [jax.ShapeDtypeStruct((count,) + grad.shape, BF16) for grad in ffn]
@@ -632,26 +740,35 @@
             ring,
             ring,
             [pltpu.VMEM((8, width), F32)] + small_sum_scratch((8, width)),
+            [pltpu.VMEM((tall, width), F32), pltpu.VMEM((tall, count * hidden), BF16)],
+            [swapped, swapped] + swap_sems(count),
+            [heads, heads, heads],
         ]
         self.sizes = [len(group) for group in groups]
         self.scratch = sum(groups, [])
 
     def run(self, ring, ins, outs, scratch):
-        groups, at = [], 0
-        for size in self.sizes:
-            groups.append(scratch[at : at + size])
-            at += size
-        named = dict(zip(self.names, ins[5:]))
+        groups = split_refs(scratch, self.sizes)
+        named = dict(zip(self.names, ins))
         gated_all, *gated_sems = groups[3]
         rows_part, rows_held, rows_sum, *rows_sems = groups[4]
         grad_mixed = groups[2][0]
         grads_part, grads_sum, *grads_rest = groups[5]
         small, *small_rest = groups[9]
+        named["grad_middle"], grad_gated = groups[10]
+        named["grad_attn"], named["grad_gatelog"], named["grad_branch"] = groups[12]
         count, tall, width = gated_all.shape
 
         def main():
+            yield
+            self.branch_back(named, grad_gated, groups[11][0], small)
             yield from together(
-                self.attention(ins, named, *groups[0], *groups[1]),
+                swap(ring, *groups[11]),
+                idle(RING_PIECES),
+            )
+            self.gate_back(named, groups[11][1])
+            yield from together(
+                self.attention(named, *groups[0], *groups[1]),
                 ring_gather(ring, named["gated"], gated_all, *gated_sems, True),
             )
             self.join(named, *groups[0], *groups[1], grad_mixed, small)
@@ -674,9 +791,9 @@
             yield from shard_sum(ring, grads_part, grads_sum, *grads_rest)
 
         yield from together(
-            main(),
             slow(ring_gather(ring, named["grad_ffn_in"], outs[1], *groups[6], True), 2),
             slow(ring_gather(ring, named["grad_ffn_out"], outs[2], *groups[7], True), 2),
+            main(),
         )
         self.norm_back(named, rows_sum, outs[0], small)
         yield from together(
@@ -684,22 +801,68 @@
             small_sum(ring, small, outs[4], *small_rest),
         )
 
-    def attention(self, ins, named, grads, sums_rows, sums_columns):
-        log_totals, grad_attn = named["log_totals"], named["grad_attn"]
+    def branch_back(self, named, grad_gated, sent, small):
+        grad, normed = named["grad_normed_two"][...], named["normed_two"][...]
+        small[...] = jnp.zeros_like(small)
+        small[1:2] = jnp.sum(grad * normed, axis=0, keepdims=True)
+        grad_normed = grad * named["gain_two"][...]
+        inner = jnp.mean(grad_normed * normed, axis=1, keepdims=True)
+        named["grad_middle"][...] = named["cotangent"][...].astype(F32) + named["rstat_two"][...] * (
+            grad_normed - normed * inner
+        )
+        count, tall, both = sent.shape
+        width = grad.shape[1]
+        block = 256 if width % 256 == 0 else width
+        if grad_gated.shape[1] > width:
+            grad_gated[...] = jnp.zeros_like(grad_gated)
+
+        @pl.loop(0, width // block)
+        def _(index):
+            columns = pl.ds(pl.multiple_of(index * block, block), block)
+            low = named["grad_middle"][...].astype(BF16)
+            grad_gated[:, columns] = matmul_rows(low, named["full_out"][columns]).astype(BF16)
+
+        low = named["grad_middle"][...].astype(BF16)
+        if grad_gated.shape[1] > width:
+            low = jnp.concatenate(
+                [low, jnp.zeros((tall, grad_gated.shape[1] - width), BF16)], axis=1
+            )
+        for i in range(count):
+            own = slice(i * both // 2, (i + 1) * both // 2)
+            sent[i] = jnp.concatenate([grad_gated[:, own], low[:, own]], axis=1)
+
+    def gate_back(self, named, received):
+        count, tall, both = received.shape
+        for i in range(count):
+            rows = slice(i * tall, (i + 1) * tall)
+            grad = received[i, :, : both // 2].astype(F32)
+            gate = named["gate_value"][rows]
+            named["grad_attn"][rows] = (grad * gate).astype(BF16)
+            named["grad_gatelog"][rows] = (
+                grad * named["attended"][rows] * (gate * (1.0 - gate))
+            ).astype(BF16)
+            named["grad_branch"][rows] = received[i, :, both // 2 :]
+
+    def attention(self, named, grads, sums_rows, sums_columns):
+        qkv, info, across, grad_attn = [
+            named[name] for name in ("qkv", "info", "across", "grad_attn")
+        ]
         grad_q, grad_k, grad_v = [grads.at[i] for i in range(3)]
         blocks = self.rows // self.tall
         sums_columns[...] = jnp.zeros_like(sums_columns)
         pad = jnp.zeros((self.tall, 128 - self.heads), F32)
         for index in reversed(range(blocks)):
             rows, wide = self.block(index)
-            allowed = self.allowed(rows, wide, *ins[3:5])
+            allowed = self.allowed(rows, wide, info, across)
             own = slice(0, wide)
             row_sums = []
             for head in range(self.heads):
-                queries, keys, scores = self.scores(ins, head, rows, wide, allowed)
-                probabilities = jnp.exp(scores - log_totals[rows, head : head + 1])
+                queries, keys, scores = self.scores(
+                    qkv, info, across, head, rows, wide, allowed
+                )
+                probabilities = jnp.exp(scores - info[rows, 16 + head : 17 + head])
                 grad_part = grad_attn[rows, head * self.dim : (head + 1) * self.dim]
-                grad_probs = matmul_rows(grad_part, self.part(ins[0], 2, head, own))
+                grad_probs = matmul_rows(grad_part, self.part(qkv, 2, head, own))
                 row_inner = jnp.sum(probabilities * grad_probs, axis=1, keepdims=True)
                 grad_scores = (probabilities * (grad_probs - row_inner)).astype(BF16)
                 grad_q[head, rows] = matmul(grad_scores, keys) * self.scaling
@@ -731,19 +894,17 @@
         there = lax.broadcasted_iota(jnp.int32, (tall, tall), 1)
         wedge = (here <= there).astype(F32)
         later, bias = jnp.zeros((1, 8), F32), jnp.zeros((1, 8), F32)
-        exact = dict(preferred_element_type=F32, precision=lax.Precision.HIGHEST)
         pad = jnp.zeros((tall, 120), BF16)
         for index in reversed(range(self.rows // tall)):
             rows = slice(index * tall, (index + 1) * tall)
-            inside = jnp.dot(wedge, sums_rows[rows], **exact)[:, :8] - lax.dot_general(
-                wedge, sums_columns[:, rows], (((1,), (1,)), ((), ())), **exact
+            inside = jnp.dot(wedge, sums_rows[rows], **EXACT)[:, :8] - lax.dot_general(
+                wedge, sums_columns[:, rows], (((1,), (1,)), ((), ())), **EXACT
             )
-            logits = named["forget_logits"][rows]
+            logits = named["info"][rows, 8:16]
             grad_logits = ((inside + later) * jax.nn.sigmoid(-logits)).astype(BF16)
             later = later + inside[:1]
             bias = bias + jnp.sum(grad_logits.astype(F32), axis=0, keepdims=True)
             grad_mixed[rows, self.main :] = jnp.concatenate([grad_logits, pad], axis=1)
-        small[...] = named["small"][...]
         small[2:3] = sum(
             bias[:, head : head + 1] * named["places"][head : head + 1]
             for head in range(self.heads)
@@ -775,17 +936,6 @@
         grad_tokens[...] = named["grad_middle"][...] + named["rstat_one"][...] * (
             grad_normed - normed * inner
         )
-
-
-def running_sum(values):
-    tall = 128 if values.shape[0] % 128 == 0 else values.shape[0]
-    blocks = values.reshape(-1, tall, values.shape[1])
-    wedge = jnp.tril(jnp.ones((tall, tall), F32))
-    inside = jnp.einsum("st,btk->bsk", wedge, blocks, precision=lax.Precision.HIGHEST)
-    totals = jnp.sum(blocks, axis=1)
-    before = jnp.tril(jnp.ones((totals.shape[0],) * 2, F32), -1)
-    before = jnp.sum(before[:, :, None] * totals[None], axis=1)
-    return (inside + before[:, None]).reshape(values.shape)
 
 
 def exchange(ident, name, *tasks):
@@ -830,7 +980,7 @@
         out_specs=sum([task.out_specs for task in tasks], []),
         scratch_shapes=sum([task.scratch for task in tasks], []),
         compiler_params=pltpu.CompilerParams(
-            collective_id=ident, has_side_effects=True, vmem_limit_bytes=58 * 2**20
+            collective_id=ident, has_side_effects=True, vmem_limit_bytes=62 * 2**20
         ),
         cost_estimate=pl.CostEstimate(flops=0, bytes_accessed=100_000_000, transcendentals=0),
         name=name,
@@ -900,14 +1050,6 @@
         ),
         name="head_columns",
     )(blocks)
-
-
-def rows_to_columns(value):
-    return lax.all_to_all(value, "ctx", split_axis=1, concat_axis=0, tiled=True)
-
-
-def columns_to_rows(value):
-    return lax.all_to_all(value, "ctx", split_axis=0, concat_axis=1, tiled=True)
 
 
 def shards(
@@ -967,70 +1109,62 @@
     inputs = tokens[0].astype(F32)
     gain_one = gain_attn.astype(F32)
     normed_one, rstat_one = rms_stats(inputs)
-    (normed,), (mixed_in,) = exchange(
+    (
+        (
+            normed,
+            grad_out_low,
+            mixed_in,
+            full_out,
+            qkv,
+            attended,
+            gate_value,
+            info,
+            across,
+            gated,
+        ),
+    ) = exchange(
         0,
-        "gather_start",
-        RingGather((normed_one * gain_one).astype(BF16), absolute=True),
-        ShardGather(mixed_shard),
+        "forward",
+        Forward(
+            (normed_one * gain_one).astype(BF16),
+            cotangent[0],
+            mixed_shard,
+            w_out,
+            bias_own[None],
+            segments[0],
+            own_heads,
+            head_dim,
+        ),
     )
-    normed_rows = flat(normed)
-    normed_rows, out_shard = lax.optimization_barrier((normed_rows, w_out))
-    full_out = lax.all_gather(out_shard, "fsdp", axis=0, tiled=True)
-
-    split = [own_width * i for i in range(5)]
-    qkv = matmul(normed_rows, mixed_in[:, : split[3]]).astype(BF16)
-    mixed = matmul(normed_rows, mixed_in[:, split[3] :])
-    gate_value = jax.nn.sigmoid(mixed[:, :own_width])
-    forget_logits = mixed[:, own_width : own_width + 8] + bias_own
-    decay = running_sum(jax.nn.log_sigmoid(forget_logits))
-
-    (grad_out_low,), (attended, log_totals) = exchange(
-        5,
-        "attend",
-        RingGather(cotangent[0]),
-        AttentionForward(qkv, decay, seg, own_heads),
-    )
-    gated = columns_to_rows((attended * gate_value).astype(BF16))[:, :width]
-
-    middle = inputs + matmul(gated, full_out)
-    gain_two = gain_ffn.astype(F32)
-    normed_two_f, rstat_two = rms_stats(middle)
+    gain_two = gain_ffn.astype(F32)[None]
     w_in = [w_gate, w_up]
     if ffn_piece % 128 != 0:
         w_in = [jnp.concatenate(own_ffn(w_gate) + own_ffn(w_up), axis=1)]
-    ((out_sum, grad_normed_two, grad_ffn_in, grad_ffn_out),) = exchange(
+    ((output, grad_normed_two, normed_two, rstat_two, grad_ffn_in, grad_ffn_out),) = exchange(
         1,
         "ffn",
-        Ffn((normed_two_f * gain_two).astype(BF16), grad_out_low, w_in, w_down, ffn_piece),
+        Ffn(tokens[0], gated, full_out, gain_two, grad_out_low, w_in, w_down, ffn_piece),
     )
-    output = middle + out_sum
-    back_two, grad_gain_two = norm_back(grad_normed_two, normed_two_f, rstat_two, gain_two)
-    grad_middle = cotangent[0].astype(F32) + back_two
-
-    grad_branch_low = grad_middle.astype(BF16)
-    grad_gated = matmul_rows(grad_branch_low, full_out).astype(BF16)
-    grad_gated = rows_to_columns(widen(grad_gated, padded)).astype(F32)
-    grad_branch_own = rows_to_columns(widen(grad_branch_low, padded))
-    grad_attn_low = (grad_gated * gate_value).astype(BF16)
-    grad_gatelog_low = (grad_gated * attended * (gate_value * (1.0 - gate_value))).astype(BF16)
-
     spots = jnp.arange(own_heads, dtype=jnp.int32)[:, None] + me * own_heads
     places = (spots == jnp.arange(width, dtype=jnp.int32)[None, :]).astype(F32)
     ((grad_inputs, spread_ffn_in, spread_ffn_out, spread_attn, small),) = exchange(
         2,
         "backward",
         Backward(
-            qkv,
-            decay,
-            seg,
             own_heads,
             {
-                "log_totals": log_totals,
-                "grad_attn": grad_attn_low,
-                "grad_gatelog": grad_gatelog_low,
-                "forget_logits": forget_logits,
-                "grad_branch": grad_branch_own,
-                "gated": gated,
+                "qkv": qkv,
+                "info": info,
+                "across": across,
+                "attended": attended,
+                "gate_value": gate_value,
+                "grad_normed_two": grad_normed_two,
+                "normed_two": normed_two,
+                "rstat_two": rstat_two,
+                "gain_two": gain_two,
+                "cotangent": cotangent[0],
+                "full_out": full_out,
+                "gated": gated[:, :width],
                 "grad_ffn_in": grad_ffn_in,
                 "grad_ffn_out": grad_ffn_out,
                 "normed": normed,
@@ -1038,9 +1172,7 @@
                 "normed_one": normed_one,
                 "rstat_one": rstat_one,
                 "gain_one": gain_one[None],
-                "grad_middle": grad_middle,
                 "places": places,
-                "small": jnp.pad(grad_gain_two[None], ((1, 6), (0, 0))),
             },
         ),
     )
@@ -1053,7 +1185,7 @@
         grad_gate, grad_up = whole[0], whole[1]
     grad_weights = head_columns(spread_attn, sizes, [width] * 5 + [n_heads])
     return (
-        output.astype(BF16)[None],
+        output[None],
         grad_inputs[None],
         small[0],
         grad_weights[0],

time: 545 us -> 496 us (0.910)
  Pallas kernels: 421 us -> 458 us
  waiting for transfers between devices: 21.8 us -> 0 us
  matrix products: 18.5 us -> 0 us
  between operations: 14.5 us -> 1.22 us
  starting transfers between devices: 12.9 us -> 0 us
  other arithmetic: 19.8 us -> 9.1 us
  local copies, waits for them, and re-layouts: 26 us -> 18.1 us
    pallas_call x4 -> x3, Pallas kernels: 409 us -> 446 us  [exchange(): pl.pallas_call(kernel, out_shape=sum([task.outs for task in tasks], []),...]
    all_to_all x3 -> x0, waiting for transfers between devices: 21.8 us -> none  [the longest x2 11.8 us: rows_to_columns(): return lax.all_to_all(value, 'ctx', split_axis=1, concat_axis=0, tiled=True)]
    dot_general x5 -> x0, matrix products: 18.5 us -> none  [the longest x3 14.2 us: matmul(): return jnp.dot(left, right, preferred_element_type=F32)]
    all_to_all x3 -> x0, starting transfers between devices: 12.8 us -> none  [the longest x2 8.53 us: rows_to_columns(): return lax.all_to_all(value, 'ctx', split_axis=1, concat_axis=0, tiled=True)]
    convert_element_type x6 -> x1, other arithmetic: 8.44 us -> 0.6 us  [__init__(): documents = seg.astype(F32)]
  transfers between devices with their start and end apart: 4 -> 0, of which waited for: 3 -> 0; matrix products, arithmetic and copies ran while one was open for 5% -> 0% of each run, Pallas kernels for 7% -> 0%
where the time goes in v4:
time: 496 us; the launch traced here: 487 us
  Pallas kernels  458 us (92%)
  local copies, waits for them, and re-layouts  18.1 us (4%)
  other arithmetic  9.1 us (2%)
    pallas_call x3, Pallas kernels, exchange(): pl.pallas_call(kernel, out_shape=sum([task.outs for task in tasks], []),...  446 us

profile of v4, /device:TPU:0, one launch (start us, length us, event | category | flops | bytes accessed | tf_op | source)
XLA Modules:
  0.0 486.8 jit_solution(10645704860178573270)
XLA Ops:
  0.6 0.0 copy-start
  0.7 1.2 fusion
  1.9 0.7 convert_element_type.38
  2.6 2.2 convert_multiply_fusion
  4.7 1.2 constant_dynamic-slice_fusion.3
  6.0 1.2 constant_dynamic-slice_fusion.1
  7.2 0.2 copy.36
  7.4 0.0 copy-start.9
  7.5 1.2 concatenate.3.refs_2_
  8.6 0.1 dynamic_slice.23
  8.7 0.5 pad_bitcast_fusion.refs_4_
  9.2 0.6 fusion.3
  9.8 1.0 copy.33.refs_5_
  10.8 85.0 %forward.1 = (bf16[8,128,1536]{2,1,0:T(8,128)(2,1)}, bf16[8,128,1536]{2,1,0:T(8,128)(2,1)}, bf16[1536,896]{1,0:T(8,128)(2,1)}, bf16[1536,1536]{1,0:T(8,128)(2,1)...) custom-call(bf16[128,1536]{1,0:T(8,128)(2,1)} %get-tuple-element.103, ...), custom_call_target="tpu_custom_call" | custom-call | bytes 100000000 | tf_op jit(solution)/shard_map/forward/pallas_call | solution.py:976
  95.9 0.6 reshape.69.refs_4_.refs_8_
  96.5 111.7 %ffn.1 = (bf16[128,1536]{1,0:T(8,128)(2,1)}, f32[128,1536]{1,0:T(8,128)}, f32[128,1536]{1,0:T(8,128)}, f32[128,1]{1,0:T(8,128)}, bf16[384,1024]{1,0:T(8,128)(2,1)}, /*index=5*/bf16[128,1536]{1,0:T(8,128)(2,1)}) custom-call(bf16[8,128,1536]{2,1,0:T(8,128)(2,1)} %get-tuple-element.43.refs_0_, bf16[128,1536]{1,0:T(8,128)(2,1)} %bitcast.19, ...), custom_call_target="tpu_custom_call" | custom-call | bytes 100000000 | tf_op jit(solution)/shard_map/ffn/pallas_call | solution.py:976
  208.2 0.7 copy.34.refs_17_
  208.9 0.0 copy-done.7
  208.9 0.6 broadcast_in_dim.27.refs_18_
  209.5 0.7 fusion.1.refs_19_
  210.2 249.6 %backward.1 = (f32[128,1536]{1,0:T(8,128)}, bf16[8,384,1024]{2,1,0:T(8,128)(2,1)}, bf16[8,128,1536]{2,1,0:T(8,128)(2,1)}, bf16[8,384,1024]{2,1,0:T(8,128)(2,1)}, f32[8,1536]{1,0:T(8,128)}) custom-call(bf16[1024,576]{1,0:T(8,128)(2,1)} %get-tuple-element.47.refs_0_, f32[1024,128]{1,0:T(8,128)} %get-tuple-element.48.refs_1_, ...), custom_call_target="tpu_custom_call" | custom-call | bytes 100000000 | tf_op jit(solution)/shard_map/backward/pallas_call | solution.py:976
  459.9 1.5 slice_reduce_fusion
  461.4 2.8 copy-done.3
  464.1 6.8 %head_columns.1 = (f32[384,1536]{1,0:T(8,128)}, f32[384,1536]{1,0:T(8,128)}, f32[384,1536]{1,0:T(8,128)}, f32[384,1536]{1,0:T(8,128)}, f32[384,1536]{1,0:T(8,128)}, /*index=5*/f32[384,24]{1,0:T(8,128)S(1)}) custom-call(bf16[8,384,1024]{2,1,0:T(8,128)(2,1)S(1)} %copy-done.3), custom_call_target="tpu_custom_call" | custom-call | bytes 18874368 | tf_op jit(solution)/shard_map/head_columns/pallas_call | solution.py:1041
  470.9 0.7 copy.35
  471.6 1.2 slice_bitcast_fusion
  472.8 2.8 copy-done.2
  475.6 5.3 %ffn_columns.1 = (f32[384,4096]{1,0:T(8,128)}, f32[384,4096]{1,0:T(8,128)}) custom-call(bf16[8,384,1024]{2,1,0:T(8,128)(2,1)S(1)} %copy-done.2), custom_call_target="tpu_custom_call" | custom-call | bytes 18874368 | tf_op jit(solution)/shard_map/ffn_columns/pallas_call | solution.py:1010
  480.9 0.0 copy-start.1
  481.0 3.8 bitcast_convert_fusion
  484.7 0.7 copy.39
  485.5 0.9 copy.40
  (20 shorter events, 0.1 us)
Async XLA Ops:
  0.6 6.6 %copy-start = (bf16[384,24]{0,1:T(8,128)(2,1)S(1)}, bf16[384,24]{0,1:T(8,128)(2,1)}, u32[]{:S(2)}) copy-start(bf16[384,24]{0,1:T(8,128)(2,1)} %param.21) | copy-start | bytes 55300
  0.7 8.0 %copy-start.10 = (f32[24]{0:T(128)S(1)}, f32[24]{0:T(128)}, u32[]{:S(2)}) copy-start(f32[24]{0:T(128)} %param.22) | copy-start | bytes 292
  0.7 8.5 %copy-start.8 = (s32[1,1024]{1,0:T(1,128)S(1)}, s32[1,1024]{1,0:T(1,128)}, u32[]{:S(2)}) copy-start(s32[1,1024]{1,0:T(1,128)} %param.16) | copy-start | bytes 12292
  7.4 88.5 %copy-start.9 = (bf16[1536]{0:T(1024)(128)(2,1)S(1)}, bf16[1536]{0:T(1024)(128)(2,1)}, u32[]{:S(2)}) copy-start(bf16[1536]{0:T(1024)(128)(2,1)} %param.25) | copy-start | bytes 9220
  96.5 112.4 %copy-start.7 = (bf16[1536]{0:T(1024)(128)(2,1)S(1)}, bf16[1536]{0:T(1024)(128)(2,1)}, u32[]{:S(2)}) copy-start(bf16[1536]{0:T(1024)(128)(2,1)} %param.17) | copy-start | bytes 9220
  461.4 2.8 copy-start.3
  472.8 2.8 copy-start.2
  475.6 5.3 %copy-start.4 = (bf16[8,128,1536]{2,1,0:T(8,128)(2,1)S(1)}, bf16[8,128,1536]{2,1,0:T(8,128)(2,1)}, u32[]{:S(2)}) copy-start(bf16[8,128,1536]{2,1,0:T(8,128)(2,1)} %get-tuple-element.71) | copy-start | bytes 9437188
  480.9 3.8 copy-start.6
  480.9 4.5 copy-start.5
  480.9 5.4 %copy-start.1 = (bf16[384,24]{0,1:T(8,128)(2,1)S(1)}, bf16[384,24]{0,1:T(8,128)(2,1)}, u32[]{:S(2)}) copy-start(bf16[384,24]{0,1:T(8,128)(2,1)} %param.21) | copy-start | bytes 55300
